TPU v7x, 32 devices: a whole 2x2x4 slice. The times are simulated.
32 devices in a mesh: img: 2 (over x), row: 4 (over y, core), col: 4 (over z).
Axes of the slice: x: 2, y: 2, z: 4, core: 2. Of those that a mesh axis runs over, the one named last changes fastest.
Arguments:
- image_in: bfloat16 [4, 64, 64, 768], P('img', 'row', 'col'), may hold values from -6 to 6
- cotangent: bfloat16 [4, 64, 64, 768], P('img', 'row', 'col'), may hold values from -6 to 6
- qkv_weight: bfloat16 [768, 2304], P(('row', 'col'), 'img'), may hold values from -0.21875 to 0.21875
- out_weight: bfloat16 [768, 768], P(('row', 'col'), 'img'), may hold values from -0.875 to 0.875
- up_weight: bfloat16 [768, 3072], P(('row', 'col'), 'img'), may hold values from -0.21875 to 0.21875
- down_weight: bfloat16 [3072, 768], P(('row', 'col'), 'img'), may hold values from -0.109375 to 0.109375
- query_bias: float32 [768], replicated, may hold values from -4 to 4
- value_bias: float32 [768], replicated, may hold values from -4 to 4
- out_bias: float32 [768], replicated, may hold values from -4 to 4
- up_bias: float32 [3072], replicated, may hold values from -4 to 4
- down_bias: float32 [768], replicated, may hold values from -4 to 4
- first_gain: float32 [768], replicated, may hold values from 0.25 to 1.75
- first_shift: float32 [768], replicated, may hold values from -4 to 4
- second_gain: float32 [768], replicated, may hold values from 0.25 to 1.75
- second_shift: float32 [768], replicated, may hold values from -4 to 4
- rows_table: bfloat16 [27, 64], replicated, may hold values from -2 to 2
- cols_table: bfloat16 [27, 64], replicated, may hold values from -2 to 2
Outputs:
- image_out: bfloat16 [4, 64, 64, 768], P('img', 'row', 'col')
- image_grad: float32 [4, 64, 64, 768], P('img', 'row', 'col')
- grad_qkv_weight: float32 [768, 2304], P(('row', 'col'), 'img')
- grad_out_weight: float32 [768, 768], P(('row', 'col'), 'img')
- grad_up_weight: float32 [768, 3072], P(('row', 'col'), 'img')
- grad_down_weight: float32 [3072, 768], P(('row', 'col'), 'img')
- grad_query_bias: float32 [768], replicated
- grad_value_bias: float32 [768], replicated
- grad_out_bias: float32 [768], replicated
- grad_up_bias: float32 [3072], replicated
- grad_down_bias: float32 [768], replicated
- grad_first_gain: float32 [768], replicated
- grad_first_shift: float32 [768], replicated
- grad_second_gain: float32 [768], replicated
- grad_second_shift: float32 [768], replicated
- grad_rows_table: float32 [27, 64], replicated
- grad_cols_table: float32 [27, 64], replicated
All inputs are finite; a program needn't handle non-finite values.
Results may differ from a plain program's by a relative error of at most 0.018.
Values may be sent and summed in bfloat16 or wider, within the bound.
A program may use at most 256 MiB of HBM per device.

v0:
```python
from functools import partial

import jax
import jax.numpy as jnp
from jax import lax
from jax.sharding import PartitionSpec as P

HEADS = 12
HEAD_DIM = 64
WIN = 14


exact_mode = lax.Precision.HIGHEST
epsilon = 1e-06


def from_behind(block, axis, distance):
    devices = range(lax.axis_size(axis))
    route = [(i - distance, i) for i in devices if i - distance in devices]
    return lax.ppermute(block, axis, route)


def rounded(values):
    return lax.optimization_barrier(values.astype(jnp.bfloat16)).astype(jnp.float32)


def layer_norm(values, gain_vector, shift_vector):
    center = values - jnp.mean(values, axis=-1, keepdims=True)
    inverse = lax.rsqrt(jnp.mean(center * center, axis=-1, keepdims=True) + epsilon)
    unit_rows = center * inverse
    return (unit_rows * gain_vector + shift_vector, unit_rows, inverse)


def norm_back(grad_out, unit_rows, inverse, gain_vector):
    scaled = grad_out * gain_vector
    first_mean = jnp.mean(scaled, axis=-1, keepdims=True)
    second_mean = jnp.mean(scaled * unit_rows, axis=-1, keepdims=True)
    return inverse * (scaled - first_mean - unit_rows * second_mean)


def gather_weights(qkv_weight, out_weight, up_weight, down_weight):
    widened = (
        lax.all_gather(qkv_weight, "img", axis=1, tiled=True),
        lax.all_gather(out_weight, "img", axis=1, tiled=True),
        lax.all_gather(up_weight, "img", axis=1, tiled=True),
        lax.all_gather(down_weight, "img", axis=1, tiled=True),
    )
    return (
        lax.all_gather(widened[0], ("row", "col"), axis=0, tiled=True),
        lax.all_gather(widened[1], ("row", "col"), axis=0, tiled=True),
        lax.all_gather(widened[2], ("row", "col"), axis=0, tiled=True),
        lax.all_gather(widened[3], ("row", "col"), axis=0, tiled=True),
    )


def extend(own):
    tile_side = own.shape[1]
    margin = 2 * WIN - tile_side
    beneath = from_behind(own[:, :margin], "row", -1)
    taller = jnp.concatenate([own, beneath], axis=1)
    beside = from_behind(taller[:, :, :margin], "col", -1)
    return jnp.concatenate([taller, beside], axis=2)


def fold_back(region, tile_side):
    margin = 2 * WIN - tile_side
    arrived = from_behind(region[:, :, tile_side:], "col", 1)
    narrow = jnp.concatenate(
        [region[:, :, :margin] + arrived, region[:, :, margin:tile_side]], axis=2
    )
    lifted = from_behind(narrow[:, tile_side:], "row", 1)
    return jnp.concatenate([narrow[:, :margin] + lifted, narrow[:, margin:tile_side]], axis=1)


def slot_starts(position, tile_side):
    first_start = (WIN - position % WIN) % WIN
    second_start = first_start + WIN
    starts = (first_start, jnp.minimum(second_start, WIN))
    return (starts, (first_start < tile_side, second_start < tile_side))


def cut_windows(region, rows_start, cols_start):
    zero_index = jnp.zeros((), jnp.int32)
    images_here = region.shape[0]
    features = region.shape[3]
    pieces = []
    for row_slot in range(2):
        for col_slot in range(2):
            corner = (zero_index, rows_start[row_slot], cols_start[col_slot], zero_index)
            block_cut = lax.dynamic_slice(region, corner, (images_here, WIN, WIN, features))
            pieces.append(block_cut.reshape(images_here, WIN * WIN, features))
    return jnp.stack(pieces, axis=1).reshape(images_here * 4, WIN * WIN, features)


def place_windows(windows, images_here, rows_start, cols_start):
    zero_index = jnp.zeros((), jnp.int32)
    features = windows.shape[-1]
    grouped = windows.reshape(images_here, 4, WIN, WIN, features)
    region = jnp.zeros((images_here, 2 * WIN, 2 * WIN, features), windows.dtype)
    for row_slot in range(2):
        for col_slot in range(2):
            corner = (zero_index, rows_start[row_slot], cols_start[col_slot], zero_index)
            present = lax.dynamic_slice(region, corner, (images_here, WIN, WIN, features))
            region = lax.dynamic_update_slice(
                region, present + grouped[:, 2 * row_slot + col_slot], corner
            )
    return region


def split_heads(packed, features):
    window_total = packed.shape[0]
    queries = packed[:, :, :features].reshape(window_total, WIN * WIN, HEADS, HEAD_DIM)
    key_rows = packed[:, :, features : 2 * features].reshape(
        window_total, WIN * WIN, HEADS, HEAD_DIM
    )
    value_rows = packed[:, :, 2 * features :].reshape(window_total, WIN * WIN, HEADS, HEAD_DIM)
    return (queries, key_rows, value_rows)


def relative_tables(rows_table, cols_table):
    places = jnp.arange(WIN)
    offset = places[:, None] - places[None, :] + WIN - 1
    chooser = (offset[:, :, None] == jnp.arange(2 * WIN - 1)[None, None, :]).astype(jnp.bfloat16)
    near_rows = jnp.einsum(
        "qkr,rc->qkc", chooser, rows_table, preferred_element_type=jnp.float32
    ).astype(jnp.bfloat16)
    near_cols = jnp.einsum(
        "qkr,rc->qkc", chooser, cols_table, preferred_element_type=jnp.float32
    ).astype(jnp.bfloat16)
    return (chooser, near_rows, near_cols)


def spread_table():
    keys = jnp.arange(WIN * WIN)
    places = jnp.arange(WIN)
    by_row = keys[None, :] // WIN == places[:, None]
    by_col = keys[None, :] % WIN == places[:, None]
    return jnp.concatenate([by_row, by_col], axis=0).astype(jnp.float32)


def window_scores(queries, key_rows, near_rows, near_cols, spread):
    window_total = queries.shape[0]
    grid_q = queries.reshape(window_total, WIN, WIN, HEADS, HEAD_DIM)
    products = jnp.einsum(
        "bqnc,bknc->bnqk", queries, key_rows, preferred_element_type=jnp.float32
    ) * HEAD_DIM ** (-0.5)
    along_rows = jnp.einsum(
        "bhwnc,hkc->bnhwk", grid_q, near_rows, preferred_element_type=jnp.float32
    )
    along_cols = jnp.einsum(
        "bhwnc,wkc->bnhwk", grid_q, near_cols, preferred_element_type=jnp.float32
    )
    joined = jnp.concatenate(
        [
            along_rows.reshape(window_total, HEADS, WIN * WIN, WIN),
            along_cols.reshape(window_total, HEADS, WIN * WIN, WIN),
        ],
        axis=-1,
    )
    relative = jnp.einsum("bnqr,rk->bnqk", joined, spread, precision=exact_mode)
    return products + relative


def on_device(
    image_in,
    cotangent,
    qkv_weight,
    out_weight,
    up_weight,
    down_weight,
    query_bias,
    value_bias,
    out_bias,
    up_bias,
    down_bias,
    first_gain,
    first_shift,
    second_gain,
    second_shift,
    rows_table,
    cols_table,
):
    images_here = image_in.shape[0]
    tile_side = image_in.shape[1]
    features = image_in.shape[3]
    tokens = images_here * tile_side * tile_side
    score_scale = HEAD_DIM ** (-0.5)
    full_qkv, full_out, full_up, full_down = gather_weights(
        qkv_weight, out_weight, up_weight, down_weight
    )
    rows_start, rows_valid = slot_starts(lax.axis_index("row") * tile_side, tile_side)
    cols_start, cols_valid = slot_starts(lax.axis_index("col") * tile_side, tile_side)
    slot_mask = jnp.stack(
        [
            rows_valid[0] & cols_valid[0],
            rows_valid[0] & cols_valid[1],
            rows_valid[1] & cols_valid[0],
            rows_valid[1] & cols_valid[1],
        ]
    ).astype(jnp.float32)
    window_mask = jnp.tile(slot_mask, images_here)[:, None, None]
    picture = image_in.astype(jnp.float32).reshape(tokens, features)
    normed, unit_first, inverse_first = layer_norm(picture, first_gain, first_shift)
    normed_low = normed.astype(jnp.bfloat16)
    bias_all = jnp.concatenate([query_bias, jnp.zeros_like(query_bias), value_bias])
    region = extend(normed_low.reshape(images_here, tile_side, tile_side, features))
    inputs_win = cut_windows(region, rows_start, cols_start)
    packed = (
        jnp.einsum("bpd,de->bpe", inputs_win, full_qkv, preferred_element_type=jnp.float32)
        + bias_all
    ).astype(jnp.bfloat16)
    chooser, near_rows, near_cols = relative_tables(rows_table, cols_table)
    spread = spread_table()
    queries, key_rows, value_rows = split_heads(packed, features)
    scores = window_scores(queries, key_rows, near_rows, near_cols, spread)
    row_max = jnp.max(scores, axis=-1, keepdims=True)
    exponent = jnp.exp(scores - row_max)
    row_total = jnp.sum(exponent, axis=-1, keepdims=True)
    log_total = row_max + jnp.log(row_total)
    blended = jnp.einsum(
        "bnqk,bknc->bqnc",
        (exponent / row_total).astype(jnp.bfloat16),
        value_rows,
        preferred_element_type=jnp.float32,
    )
    blended = (blended.reshape(-1, WIN * WIN, features) * window_mask).astype(jnp.bfloat16)
    mixed_own = fold_back(
        place_windows(blended, images_here, rows_start, cols_start), tile_side
    ).reshape(tokens, features)
    branch = jnp.dot(mixed_own, full_out, preferred_element_type=jnp.float32) + out_bias
    middle = picture + branch
    second_normed, unit_second, inverse_second = layer_norm(middle, second_gain, second_shift)
    second_low = second_normed.astype(jnp.bfloat16)
    hidden = jnp.dot(second_low, full_up, preferred_element_type=jnp.float32) + up_bias
    active = jax.nn.gelu(hidden, approximate=False).astype(jnp.bfloat16)
    result = middle + (jnp.dot(active, full_down, preferred_element_type=jnp.float32) + down_bias)
    image_out = result.astype(jnp.bfloat16).reshape(images_here, tile_side, tile_side, features)
    full_qkv, full_out, full_up, full_down = gather_weights(
        qkv_weight, out_weight, up_weight, down_weight
    )
    upstream = cotangent.astype(jnp.float32).reshape(tokens, features)
    grad_result = cotangent.reshape(tokens, features)
    total_down = jnp.dot(active.T, grad_result, preferred_element_type=jnp.float32)
    total_down_bias = jnp.sum(upstream, axis=0)
    grad_active = jnp.dot(grad_result, full_down.T, preferred_element_type=jnp.float32)
    gelu_value, gelu_back = jax.vjp(partial(jax.nn.gelu, approximate=False), hidden)
    grad_hidden = gelu_back(grad_active)[0].astype(jnp.bfloat16)
    total_up = jnp.dot(second_low.T, grad_hidden, preferred_element_type=jnp.float32)
    total_up_bias = jnp.sum(grad_hidden.astype(jnp.float32), axis=0)
    grad_second = rounded(jnp.dot(grad_hidden, full_up.T, preferred_element_type=jnp.float32))
    total_second_gain = jnp.sum(grad_second * unit_second, axis=0)
    total_second_shift = jnp.sum(grad_second, axis=0)
    grad_middle = upstream + norm_back(grad_second, unit_second, inverse_second, second_gain)
    grad_branch = grad_middle.astype(jnp.bfloat16)
    total_out = jnp.dot(mixed_own.T, grad_branch, preferred_element_type=jnp.float32)
    total_out_bias = jnp.sum(grad_branch.astype(jnp.float32), axis=0)
    grad_mixed = jnp.dot(grad_branch, full_out.T, preferred_element_type=jnp.float32).astype(
        jnp.bfloat16
    )
    grad_region = extend(grad_mixed.reshape(images_here, tile_side, tile_side, features))
    grad_blended = jnp.where(window_mask > 0, cut_windows(grad_region, rows_start, cols_start), 0)
    attention = jnp.exp(window_scores(queries, key_rows, near_rows, near_cols, spread) - log_total)
    grad_heads = grad_blended.reshape(-1, WIN * WIN, HEADS, HEAD_DIM)
    grad_attention = jnp.einsum(
        "bqnc,bknc->bnqk", grad_heads, value_rows, preferred_element_type=jnp.float32
    )
    inner_sum = jnp.sum(grad_attention * attention, axis=-1, keepdims=True)
    grad_scores = (attention * (grad_attention - inner_sum)).astype(jnp.bfloat16)
    grad_values = jnp.einsum(
        "bnqk,bqnc->bknc",
        attention.astype(jnp.bfloat16),
        grad_heads,
        preferred_element_type=jnp.float32,
    )
    grad_keys = (
        jnp.einsum("bnqk,bqnc->bknc", grad_scores, queries, preferred_element_type=jnp.float32)
        * score_scale
    )
    grad_queries = (
        jnp.einsum("bnqk,bknc->bqnc", grad_scores, key_rows, preferred_element_type=jnp.float32)
        * score_scale
    )
    window_total = queries.shape[0]
    grad_joined = jnp.einsum(
        "bnqk,rk->bnqr",
        grad_scores,
        spread.astype(jnp.bfloat16),
        preferred_element_type=jnp.float32,
    )
    grad_along_rows = grad_joined[..., :WIN].reshape(window_total, HEADS, WIN, WIN, WIN)
    grad_along_cols = grad_joined[..., WIN:].reshape(window_total, HEADS, WIN, WIN, WIN)
    grid_q = queries.astype(jnp.float32).reshape(window_total, WIN, WIN, HEADS, HEAD_DIM)
    extra_rows = jnp.einsum(
        "bnhwk,hkc->bhwnc", grad_along_rows, near_rows.astype(jnp.float32), precision=exact_mode
    )
    extra_cols = jnp.einsum(
        "bnhwk,wkc->bhwnc", grad_along_cols, near_cols.astype(jnp.float32), precision=exact_mode
    )
    grad_queries = grad_queries + (extra_rows + extra_cols).reshape(
        window_total, WIN * WIN, HEADS, HEAD_DIM
    )
    grad_near_rows = jnp.einsum("bnhwk,bhwnc->hkc", grad_along_rows, grid_q, precision=exact_mode)
    grad_near_cols = jnp.einsum("bnhwk,bhwnc->wkc", grad_along_cols, grid_q, precision=exact_mode)
    chooser_float = chooser.astype(jnp.float32)
    total_rows_table = jnp.einsum(
        "qkr,qkc->rc", chooser_float, grad_near_rows, precision=exact_mode
    )
    total_cols_table = jnp.einsum(
        "qkr,qkc->rc", chooser_float, grad_near_cols, precision=exact_mode
    )
    grad_packed = jnp.concatenate(
        [
            grad_queries.reshape(window_total, WIN * WIN, features),
            grad_keys.reshape(window_total, WIN * WIN, features),
            grad_values.reshape(window_total, WIN * WIN, features),
        ],
        axis=-1,
    ).astype(jnp.bfloat16)
    total_qkv = jnp.einsum(
        "bpd,bpe->de", inputs_win, grad_packed, preferred_element_type=jnp.float32
    )
    total_bias_all = jnp.sum(grad_packed.astype(jnp.float32), axis=(0, 1))
    grad_inputs = jnp.einsum(
        "bpe,de->bpd", grad_packed, full_qkv, preferred_element_type=jnp.float32
    ).astype(jnp.bfloat16)
    grad_first = fold_back(
        place_windows(grad_inputs, images_here, rows_start, cols_start), tile_side
    ).reshape(tokens, features)
    grad_first_float = grad_first.astype(jnp.float32)
    total_first_gain = jnp.sum(grad_first_float * unit_first, axis=0)
    total_first_shift = jnp.sum(grad_first_float, axis=0)
    grad_picture = grad_middle + norm_back(grad_first_float, unit_first, inverse_first, first_gain)
    image_grad = grad_picture.reshape(images_here, tile_side, tile_side, features)
    tile_sums = (
        lax.psum_scatter(
            total_qkv.astype(jnp.bfloat16), ("row", "col"), scatter_dimension=0, tiled=True
        ).astype(jnp.float32),
        lax.psum_scatter(
            total_out.astype(jnp.bfloat16), ("row", "col"), scatter_dimension=0, tiled=True
        ).astype(jnp.float32),
        lax.psum_scatter(
            total_up.astype(jnp.bfloat16), ("row", "col"), scatter_dimension=0, tiled=True
        ).astype(jnp.float32),
        lax.psum_scatter(
            total_down.astype(jnp.bfloat16), ("row", "col"), scatter_dimension=0, tiled=True
        ).astype(jnp.float32),
    )
    shard_sums = (
        lax.psum_scatter(
            tile_sums[0].astype(jnp.bfloat16), "img", scatter_dimension=1, tiled=True
        ).astype(jnp.float32),
        lax.psum_scatter(
            tile_sums[1].astype(jnp.bfloat16), "img", scatter_dimension=1, tiled=True
        ).astype(jnp.float32),
        lax.psum_scatter(
            tile_sums[2].astype(jnp.bfloat16), "img", scatter_dimension=1, tiled=True
        ).astype(jnp.float32),
        lax.psum_scatter(
            tile_sums[3].astype(jnp.bfloat16), "img", scatter_dimension=1, tiled=True
        ).astype(jnp.float32),
    )
    small_sums = lax.psum(
        (
            total_bias_all[:features],
            total_bias_all[2 * features :],
            total_out_bias,
            total_up_bias,
            total_down_bias,
            total_first_gain,
            total_first_shift,
            total_second_gain,
            total_second_shift,
            total_rows_table,
            total_cols_table,
        ),
        ("img", "row", "col"),
    )
    return (
        image_out,
        image_grad,
        shard_sums[0],
        shard_sums[1],
        shard_sums[2],
        shard_sums[3],
        small_sums[0],
        small_sums[1],
        small_sums[2],
        small_sums[3],
        small_sums[4],
        small_sums[5],
        small_sums[6],
        small_sums[7],
        small_sums[8],
        small_sums[9],
        small_sums[10],
    )


def solution(mesh):
    placed = (
        P("img", "row", "col", None),
        P("img", "row", "col", None),
        P(("row", "col"), "img"),
        P(("row", "col"), "img"),
        P(("row", "col"), "img"),
        P(("row", "col"), "img"),
        P(),
        P(),
        P(),
        P(),
        P(),
        P(),
        P(),
        P(),
        P(),
        P(),
        P(),
    )
    return jax.shard_map(
        on_device,
        mesh=mesh,
        in_specs=placed,
        out_specs=(
            P("img", "row", "col", None),
            P("img", "row", "col", None),
            P(("row", "col"), "img"),
            P(("row", "col"), "img"),
            P(("row", "col"), "img"),
            P(("row", "col"), "img"),
            P(),
            P(),
            P(),
            P(),
            P(),
            P(),
            P(),
            P(),
            P(),
            P(),
            P(),
        ),
        check_vma=False,
    )
```

profile of v0, /device:TPU:0, one launch (start us, length us, event | category | flops | bytes accessed | tf_op | source)
XLA Modules:
  0.0 906.2 jit_solution(11500586633763880601)
XLA Ops:
  48.7 31.1 %collective-permute-done.1 = bf16[2,28,12,768]{3,0,2,1:T(2,128)(2,1)S(1)} collective-permute-done((bf16[2,28,12,768]{3,0,2,1:T(2,128)(2,1)}, bf16[2,28,12,768]{3,0,2,1:T(2,128)(2,1)S(1)}, u32[]{:S(2)}, u32[]{:S(2)}) %collective-permute-start.1) | collective-permute-done | bytes 1032224 | tf_op jit(solution)/shard_map/ppermute | solution.py:20
  125.4 19.9 %fusion.26 = f32[8,12,14,14,14]{2,4,1,0,3:T(8,128)} fusion(bf16[14,14,64,1,1]{2,1,4,3,0:T(8,128)(2,1)S(1)} %fusion.70, bf16[8,14,14,12,64]{4,3,0,2,1:T(8,128)(2,1)} %reshape_reshape.4), kind=kOutput, calls=%fused_computation.51 | convolution fusion | flops 33718272 | bytes 3487232 | tf_op jit(solution)/shard_map/bhwnc,wkc->bnhwk/dot_general | solution.py:150
  145.3 14.0 %copy.418 = f32[8,12,14,14,14]{3,2,4,1,0:T(8,128)} copy(f32[8,12,14,14,14]{2,4,1,0,3:T(8,128)} %fusion.26) | data formatting | bytes 2107392 | tf_op jit(solution)/shard_map/reshape | solution.py:156
  168.3 15.7 %fusion.23 = f32[8,12,14,14,14]{3,4,1,0,2:T(8,128)S(1)} fusion(bf16[14,14,64,1,1]{2,1,4,3,0:T(8,128)(2,1)S(1)} %fusion.69, bf16[8,14,14,12,64]{4,3,0,2,1:T(8,128)(2,1)} %reshape_reshape.4), kind=kOutput, calls=%fused_computation.50 | convolution fusion | flops 33718272 | bytes 3487232 | tf_op jit(solution)/shard_map/bhwnc,hkc->bnhwk/dot_general | solution.py:147
  214.6 20.3 %fusion.125 = (f32[8,12,196]{2,1,0:T(8,128)S(1)}, f32[8,12,196,196]{2,3,1,0:T(8,128)}) fusion(pred[14,196]{1,0:T(8,128)(4,1)S(1)} %iota_compare_fusion.4, pred[14,196]{1,0:T(8,128)(4,1)S(1)} %iota_compare_fusion.5, f32[8,12,196,14]{2,3,1,0:T(8,128)S(1)} %copy-done.21, f32[8,12,196,14]{2,3,1,0:T(8,128)S(1)} %copy-done.22, f32[8,12,196,196]{2,3,1,0:T(8,128)} %fusion.127), kind=kOutput, calls=%fused_computation.219 | convolution fusion | flops 1250723840 | bytes 31691632 | tf_op jit(solution)/shard_map/bnqr,rk->bnqk/dot_general | solution.py:160
  234.9 12.3 %fusion = f32[8,12,196]{2,1,0:T(8,128)S(1)} fusion(f32[8,12,196,196]{2,3,1,0:T(8,128)} %get-tuple-element.68, f32[8,12,196]{2,1,0:T(8,128)S(1)} %get-tuple-element.67), kind=kLoop, calls=%fused_computation.6 | loop fusion | flops 7357056 | bytes 14902272 | tf_op jit(solution)/shard_map/reduce_sum | solution.py:218
  257.5 12.4 %copy.373 = f32[8,196,12,64]{3,2,0,1:T(8,128)} copy(f32[8,196,12,64]{1,3,2,0:T(8,128)} %fusion.37) | data formatting | bytes 9633792 | tf_op jit(solution)/shard_map/bnqk,bknc->bqnc/transpose | solution.py:220
  297.2 21.3 %collective-permute-done.2 = bf16[2,28,12,768]{3,0,2,1:T(2,128)(2,1)S(1)} collective-permute-done((bf16[2,28,12,768]{3,0,2,1:T(2,128)(2,1)S(1)}, bf16[2,28,12,768]{3,0,2,1:T(2,128)(2,1)S(1)}, u32[]{:S(2)}, u32[]{:S(2)}) %collective-permute-start.2) | collective-permute-done | bytes 1032224 | tf_op jit(solution)/shard_map/ppermute | solution.py:20
  338.7 20.4 %convert_reduce_fusion.1 = (f32[3072]{0:T(1024)}, bf16[512,3072]{1,0:T(8,128)(2,1)S(1)}, f32[512,3072]{1,0:T(8,128)}) fusion(f32[512,3072]{1,0:T(8,128)} %fusion.116, f32[3072]{0:T(1024)S(1)} %copy-done.55, bf16[512,768]{1,0:T(8,128)(2,1)S(1)} %bitcast.217, bf16[3072,768]{1,0:T(8,128)(2,1)} %all-gather.11.cloned.1.call-done), kind=kOutput, calls=%fused_computation.26 | convolution fusion | flops 2533880832 | bytes 21258240 | tf_op jit(solution)/shard_map/dot_general | solution.py:245
  382.7 15.6 %collective-permute-done.5 = bf16[2,28,12,768]{3,0,2,1:T(2,128)(2,1)} collective-permute-done((bf16[2,28,12,768]{3,0,2,1:T(2,128)(2,1)}, bf16[2,28,12,768]{3,0,2,1:T(2,128)(2,1)}, u32[]{:S(2)}, u32[]{:S(2)}) %collective-permute-start.5) | collective-permute-done | bytes 1032224 | tf_op jit(solution)/shard_map/ppermute | solution.py:20
  419.0 11.8 %fusion.38 = bf16[8,12,64,196]{3,2,1,0:T(8,128)(2,1)} fusion(f32[8,12,196,196]{2,3,1,0:T(8,128)} %get-tuple-element.68, f32[8,12,196]{2,1,0:T(8,128)S(1)} %log_add_fusion, bf16[8,196,12,64]{1,3,2,0:T(8,128)(2,1)S(1)} %bitcast.210, pred[8]{0:T(512)(128)(4,1)S(1)} %gt.13), kind=kOutput, calls=%fused_computation.66 | convolution fusion | flops 481840128 | bytes 19643912 | tf_op jit(solution)/shard_map/bnqk,bqnc->bknc/dot_general | solution.py:269
  430.8 14.9 %multiply_reduce_fusion = (f32[8,12,196]{2,1,0:T(8,128)S(1)}, f32[8,12,196,196]{2,3,1,0:T(8,128)}) fusion(f32[8,12,196,196]{2,3,1,0:T(8,128)} %get-tuple-element.68, f32[8,12,196]{2,1,0:T(8,128)S(1)} %log_add_fusion, bf16[8,196,12,64]{1,3,2,0:T(8,128)(2,1)} %bitcast.213, bf16[8,196,12,64]{1,3,2,0:T(8,128)(2,1)S(1)} %bitcast.211, pred[8]{0:T(512)(128)(4,1)S(1)} %gt.13), kind=kOutput, calls=%fused_computation.1 | convolution fusion | flops 484305024 | bytes 34470920 | tf_op jit(solution)/shard_map/bqnc,bknc->bnqk/dot_general | solution.py:264
  445.7 14.6 %multiply_convert_fusion = bf16[8,12,196,196]{2,3,1,0:T(8,128)(2,1)S(1)} fusion(f32[8,12,196,196]{2,3,1,0:T(8,128)} %get-tuple-element.72, f32[8,12,196,196]{2,3,1,0:T(8,128)} %get-tuple-element.68, f32[8,12,196]{2,1,0:T(8,128)S(1)} %get-tuple-element.71, f32[8,12,196]{2,1,0:T(8,128)S(1)} %log_add_fusion), kind=kLoop, calls=%fused_computation | loop fusion | flops 14751744 | bytes 37029888 | tf_op jit(solution)/shard_map/convert_element_type | solution.py:268
  481.3 16.1 %copy.383 = f32[8,12,14,14,14]{4,2,1,0,3:T(8,128)} copy(f32[8,12,14,14,14]{3,2,0,4,1:T(8,128)} %reshape.362) | data formatting | bytes 2107392 | tf_op jit(solution)/shard_map/reshape | solution.py:291
  506.0 24.1 %bitcast_add_fusion = f32[8,14,14,12,64]{4,2,3,0,1:T(8,128)} fusion(f32[14,64,8,12,14]{1,4,3,2,0:T(8,128)S(1)} %fusion.128, bf16[14,14,64,1,1]{2,1,4,3,0:T(8,128)(2,1)S(1)} %copy-done.33, f32[8,12,14,14,14]{3,2,0,4,1:T(8,128)S(1)} %copy-done.3), kind=kOutput, calls=%fused_computation.10 | convolution fusion | flops 203513856 | bytes 10712576 | tf_op jit(solution)/shard_map/bnhwk,hkc->bhwnc/dot_general | solution.py:293
  530.1 15.0 %copy.385 = f32[8,14,14,12,64]{4,0,3,2,1:T(8,128)} copy(f32[8,14,14,12,64]{4,2,3,0,1:T(8,128)} %bitcast_add_fusion) | data formatting | bytes 9633792 | tf_op jit(solution)/shard_map/add | solution.py:299
  584.2 12.3 %bitcast_convert_fusion = bf16[768,2304]{1,0:T(8,128)(2,1)} fusion(bf16[8,196,768]{2,1,0:T(8,128)(2,1)} %bitcast.222, bf16[8,196,768]{2,1,0:T(8,128)(2,1)} %copy.391, bf16[8,196,768]{2,1,0:T(8,128)(2,1)} %copy.390, bf16[8,196,768]{2,1,0:T(8,128)(2,1)} %copy.389), kind=kOutput, calls=%fused_computation.18 | convolution fusion | flops 5572509696 | bytes 13172736 | tf_op jit(solution)/shard_map/bpd,bpe->de/dot_general | solution.py:319
  630.2 16.8 %copy.400 = f32[8,12,14,14,14]{1,4,3,0,2:T(8,128)} copy(f32[8,12,14,14,14]{3,2,0,4,1:T(8,128)} %reshape.361) | data formatting | bytes 2107392 | tf_op jit(solution)/shard_map/reshape | solution.py:290
  670.7 16.6 %fusion.63 = f32[14,14,64]{2,1,0:T(8,128)} fusion(f32[8,12,14,14,14]{1,4,3,0,2:T(8,128)} %copy.400, bf16[8,14,14,12,64]{4,3,0,2,1:T(8,128)(2,1)S(1)} %bitcast.204), kind=kOutput, calls=%fused_computation.111 | convolution fusion | flops 202309632 | bytes 3512320 | tf_op jit(solution)/shard_map/bnhwk,bhwnc->hkc/dot_general | solution.py:302
  688.3 17.8 %copy.403 = f32[8,12,14,14,14]{1,4,2,0,3:T(8,128)} copy(f32[8,12,14,14,14]{3,2,0,4,1:T(8,128)} %reshape.362) | data formatting | bytes 2107392 | tf_op jit(solution)/shard_map/reshape | solution.py:291
  706.2 17.9 %fusion.66 = f32[14,14,64]{2,1,0:T(8,128)} fusion(f32[8,12,14,14,14]{1,4,2,0,3:T(8,128)} %copy.403, bf16[8,14,14,12,64]{4,3,0,2,1:T(8,128)(2,1)} %reshape_reshape.4), kind=kOutput, calls=%fused_computation.112 | convolution fusion | flops 202309632 | bytes 3512320 | tf_op jit(solution)/shard_map/bnhwk,bhwnc->wkc/dot_general | solution.py:303
  745.2 21.7 %reduce-scatter.23.cloned.1.call-done = bf16[192,768]{1,0:T(8,128)(2,1)} async-done(((bf16[3072,768]{1,0:T(8,128)(2,1)}), bf16[192,768]{1,0:T(8,128)(2,1)}) %reduce-scatter.23.cloned.1.call-update) | async-done | bytes 294928 | tf_op jit(solution)/shard_map/reduce_scatter | solution.py:344
  779.0 66.9 %reduce-scatter.19.cloned.1.call-done = bf16[48,3072]{1,0:T(8,128)(2,1)} async-done(((bf16[768,3072]{1,0:T(8,128)(2,1)}), bf16[48,3072]{1,0:T(8,128)(2,1)}) %reduce-scatter.19.cloned.1.call-update) | async-done | bytes 294928 | tf_op jit(solution)/shard_map/reduce_scatter | solution.py:341
  848.6 41.7 %all-reduce = (f32[768]{0:T(1024)}, f32[768]{0:T(1024)}, f32[768]{0:T(1024)}, f32[3072]{0:T(1024)}, f32[768]{0:T(1024)}, /*index=5*/f32[768]{0:T(1024)}, f32[768...) all-reduce(f32[768]{0:T(1024)S(1)} %get-tuple-element.66, ...), channel_id=1, replica_groups=mesh['img'=2,'row'=4,'col'=4] {'img','row','col'}, use_global_device_ids=true, to_apply=%region_20.21 | all-reduce | flops 12672 | bytes 101376 | tf_op jit(solution)/shard_map/psum | solution.py:362
  (329 shorter events, 399.2 us)
Async XLA Ops:
  7.2 85.0 %all-gather.5.cloned.1.call-start = ((), (), s32[]{:S(2)}) async-start(), calls=%async_computation.8 | async-start | bytes 3760128 | tf_op jit(solution)/shard_map/all_gather | solution.py:49
  15.9 312.6 %all-gather.7.cloned.1.call-start = ((), (), s32[]{:S(2)}) async-start(), calls=%async_computation.9 | async-start | bytes 1253376 | tf_op jit(solution)/shard_map/all_gather | solution.py:50
  21.0 310.4 %all-gather.9.cloned.1.call-start = ((), (), s32[]{:S(2)}) async-start(), calls=%async_computation.10 | async-start | bytes 5013504 | tf_op jit(solution)/shard_map/all_gather | solution.py:51
  28.1 310.7 %all-gather.11.cloned.1.call-start = ((), (), s32[]{:S(2)}) async-start(), calls=%async_computation.11 | async-start | bytes 5013504 | tf_op jit(solution)/shard_map/all_gather | solution.py:52
  34.9 8.9 collective-permute-start
  43.6 561.6 %reduce-scatter.17.cloned.1.call-start = ((), (), s32[]{:S(2)}) async-start(), calls=%async_computation.13 | async-start | bytes 1253376 | tf_op jit(solution)/shard_map/reduce_scatter | solution.py:338
  46.0 33.7 %collective-permute-start.1 = (bf16[2,28,12,768]{3,0,2,1:T(2,128)(2,1)}, bf16[2,28,12,768]{3,0,2,1:T(2,128)(2,1)S(1)}, u32[]{:S(2)}, u32[]{:S(2)}) collective-permute-start(bf16[2,28,12,768]{3,0,2,1:T(2,128)(2,1)} %pad_maximum_fusion.4), channel_id=1, source_target_pairs={{1,0},{2,1},{3,2},{5,4},{6,5},{7,6},{9,8},{10,9},{11,10},{13,12},{... | collective-permute-start | bytes 3096584 | tf_op jit(solution)/shard_map/ppermute | solution.py:20
  48.6 119.7 %copy-start.32 = (bf16[14,14,64,1,1]{2,1,4,3,0:T(8,128)(2,1)}, bf16[14,14,64,1,1]{2,1,4,3,0:T(8,128)(2,1)S(1)}, u32[]{:S(2)}) copy-start(bf16[14,14,64,1,1]{2,1,4,3,0:T(8,128)(2,1)S(1)} %fusion.69) | copy-start | bytes 75268
  48.6 166.0 %copy-start.46 = (pred[14,196]{1,0:T(8,128)(4,1)}, pred[14,196]{1,0:T(8,128)(4,1)S(1)}, u32[]{:S(2)}) copy-start(pred[14,196]{1,0:T(8,128)(4,1)S(1)} %iota_compare_fusion.4) | copy-start | bytes 8236
  48.6 166.0 %copy-start.48 = (pred[14,196]{1,0:T(8,128)(4,1)}, pred[14,196]{1,0:T(8,128)(4,1)S(1)}, u32[]{:S(2)}) copy-start(pred[14,196]{1,0:T(8,128)(4,1)S(1)} %iota_compare_fusion.5) | copy-start | bytes 8236
  293.3 25.1 %collective-permute-start.2 = (bf16[2,28,12,768]{3,0,2,1:T(2,128)(2,1)S(1)}, bf16[2,28,12,768]{3,0,2,1:T(2,128)(2,1)S(1)}, u32[]{:S(2)}, u32[]{:S(2)}) collective-permute-start(bf16[2,28,12,768]{3,0,2,1:T(2,128)(2,1)S(1)} %slice.133), channel_id=1, source_target_pairs={{0,1},{1,2},{2,3},{4,5},{5,6},{6,7},{8,9},{9,10},{10,11},{12,13},{... | collective-permute-start | bytes 3096584 | tf_op jit(solution)/shard_map/ppermute | solution.py:20
  320.3 5.2 collective-permute-start.3
  366.0 10.0 %collective-permute-start.4 = (bf16[2,12,16,768]{3,0,2,1:T(2,128)(2,1)S(1)}, bf16[2,12,16,768]{3,0,2,1:T(2,128)(2,1)S(1)}, u32[]{:S(2)}, u32[]{:S(2)}) collective-permute-start(bf16[2,12,16,768]{3,0,2,1:T(2,128)(2,1)S(1)} %copy.498), channel_id=1, source_target_pairs={{4,0},{8,4},{12,8},{5,1},{9,5},{13,9},{6,2},{10,6},{14,10},{7,3},{... | collective-permute-start | bytes 1769480 | tf_op jit(solution)/shard_map/ppermute | solution.py:20
  378.3 20.0 %collective-permute-start.5 = (bf16[2,28,12,768]{3,0,2,1:T(2,128)(2,1)}, bf16[2,28,12,768]{3,0,2,1:T(2,128)(2,1)}, u32[]{:S(2)}, u32[]{:S(2)}) collective-permute-start(bf16[2,28,12,768]{3,0,2,1:T(2,128)(2,1)} %slice.140), channel_id=1, source_target_pairs={{1,0},{2,1},{3,2},{5,4},{6,5},{7,6},{9,8},{10,9},{11,10},{13,12},{... | collective-permute-start | bytes 3096584 | tf_op jit(solution)/shard_map/ppermute | solution.py:20
  382.7 355.8 %reduce-scatter.15.cloned.1.call-start = ((), (), s32[]{:S(2)}) async-start(), calls=%async_computation.12 | async-start | bytes 3760128 | tf_op jit(solution)/shard_map/reduce_scatter | solution.py:335
  596.6 145.3 %reduce-scatter.27.cloned.1.call-start = ((), (), s32[]{:S(2)}) async-start(), calls=%async_computation.18 | async-start | bytes 294912
  606.8 160.1 %reduce-scatter.23.cloned.1.call-start = ((), (), s32[]{:S(2)}) async-start(), calls=%async_computation.16 | async-start | bytes 5013504 | tf_op jit(solution)/shard_map/reduce_scatter | solution.py:344
  613.6 232.3 %reduce-scatter.19.cloned.1.call-start = ((), (), s32[]{:S(2)}) async-start(), calls=%async_computation.14 | async-start | bytes 5013504 | tf_op jit(solution)/shard_map/reduce_scatter | solution.py:341
  622.1 271.8 %reduce-scatter.25.cloned.1.call-start = ((), (), s32[]{:S(2)}) async-start(), calls=%async_computation.17 | async-start | bytes 884736
  665.4 58.6 %collective-permute-start.6 = (bf16[2,28,12,768]{3,0,2,1:T(2,128)(2,1)S(1)}, bf16[2,28,12,768]{3,0,2,1:T(2,128)(2,1)}, u32[]{:S(2)}, u32[]{:S(2)}) collective-permute-start(bf16[2,28,12,768]{3,0,2,1:T(2,128)(2,1)S(1)} %slice.148), channel_id=1, source_target_pairs={{0,1},{1,2},{2,3},{4,5},{5,6},{6,7},{8,9},{9,10},{10,11},{12,13},{... | collective-permute-start | bytes 3096584 | tf_op jit(solution)/shard_map/ppermute | solution.py:20
  727.9 15.6 %collective-permute-start.7 = (bf16[2,12,16,768]{3,0,2,1:T(2,128)(2,1)S(1)}, bf16[2,12,16,768]{3,0,2,1:T(2,128)(2,1)S(1)}, u32[]{:S(2)}, u32[]{:S(2)}) collective-permute-start(bf16[2,12,16,768]{3,0,2,1:T(2,128)(2,1)S(1)} %fusion.89), channel_id=1, source_target_pairs={{0,4},{4,8},{8,12},{1,5},{5,9},{9,13},{2,6},{6,10},{10,14},{3,7},{... | collective-permute-start | bytes 1769480 | tf_op jit(solution)/shard_map/ppermute | solution.py:20
  740.6 155.1 %reduce-scatter.29.cloned.1.call-start = ((), (), s32[]{:S(2)}) async-start(), calls=%async_computation.19 | async-start | bytes 589824
  768.9 121.4 %copy-start.11 = (f32[512,768]{1,0:T(8,128)S(1)}, f32[512,768]{1,0:T(8,128)}, u32[]{:S(2)}) copy-start(f32[512,768]{1,0:T(8,128)} %copy-done.10) | copy-start | bytes 4718596
  768.9 128.6 %reduce-scatter.21.cloned.1.call-start = ((), (), s32[]{:S(2)}) async-start(), calls=%async_computation.15 | async-start | bytes 442368 | tf_op jit(solution)/shard_map/reduce_scatter | solution.py:355
  (68 other events, 1218.2 us)
Sparse Core Ops, SparseCore 0:
  16.1 51.6 all-gather.4
  70.0 39.8 all-gather.6
  112.2 52.3 all-gather.8
  166.8 51.7 all-gather.10
  382.8 69.9 reduce-scatter.16
  596.7 77.9 reduce-scatter.14
  677.4 10.0 reduce-scatter.26
  691.4 75.4 reduce-scatter.22
  771.3 74.5 reduce-scatter.18
  848.0 14.8 reduce-scatter.24
  865.2 13.0 reduce-scatter.28
  880.4 12.1 reduce-scatter.20
where the time goes:
time: 915 us; the launch traced here: 906 us
  matrix products  282 us (31%)
  local copies, waits for them, and re-layouts  241 us (26%)
  waiting for transfers between devices  165 us (18%)
  other arithmetic  105 us (11%)
  blocking collectives  69.6 us (8%)
  starting transfers between devices  27.7 us (3%)
  between operations  15.7 us (2%)
    ppermute x8, waiting for transfers between devices, from_behind(): return lax.ppermute(block, axis, route)  75.9 us
    reduce_scatter x1, waiting for transfers between devices, on_device(): lax.psum_scatter(total_up.astype(jnp.bfloat16), ('row', 'col'), scatter_d...  66.9 us
    psum x1, blocking collectives, on_device(): lax.psum((total_bias_all[:features], total_bias_all[2 * features:], total...  41.7 us
    reshape x3, local copies, waits for them, and re-layouts, on_device(): grad_joined[..., WIN:].reshape(window_total, HEADS, WIN, WIN, WIN)  41.3 us
    ppermute x8, starting transfers between devices, from_behind(): return lax.ppermute(block, axis, route)  27.2 us
    reshape x2, local copies, waits for them, and re-layouts, on_device(): grad_joined[..., :WIN].reshape(window_total, HEADS, WIN, WIN, WIN)  24.3 us
    dot_general x1, matrix products, on_device(): jnp.einsum('bnhwk,hkc->bhwnc', grad_along_rows, near_rows.astype(jnp.floa...  24.1 us
    reshape x2, local copies, waits for them, and re-layouts, window_scores(): along_cols.reshape(window_total, HEADS, WIN * WIN, WIN)  22.9 us
  transfers between devices with their start and end apart: 20, of which 7 were waited for; matrix products, arithmetic and copies ran while one was open for 65% of the time, Pallas kernels for 0%

commit v1 on v0

v1 whole, which is shorter than its diff:
```python
import functools

import jax
import jax.numpy as jnp
import numpy as np
from jax import lax
from jax.experimental import pallas as pl
from jax.experimental.pallas import tpu as pltpu
from jax.sharding import PartitionSpec as P

MESH = pl.DeviceIdType.MESH


def place():
    return lax.axis_index("img"), lax.axis_index("row"), lax.axis_index("col")


def side_owner(window_row, image):
    return lax.rem(window_row, 2), 3 - image - 2 * (window_row // 2)


def piece_target(kind, image, row, col):
    last_row, last_col = row == 3, col == 3
    side_row, side_col = side_owner(row, image)
    next_row, next_col = side_owner(lax.rem(row + 1, 4), image)
    if kind == 0:
        return (jnp.where(last_row, 3 - image, row + 1), col, jnp.where(last_row, 2, image))
    if kind == 1:
        return (jnp.where(last_col, side_row, row), jnp.where(last_col, side_col, col + 1), jnp.where(last_col, 2, image))
    target_row = jnp.where(last_row, 3 - image, jnp.where(last_col, next_row, row + 1))
    target_col = jnp.where(last_col, jnp.where(last_row, 3, next_col), col + 1)
    slot = jnp.where(last_row & last_col, 3, jnp.where(last_row | last_col, 2, image))
    return (target_row, target_col, slot)


def arrivals(row, col):
    wide = row >= 2
    side_row = row + 2 * (1 - col // 2)
    table = []
    for image in range(2):
        table.append((image, 0, row > 0))
        table.append((image, 1, col > 0))
        table.append((image, 2, (row > 0) & (col > 0)))
    table.append((2, 0, wide))
    table.append((2, 1, jnp.logical_not(wide)))
    table.append((2, 2, jnp.where(wide, col, side_row) > 0))
    table.append((3, 2, wide & (col == 3)))
    return table


def tile_part(ref, image, kind):
    if kind == 0:
        return ref.at[image, pl.ds(8, 8), pl.ds(0, 2)]
    if kind == 1:
        return ref.at[image, pl.ds(0, 14), pl.ds(1, 1)]
    return ref.at[image, pl.ds(8, 8), pl.ds(1, 1)]


def window_part(ref, slot, kind):
    if kind == 0:
        return ref.at[slot, pl.ds(0, 8), pl.ds(1, 2)]
    if kind == 1:
        return ref.at[slot, pl.ds(8, 14), pl.ds(0, 1)]
    return ref.at[slot, pl.ds(0, 8), pl.ds(0, 1)]


def greet(img, row, col, pairs=True):
    barrier = pltpu.get_barrier_semaphore()
    for row_step in range(4):
        for col_step in range(4):
            if row_step or col_step:
                pl.semaphore_signal(
                    barrier,
                    inc=1,
                    device_id={"row": lax.rem(row + row_step, 4), "col": lax.rem(col + col_step, 4)},
                    device_id_type=MESH,
                )
    if pairs:
        pl.semaphore_signal(barrier, inc=1, device_id={"img": 1 - img}, device_id_type=MESH)
    pl.semaphore_wait(barrier, 16 if pairs else 15)


CHUNKS = ((0, 0, 640), (0, 640, 1152), (1, 0, 384), (2, 0, 768), (2, 768, 1536), (3, 0, 128), (3, 128, 384))


def links(shards, fulls, wsend, wrecv, wloc):
    img, row, col = place()
    y_row = lax.rem(row + 2, 4)
    core_row = row + 1 - 2 * lax.rem(row, 2)
    other = 1 - img
    sent = []

    def rows_of(w, rw, half=None):
        kb = fulls[w].shape[0] // 4
        if half is None:
            return pl.ds(pl.multiple_of(rw * kb, kb), kb)
        return pl.ds(pl.multiple_of(rw * kb + half * (kb // 2), kb // 2), kb // 2)

    def cols_of(n, im):
        w, lo, hi = CHUNKS[n]
        nb = fulls[w].shape[1] // 2
        return pl.ds(pl.multiple_of(im * nb + lo, 128), hi - lo)

    def block(n, rw, im, half=None):
        w = CHUNKS[n][0]
        return fulls[w].at[rows_of(w, rw, half), cols_of(n, im)]

    def slot(n, cl):
        w = CHUNKS[n][0]
        k16 = fulls[w].shape[0] // 16
        return fulls[w].at[pl.ds(pl.multiple_of((row * 4 + cl) * k16, k16), k16), cols_of(n, img)]

    def source(n):
        w, lo, hi = CHUNKS[n]
        return shards[w].at[:, pl.ds(lo, hi - lo)]

    def push(n, k, where, target, start=None):
        def copy():
            ref = block(n, *where)
            return pltpu.make_async_remote_copy(
                src_ref=source(n) if start else ref,
                dst_ref=slot(n, col) if start else ref,
                send_sem=wsend.at[n, k],
                recv_sem=wrecv.at[n, k],
                device_id=target(),
                device_id_type=MESH,
            )

        copy().start()
        sent.append(copy)

    def arrive(n, k, ref):
        pltpu.make_async_copy(ref, ref, wrecv.at[n, k]).wait()

    def along_col(n):
        pltpu.make_async_copy(source(n), slot(n, col), wloc.at[n]).start()
        for d in range(1, 4):
            push(n, d - 1, (row, img), lambda d=d: {"col": lax.rem(col + d, 4)}, True)

    def first(n):
        pltpu.make_async_copy(source(n), slot(n, col), wloc.at[n]).wait()
        for d in range(1, 4):
            arrive(n, d - 1, slot(n, lax.rem(col + 4 - d, 4)))
        push(n, 3, (row, img, 0), lambda: {"img": other})
        push(n, 4, (row, img, 1), lambda: {"row": y_row})
        push(n, 5, (row, img), lambda: {"row": core_row})

    def second(n):
        arrive(n, 3, block(n, row, other, 0))
        arrive(n, 4, block(n, y_row, img, 1))
        push(n, 6, (row, img, 0), lambda: {"row": y_row})
        push(n, 7, (row, other, 0), lambda: {"row": y_row})
        push(n, 8, (row, img, 1), lambda: {"img": other})
        push(n, 9, (y_row, img, 1), lambda: {"img": other})
        push(n, 10, (row, other, 0), lambda: {"row": core_row})
        push(n, 11, (y_row, img, 1), lambda: {"row": core_row})

    def third(n):
        arrive(n, 6, block(n, y_row, img, 0))
        arrive(n, 7, block(n, y_row, other, 0))
        arrive(n, 8, block(n, row, other, 1))
        arrive(n, 9, block(n, y_row, other, 1))
        push(n, 12, (y_row, img, 0), lambda: {"row": core_row})
        push(n, 13, (y_row, other, 0), lambda: {"row": core_row})
        push(n, 14, (row, other, 1), lambda: {"row": core_row})
        push(n, 15, (y_row, other, 1), lambda: {"row": core_row})

    def last(n):
        core_y = lax.rem(core_row + 2, 4)
        arrive(n, 5, block(n, core_row, img))
        arrive(n, 10, block(n, core_row, other, 0))
        arrive(n, 11, block(n, core_y, img, 1))
        arrive(n, 12, block(n, core_y, img, 0))
        arrive(n, 13, block(n, core_y, other, 0))
        arrive(n, 14, block(n, core_row, other, 1))
        arrive(n, 15, block(n, core_y, other, 1))

    return along_col, first, second, third, last, sent


def window_moves(tiles, raws, send, recv, loc):
    img, row, col = place()

    def each(t, act):
        for image in range(2):
            for kind in range(3):
                target_row, target_col, target_slot = piece_target(kind, image, row, col)
                here = (target_row == row) & (target_col == col)
                part = tile_part(tiles[t], image, kind)
                goal = window_part(raws[t], target_slot, kind)
                act(here, part, goal, send.at[t, image, kind], recv.at[t, target_slot, kind], target_row, target_col)

    def remote(part, goal, leave, arrival, target_row, target_col):
        return pltpu.make_async_remote_copy(
            src_ref=part,
            dst_ref=goal,
            send_sem=leave,
            recv_sem=arrival,
            device_id={"row": target_row, "col": target_col},
            device_id_type=MESH,
        )

    def own(t, image):
        return pltpu.make_async_copy(tiles[t].at[image, pl.ds(0, 14)], raws[t].at[image, pl.ds(8, 14), pl.ds(1, 2)], loc.at[t, image])

    def start(t):
        for image in range(2):
            own(t, image).start()

        def act(here, part, goal, leave, arrival, target_row, target_col):
            @pl.when(here)
            def _():
                pltpu.make_async_copy(part, goal, arrival).start()

            @pl.when(jnp.logical_not(here))
            def _():
                remote(part, goal, leave, arrival, target_row, target_col).start()

        each(t, act)

    def arrived(t):
        for image in range(2):
            own(t, image).wait()
        for slot_index, kind, present in arrivals(row, col):
            part = window_part(raws[t], slot_index, kind)

            @pl.when(present)
            def _():
                pltpu.make_async_copy(part, part, recv.at[t, slot_index, kind]).wait()

    def left(t):
        def act(here, part, goal, leave, arrival, target_row, target_col):
            @pl.when(jnp.logical_not(here))
            def _():
                remote(part, goal, leave, arrival, target_row, target_col).wait_send()

        each(t, act)

    return start, arrived, left


BF = jnp.bfloat16
F32 = jnp.float32
ROWS = 704
SPAN = 800
FEATURES = 768
EPS = 1e-06


def row_params(step, row, col):
    wide = row >= 2
    side_row = row + 2 * (1 - col // 2)
    third_step = step - 28
    in_corner = wide & (third_step >= 8)
    slot = jnp.where(step < 14, 0, jnp.where(step < 28, 1, jnp.where(in_corner, 3, 2)))
    place_row = jnp.where(step < 14, step, jnp.where(step < 28, step - 14, jnp.where(in_corner, third_step - 8, third_step)))
    full = step < 28
    row_start = jnp.where(full, 8 - 2 * row, jnp.where(wide, 0, 8 - 2 * side_row))
    col_start = jnp.where(full, 8 - 2 * col, jnp.where(wide & jnp.logical_not(in_corner), 8 - 2 * col, 0))
    width = jnp.where(full, 14, jnp.where(wide & jnp.logical_not(in_corner), 14, 8))
    alive = jnp.where(full, True, jnp.where(in_corner, col == 3, jnp.where(wide, True, third_step < 14)))
    return slot, jnp.minimum(place_row + row_start, 21), col_start, jnp.where(alive, width, 0)


def window_params(window, row, col):
    wide = row >= 2
    start = jnp.where(window < 2, 14 * window, jnp.where(window == 2, 28, 36))
    tall = jnp.where(window < 2, 14, jnp.where((window == 2) & jnp.logical_not(wide), 14, 8))
    width = jnp.where(window < 2, 14, jnp.where((window == 2) & wide, 14, 8))
    return start, tall, width


def window_count(row, col):
    return jnp.where((row >= 2) & (col == 3), 4, 3)


def unit_of(values):
    center = values - jnp.mean(values, axis=-1, keepdims=True)
    inverse = lax.rsqrt(jnp.mean(center * center, axis=-1, keepdims=True) + EPS)
    return center * inverse, inverse


def relative_layout(backward):
    take = np.zeros((2, 2, 27, 128), np.float32)
    for parity in range(2):
        base = 64 if parity == 0 else 0
        for j in range(27):
            for copy in (0,) if backward else (0, 32):
                take[parity, 0, 26 - j, (base - 13 + j + copy) % 128] = 1
                if backward:
                    take[parity, 1, j, base + 16 + j] = 1
                else:
                    take[parity, 1, 26 - j, (base + 3 + j + copy) % 128] = 1
    return take


def table_operand(rows_table, cols_table, backward):
    take = jnp.asarray(relative_layout(backward), BF)
    parts = []
    for parity in range(2):
        both = []
        for which, table in ((0, rows_table), (1, cols_table)):
            both.append(lax.dot_general(table, take[parity, which], (((0,), (0,)), ((), ())), preferred_element_type=F32).astype(BF))
        block = jnp.concatenate(both, axis=1)
        zero = jnp.zeros_like(block)
        parts.append(jnp.concatenate([block, zero] if parity == 0 else [zero, block], axis=0))
    return jnp.concatenate(parts, axis=1)


def table_grads(sums):
    take = jnp.asarray(relative_layout(True), F32)
    grads = []
    for which in range(2):
        total = 0.0
        for parity in range(2):
            part = sums[64 * parity : 64 * parity + 64, 256 * parity + 128 * which : 256 * parity + 128 * which + 128]
            total = total + lax.dot_general(take[parity, which], part, (((1,), (1,)), ((), ())), precision=lax.Precision.HIGHEST)
        grads.append(total)
    return grads


def run_all(act):
    for i in range(0, len(act), 2):
        act[i](act[i + 1])


def open_kernel(weights, x_ref, c_ref, gain, shift, bias, tab, *refs):
    img, row, col = place()
    greet(img, row, col, weights)
    if weights:
        shards, refs = refs[:4], refs[4:]
    else:
        wq, refs = refs[0], refs[1:]
    xw, cw, n1_turned, qkv_s, probs, o, o_turned = refs[:7]
    refs = refs[7:]
    if weights:
        fulls, refs = refs[:4], refs[4:]
        wq = fulls[0]
    rawx, rawc, n1, send, recv, loc = refs[:6]
    if weights:
        along_col, first, second, third, last, sent = links(shards, fulls, *refs[6:])
    window_start, window_arrived, window_left = window_moves((x_ref, c_ref), (rawx, rawc), send, recv, loc)
    places = lax.broadcasted_iota(jnp.int32, (16, 1), 0)

    def cut_one(raw, step):
        slot, raw_row, col_start, width = row_params(step, row, col)
        wide_rows = raw[slot, raw_row].reshape(24, FEATURES).astype(F32)
        keep = places < width
        return keep, jnp.where(keep, pltpu.roll(wide_rows, lax.rem(24 - col_start, 24), 0)[:16], 0.0)

    def cut_x(step, _):
        at = pl.ds(pl.multiple_of(step * 16, 16), 16)
        keep, x = cut_one(rawx, step)
        xw[at, :] = x.astype(BF)
        unit, _inverse = unit_of(x)
        n1[at, :] = jnp.where(keep, unit * gain[...] + shift[...], 0.0).astype(BF)
        return 0

    def cut_c(step, _):
        at = pl.ds(pl.multiple_of(step * 16, 16), 16)
        _keep, c = cut_one(rawc, step)
        cw[at, :] = c.astype(BF)
        return 0

    def project(step, _):
        at = pl.ds(pl.multiple_of(step * 352, 32), 352)
        for part_index in range(3):
            lanes = slice(part_index * FEATURES, (part_index + 1) * FEATURES)
            part = jnp.dot(n1[at, :], wq[:, lanes], preferred_element_type=F32) + bias[:, lanes]
            qkv_s[at, lanes] = part.astype(BF)
        return 0

    def turn(source, goal):
        def step(i, _):
            lanes = pl.ds(pl.multiple_of(i * 128, 128), 128)
            goal[lanes, :] = source[0:ROWS, lanes].T
            return 0

        lax.fori_loop(0, FEATURES // 128, step, 0)

    if weights:
        along_col(0)
    window_start(0)
    if weights:
        along_col(1)
    else:
        window_start(1)
    o[...] = jnp.zeros_like(o)
    if weights:
        first(0)
        along_col(2)
        first(1)
        along_col(3)
        second(0)
    window_arrived(0)
    lax.fori_loop(0, 44, cut_x, 0)
    steps = []
    if weights:
        first(2)
        along_col(4)
        second(1)
        third(0)
        first(3)
        along_col(5)
        third(1)
        last(0)
        last(1)
        steps = [
            (second, 2),
            (first, 4, along_col, 6),
            (second, 3),
            (third, 2),
            (first, 5, window_start, 1),
            (second, 4),
            (third, 3),
            (first, 6),
            (second, 5),
            (third, 4),
            (second, 6),
            (third, 5),
            (third, 6),
        ]
    lax.fori_loop(0, 2, project, 0)
    row_of = lax.broadcasted_iota(jnp.int32, (224, 1), 0)
    lane = lax.broadcasted_iota(jnp.int32, (1, 128), 1)
    key_place = lax.broadcasted_iota(jnp.int32, (224, 128), 0)
    key_lane = lax.broadcasted_iota(jnp.int32, (224, 128), 1)
    key_a, key_b = key_place // 16, key_place % 16

    def pair(index, _):
        for turn_index, act in enumerate(steps):
            pl.when(index == turn_index)(functools.partial(run_all, act))
        window, pair_index = index // 6, index % 6
        start, tall, width = window_params(window, row, col)
        at = pl.ds(pl.multiple_of(start * 16, 16), 224)
        alive = (row_of // 16 < tall) & (row_of % 16 < width)
        lanes = lambda third: pl.ds(pl.multiple_of(third * FEATURES + pair_index * 128, 128), 128)
        q = jnp.where(alive, qkv_s[at, lanes(0)].astype(F32), 0.0)
        k = jnp.where(alive, qkv_s[at, lanes(1)].astype(F32), 0.0)
        v = jnp.where(alive, qkv_s[at, lanes(2)].astype(F32), bias[:, lanes(2)].astype(BF).astype(F32)).astype(BF)
        terms = jnp.dot(q.astype(BF), tab[...], preferred_element_type=F32)
        outs = []
        for parity in range(2):
            base = 64 if parity == 0 else 0
            own = (lane < 64) if parity == 0 else (lane >= 64)
            rel_rows = jnp.concatenate(
                [pltpu.roll(terms[16 * a : 16 * a + 16, 256 * parity : 256 * parity + 128], a, 1) for a in range(14)], axis=0
            )
            rel_cols = jnp.concatenate(
                [
                    pltpu.roll(terms[16 * a : 16 * a + 16, 256 * parity + 128 : 256 * parity + 256], 0, 1, stride=1, stride_axis=0)
                    for a in range(14)
                ],
                axis=0,
            )
            on = lane - base
            in_rows = ((on >= 0) & (on < 14)) | ((on >= 32) & (on < 46))
            in_cols = ((on >= 16) & (on < 30)) | ((on >= 48) & (on < 62))
            rel = jnp.where(in_rows, rel_rows, jnp.where(in_cols, rel_cols, 0.0))
            rough = rel.astype(BF).astype(F32)
            fine = jnp.where(on >= 32, rel - rough, rough)
            fine = jnp.where(on == 14, -1e30, fine)
            q_side = jnp.where(own, q * 0.125, fine).astype(BF)
            key_on = key_lane - base
            hot = jnp.where(
                key_on == 14,
                jnp.where(key_b >= 14, 1.0, 0.0),
                jnp.where(
                    (key_on % 32 < 14) & (key_a == key_on % 32),
                    1.0,
                    jnp.where((key_on % 32 >= 16) & (key_on % 32 < 30) & (key_b == key_on % 32 - 16), 1.0, 0.0),
                ),
            )
            k_side = jnp.where(own, k, hot).astype(BF)
            scores = lax.dot_general(q_side, k_side, (((1,), (1,)), ((), ())), preferred_element_type=F32)
            exponent = jnp.exp(scores - jnp.max(scores, axis=-1, keepdims=True))
            p = (exponent * (1.0 / jnp.sum(exponent, axis=-1, keepdims=True))).astype(BF)
            probs[window, 2 * pair_index + parity] = p
            outs.append(jnp.dot(p, v, preferred_element_type=F32))
        blended = jnp.where(lane < 64, outs[0], outs[1])
        out_lanes = pl.ds(pl.multiple_of(pair_index * 128, 128), 128)
        o_at = pl.ds(pl.multiple_of(start * 16, 16), 224)
        o[o_at, out_lanes] = jnp.where(alive, blended, 0.0).astype(BF)
        return 0

    lax.fori_loop(0, window_count(row, col) * 6, pair, 0)
    turn(n1, n1_turned)
    turn(o, o_turned)
    window_arrived(1)
    lax.fori_loop(0, 44, cut_c, 0)
    if weights:
        for n in range(2, len(CHUNKS)):
            last(n)
        for copy in sent:
            copy().wait_send()
    window_left(0)
    window_left(1)


def open_windows(x, c, shards, gain, shift, bias, tab):
    vm = pl.BlockSpec(memory_space=pltpu.VMEM)
    an = pl.BlockSpec(memory_space=pl.ANY)
    shape = jax.ShapeDtypeStruct
    dma = pltpu.SemaphoreType.DMA
    chunks = len(CHUNKS)
    weights = lax.axis_size("img") == 2
    if weights:
        given, wholes = list(shards), [(768, 2304), (768, 768), (768, 3072), (3072, 768)]
    else:
        widened = [lax.all_gather(w, "img", axis=1, tiled=True) for w in shards]
        gathered = [lax.all_gather(w, ("row", "col"), axis=0, tiled=True) for w in widened]
        given, wholes = gathered[:1], []
    raw = pltpu.VMEM((4, 22, 3, 8, FEATURES), BF)
    outs = pl.pallas_call(
        functools.partial(open_kernel, weights),
        out_shape=[
            shape((ROWS, FEATURES), BF),
            shape((ROWS, FEATURES), BF),
            shape((FEATURES, ROWS), BF),
            shape((SPAN, 3 * FEATURES), BF),
            shape((4, 12, 224, 224), BF),
            shape((SPAN, FEATURES), BF),
            shape((FEATURES, ROWS), BF),
        ]
        + [shape(s, BF) for s in wholes],
        in_specs=[vm] * (6 + len(given)),
        out_specs=[vm] * 7 + ([vm, an, an, an] if weights else []),
        scratch_shapes=[raw, raw, pltpu.VMEM((ROWS, FEATURES), BF), dma((2, 2, 3)), dma((2, 4, 3)), dma((2, 2))]
        + ([dma((chunks, 16)), dma((chunks, 16)), dma((chunks,))] if weights else []),
        compiler_params=pltpu.CompilerParams(collective_id=0, has_side_effects=True, vmem_limit_bytes=67043328),
    )(x.reshape(2, 16, 2, 8, 768), c.reshape(2, 16, 2, 8, 768), gain, shift, bias, tab, *given)
    return list(outs) if weights else list(outs) + gathered


BLOCK = 176
FF = 3072
CHUNK = 512


def nt(a, b):
    return lax.dot_general(a, b, (((1,), (1,)), ((), ())), preferred_element_type=F32)


def norm_back(grad, unit, inverse, gain):
    scaled = grad * gain
    first_mean = jnp.mean(scaled, axis=-1, keepdims=True)
    second_mean = jnp.mean(scaled * unit, axis=-1, keepdims=True)
    return inverse * (scaled - first_mean - unit * second_mean)


def fold_rows(values):
    total = values[0:8]
    for i in range(1, values.shape[0] // 8):
        total = total + values[8 * i : 8 * i + 8]
    return total


def middle_kernel(o, xw, cw, wo, wu, wd, out_bias, up_bias, down_bias, gain, shift, result, n2, g, dh, da, do, dm, sums, up_sum, y_s, d_s):
    @pl.when(pl.program_id(0) == 0)
    def _():
        sums[...] = jnp.zeros_like(sums)
        up_sum[...] = jnp.zeros_like(up_sum)

    mid = xw[...].astype(F32) + (jnp.dot(o[...], wo[...], preferred_element_type=F32) + out_bias[...])
    unit, inverse = unit_of(mid)
    low = (unit * gain[...] + shift[...]).astype(BF)
    n2[...] = low
    y_s[...] = mid + down_bias[...]
    d_s[...] = jnp.zeros_like(d_s)
    dz = cw[...]

    def hidden(step, _):
        lanes = pl.ds(pl.multiple_of(step * CHUNK, CHUNK), CHUNK)
        h = jnp.dot(n2[...], wu[:, lanes], preferred_element_type=F32) + up_bias[:, lanes]
        up = nt(cw[...], wd[lanes, :])
        phi = 0.5 * (1.0 + lax.erf(h * 0.7071067811865476))
        slope = phi + h * (jnp.exp(-0.5 * h * h) * 0.3989422804014327)
        active = (h * phi).astype(BF)
        back = (up * slope).astype(BF)
        g[:, lanes] = active
        dh[:, lanes] = back
        up_sum[:, lanes] += fold_rows(back.astype(F32))
        y_s[...] += jnp.dot(active, wd[lanes, :], preferred_element_type=F32)
        d_s[...] += nt(back, wu[:, lanes])
        return 0

    lax.fori_loop(0, FF // CHUNK, hidden, 0)
    result[...] = y_s[...].astype(BF)
    mid = xw[...].astype(F32) + (jnp.dot(o[...], wo[...], preferred_element_type=F32) + out_bias[...])
    unit, inverse = unit_of(mid)
    grad = d_s[...].astype(BF).astype(F32)
    up = cw[...].astype(F32)
    grad_mid = up + norm_back(grad, unit, inverse, gain[...])
    low_grad = grad_mid.astype(BF)
    dm[...] = grad_mid
    da[...] = low_grad
    do[...] = nt(low_grad, wo[...]).astype(BF)
    sums[0] += fold_rows(low_grad.astype(F32))
    sums[1] += fold_rows(up)
    sums[2] += fold_rows(grad * unit)
    sums[3] += fold_rows(grad)


def middle(o, xw, cw, wo, wu, wd, out_bias, up_bias, down_bias, gain, shift):
    vm = pl.BlockSpec(memory_space=pltpu.VMEM)
    shape = jax.ShapeDtypeStruct
    rows = lambda n: pl.BlockSpec((BLOCK, n), lambda i: (i, 0))
    whole = lambda s: pl.BlockSpec(s, lambda i: (0,) * len(s), pipeline_mode=pl.Buffered(1))
    return pl.pallas_call(
        middle_kernel,
        grid=(ROWS // BLOCK,),
        out_shape=[
            shape((ROWS, FEATURES), BF),
            shape((ROWS, FEATURES), BF),
            shape((ROWS, FF), BF),
            shape((ROWS, FF), BF),
            shape((ROWS, FEATURES), BF),
            shape((ROWS, FEATURES), BF),
            shape((ROWS, FEATURES), F32),
            shape((4, 8, FEATURES), F32),
            shape((8, FF), F32),
        ],
        in_specs=[rows(FEATURES)] * 3
        + [whole((FEATURES, FEATURES)), whole((FEATURES, FF)), whole((FF, FEATURES))]
        + [whole((1, FEATURES)), whole((1, FF)), whole((1, FEATURES)), whole((1, FEATURES)), whole((1, FEATURES))],
        out_specs=[rows(FEATURES), rows(FEATURES), rows(FF), rows(FF), rows(FEATURES), rows(FEATURES), rows(FEATURES)]
        + [pl.BlockSpec((4, 8, FEATURES), lambda i: (0, 0, 0)), pl.BlockSpec((8, FF), lambda i: (0, 0))],
        scratch_shapes=[pltpu.VMEM((BLOCK, FEATURES), F32)] * 2,
        compiler_params=pltpu.CompilerParams(vmem_limit_bytes=62 << 20),
    )(o, xw, cw, wo, wu, wd, out_bias, up_bias, down_bias, gain, shift)


def back_kernel(do, probs, qkv_s, o, xw, dm, result, wq, tab, bias, gain, dqkv, raw_r, raw_g, bias_sums, norm_sums, table_sums, do_s, dqkv_s, image_grad):
    row, col = lax.axis_index("row"), lax.axis_index("col")
    do_s[0:ROWS, :] = do[...]
    dqkv_s[...] = jnp.zeros_like(dqkv_s)
    bias_sums[...] = jnp.zeros_like(bias_sums)
    norm_sums[...] = jnp.zeros_like(norm_sums)
    table_sums[...] = jnp.zeros_like(table_sums)
    row_of = lax.broadcasted_iota(jnp.int32, (224, 1), 0)
    lane = lax.broadcasted_iota(jnp.int32, (1, 128), 1)
    key_place = lax.broadcasted_iota(jnp.int32, (224, 128), 0)
    key_lane = lax.broadcasted_iota(jnp.int32, (224, 128), 1)
    key_a, key_b = key_place // 16, key_place % 16

    def pair(index, _):
        window, pair_index = index // 6, index % 6
        start, tall, width = window_params(window, row, col)
        at = pl.ds(pl.multiple_of(start * 16, 16), 224)
        alive = (row_of // 16 < tall) & (row_of % 16 < width)
        lanes = lambda third: pl.ds(pl.multiple_of(third * FEATURES + pair_index * 128, 128), 128)
        q = jnp.where(alive, qkv_s[at, lanes(0)].astype(F32), 0.0)
        k = jnp.where(alive, qkv_s[at, lanes(1)].astype(F32), 0.0)
        v = jnp.where(alive, qkv_s[at, lanes(2)].astype(F32), bias[:, lanes(2)].astype(BF).astype(F32))
        grad = jnp.where(alive, do_s[at, lanes(0)].astype(F32), 0.0)
        product = grad * jnp.where(alive, o[at, lanes(0)].astype(F32), 0.0)
        q_turned = q.T.astype(BF)
        grad_turned = grad.T.astype(BF)
        value_parts, key_parts, query_parts, table_parts = [], [], [], []
        for parity in range(2):
            base = 64 if parity == 0 else 0
            own = (lane < 64) if parity == 0 else (lane >= 64)
            half = slice(64 * parity, 64 * parity + 64)
            inner = jnp.sum(jnp.where(own, product, 0.0), axis=-1, keepdims=True)
            rough = inner.astype(BF).astype(F32)
            on = lane - base
            grad_side = jnp.where(own, grad, jnp.where(on == 0, rough, jnp.where(on == 1, inner - rough, 0.0))).astype(BF)
            v_side = jnp.where(own, v, jnp.where((on == 0) | (on == 1), -1.0, 0.0)).astype(BF)
            centered = nt(grad_side, v_side)
            p = probs[window, 2 * pair_index + parity]
            ds = (p.astype(F32) * centered).astype(BF)
            value_parts.append(jnp.dot(grad_turned[half], p, preferred_element_type=F32))
            key_parts.append(jnp.dot(q_turned[half], ds, preferred_element_type=F32))
            key_on = key_lane - base
            hot = jnp.where(
                (key_on >= 0) & (key_on < 14) & (key_a == key_on),
                1.0,
                jnp.where((key_on >= 16) & (key_on < 30) & (key_b == 29 - key_on), 1.0, 0.0),
            )
            k_side = jnp.where(own, k * 0.125, hot).astype(BF)
            wide = jnp.dot(ds, k_side, preferred_element_type=F32)
            query_parts.append(wide)
            by_rows = jnp.where((on >= 0) & (on < 14), wide, 0.0)
            by_cols = jnp.where((on >= 16) & (on < 30), wide, 0.0)
            table_parts.append(
                jnp.concatenate([pltpu.roll(by_rows[16 * a : 16 * a + 16], (128 - a) % 128, 1) for a in range(14)], axis=0)
            )
            table_parts.append(
                jnp.concatenate(
                    [pltpu.roll(by_cols[16 * a : 16 * a + 16], 0, 1, stride=1, stride_axis=0) for a in range(14)], axis=0
                )
            )
        turned = jnp.concatenate(table_parts, axis=1).astype(BF)
        dq = jnp.where(lane < 64, query_parts[0], query_parts[1]) + nt(turned, tab[...])
        table_sums[...] += jnp.dot(q_turned, turned, preferred_element_type=F32)
        dk = jnp.concatenate(key_parts, axis=0).T * 0.125
        dv = jnp.concatenate(value_parts, axis=0).T
        dq = jnp.where(alive, dq, 0.0).astype(BF)
        dv = dv.astype(BF)
        bias_sums[0, :, lanes(0)] += fold_rows(dq.astype(F32))
        bias_sums[1, :, lanes(0)] += fold_rows(dv.astype(F32))
        dqkv_s[at, lanes(0)] = dq
        dqkv_s[at, lanes(1)] = jnp.where(alive, dk, 0.0).astype(BF)
        dqkv_s[at, lanes(2)] = jnp.where(alive, dv.astype(F32), 0.0).astype(BF)
        return 0

    lax.fori_loop(0, window_count(row, col) * 6, pair, 0)
    dqkv[...] = dqkv_s[0:ROWS, :]

    def finish(step, _):
        at = pl.ds(pl.multiple_of(step * 176, 16), 176)
        grad = nt(dqkv_s[at, :], wq[...]).astype(BF).astype(F32)
        unit, inverse = unit_of(xw[at, :].astype(F32))
        image_grad[at, :] = dm[at, :] + norm_back(grad, unit, inverse, gain[...])
        norm_sums[0] += fold_rows(grad * unit)
        norm_sums[1] += fold_rows(grad)
        return 0

    lax.fori_loop(0, 4, finish, 0)

    def spread(step, _):
        slot, raw_row, col_start, width = row_params(step, row, col)
        at = pl.ds(pl.multiple_of(step * 16, 16), 16)

        @pl.when(width > 0)
        def _():
            for source, raw in ((result, raw_r), (image_grad, raw_g)):
                values = source[at, :].astype(F32)
                values = jnp.concatenate([values, jnp.zeros((8, FEATURES), F32)], axis=0)
                raw[slot, raw_row] = pltpu.roll(values, col_start, 0).astype(BF).reshape(3, 8, FEATURES)

        return 0

    lax.fori_loop(0, 44, spread, 0)


def back(do, probs, qkv, o, xw, dm, result, wq, tab, bias, gain):
    vm = pl.BlockSpec(memory_space=pltpu.VMEM)
    shape = jax.ShapeDtypeStruct
    return pl.pallas_call(
        back_kernel,
        out_shape=[
            shape((ROWS, 3 * FEATURES), BF),
            shape((4, 22, 3, 8, FEATURES), BF),
            shape((4, 22, 3, 8, FEATURES), BF),
            shape((2, 8, FEATURES), F32),
            shape((2, 8, FEATURES), F32),
            shape((128, 512), F32),
        ],
        in_specs=[vm] * 11,
        out_specs=[vm] * 6,
        scratch_shapes=[pltpu.VMEM((SPAN, FEATURES), BF), pltpu.VMEM((SPAN, 3 * FEATURES), BF), pltpu.VMEM((ROWS, FEATURES), F32)],
        compiler_params=pltpu.CompilerParams(vmem_limit_bytes=62 << 20),
    )(do, probs, qkv, o, xw, dm, result, wq, tab, bias, gain)


def source_tiles(row, col):
    wide = row >= 2
    side_row = row + 2 * (1 - col // 2)
    table = []
    for image in range(2):
        table.append((image, 0, image, row - 1, col, row > 0))
        table.append((image, 1, image, row, col - 1, col > 0))
        table.append((image, 2, image, row - 1, col - 1, (row > 0) & (col > 0)))
    third_image = jnp.where(wide, 3 - row, 1 - lax.rem(col, 2))
    table.append((2, 0, third_image, 3, col, wide))
    table.append((2, 1, third_image, side_row, 3, jnp.logical_not(wide)))
    table.append((2, 2, third_image, jnp.where(wide, 3, side_row - 1), jnp.where(wide, col - 1, 3), jnp.where(wide, col, side_row) > 0))
    table.append((3, 2, 3 - row, 3, 3, wide & (col == 3)))
    return table


def return_kernel(raw_r, raw_g, out, grad_out, below_r, right_r, both_r, below_g, right_g, both_g, send, recv):
    img, row, col = place()
    greet(img, row, col, False)
    raws = (raw_r, raw_g)
    landing = ((below_r, right_r, both_r), (below_g, right_g, both_g))

    for t in range(2):
        for slot, kind, image, tile_row, tile_col, present in source_tiles(row, col):
            part = window_part(raws[t], slot, kind)
            goal = landing[t][kind].at[image]
            arrival = recv.at[t, image, kind]
            here = (tile_row == row) & (tile_col == col)

            @pl.when(present & here)
            def _():
                pltpu.make_async_copy(part, goal, arrival).start()

            @pl.when(present & jnp.logical_not(here))
            def _():
                pltpu.make_async_remote_copy(
                    src_ref=part,
                    dst_ref=goal,
                    send_sem=send.at[t, slot, kind],
                    recv_sem=arrival,
                    device_id={"row": jnp.maximum(tile_row, 0), "col": jnp.maximum(tile_col, 0)},
                    device_id_type=MESH,
                ).start()

    for t in range(2):
        for image in range(2):
            for kind in range(3):
                goal = landing[t][kind].at[image]
                pltpu.make_async_copy(goal, goal, recv.at[t, image, kind]).wait()
    places = lax.broadcasted_iota(jnp.int32, (16, 1), 0)
    left = places < 14 - 2 * col

    def rows16(values):
        return values.reshape(16, FEATURES).astype(F32)

    def right_half(values):
        low = values.reshape(8, FEATURES).astype(F32)
        return jnp.concatenate([low, low], axis=0)

    for image in range(2):

        def merge(tile_row, _):
            top = tile_row < 14 - 2 * row
            upper = jnp.minimum(tile_row, 13)
            lower = jnp.maximum(tile_row - 8, 0)
            for t, goal in ((0, out), (1, grad_out)):
                below, right, both = landing[t]
                own = jnp.where(top, rows16(raws[t][image, 8 + upper, 1:3]), rows16(below[image, lower]))
                beside = jnp.where(top, right_half(right[image, upper]), right_half(both[image, lower]))
                goal[image, tile_row] = jnp.where(left, own, beside).astype(goal.dtype)
            return 0

        lax.fori_loop(0, 16, merge, 0)
    for t in range(2):
        for slot, kind, image, tile_row, tile_col, present in source_tiles(row, col):
            here = (tile_row == row) & (tile_col == col)

            @pl.when(present & jnp.logical_not(here))
            def _():
                pltpu.make_async_remote_copy(
                    src_ref=window_part(raws[t], slot, kind),
                    dst_ref=landing[t][kind].at[image],
                    send_sem=send.at[t, slot, kind],
                    recv_sem=recv.at[t, image, kind],
                    device_id={"row": jnp.maximum(tile_row, 0), "col": jnp.maximum(tile_col, 0)},
                    device_id_type=MESH,
                ).wait_send()


def give_back(raw_r, raw_g):
    vm = pl.BlockSpec(memory_space=pltpu.VMEM)
    shape = jax.ShapeDtypeStruct
    dma = pltpu.SemaphoreType.DMA
    pieces = [pltpu.VMEM((2, 8, 2, 8, FEATURES), BF), pltpu.VMEM((2, 14, 1, 8, FEATURES), BF), pltpu.VMEM((2, 8, 1, 8, FEATURES), BF)]
    return pl.pallas_call(
        return_kernel,
        out_shape=[shape((2, 16, 16, FEATURES), BF), shape((2, 16, 16, FEATURES), F32)],
        in_specs=[vm] * 2,
        out_specs=[vm] * 2,
        scratch_shapes=pieces + pieces + [dma((2, 4, 3)), dma((2, 2, 3))],
        compiler_params=pltpu.CompilerParams(collective_id=2, has_side_effects=True, vmem_limit_bytes=62 << 20),
    )(raw_r, raw_g)


SUM_CHUNKS = ((1, 0, 384), (3, 0, 128), (3, 128, 384), (2, 0, 768), (2, 768, 1536), (0, 0, 640), (0, 640, 1152))
WHOLES = ((768, 2304), (768, 768), (768, 3072), (3072, 768))


def table_taker():
    take = relative_layout(True)
    out = np.zeros((4, 128, 128), np.float32)
    for parity in range(2):
        for which in range(2):
            out[2 * parity + which, :, 64 * which : 64 * which + 27] = take[parity, which].T
    return out


def finish_kernel(turned_n1, dqkv, turned_o, da, n2, dh, g, dz, raw_r, raw_g, sums, up_sum, bias_sums, norm_sums, table_sums, taker, *refs):
    out, grad_out, gq, go, gu, gd, small_out, table_out = refs[:8]
    below_r, right_r, both_r, below_g, right_g, both_g, own_r, own_g = refs[8:16]
    turned_n2, turned_g = refs[16:18]
    full = refs[18:22]
    small, table, small_land, table_land, small_z, table_z = refs[22:28]
    chunks = len(SUM_CHUNKS)
    lands = [refs[28 + 5 * n : 33 + 5 * n] for n in range(chunks)]
    send, recv, own_sem, wsend, wrecv, ssend, srecv = refs[28 + 5 * chunks :]
    img, row, col = place()
    greet(img, row, col)
    raws = (raw_r, raw_g)
    landing = ((below_r, right_r, both_r), (below_g, right_g, both_g))
    owns = (own_r, own_g)
    y_row = lax.rem(row + 2, 4)
    core_row = row + 1 - 2 * lax.rem(row, 2)
    core_y = lax.rem(core_row + 2, 4)
    other = 1 - img
    left_turned = (turned_n1, turned_o, turned_n2, turned_g)
    left_side = (None, None, n2, g)
    right_side = (dqkv, da, dh, dz)
    grads = (gq, go, gu, gd)
    copies = []

    for t in range(2):
        for image in range(2):
            pltpu.make_async_copy(raws[t].at[image, pl.ds(8, 14), pl.ds(1, 2)], owns[t].at[image], own_sem.at[t, image]).start()
        for slot, kind, image, tile_row, tile_col, present in source_tiles(row, col):
            part = window_part(raws[t], slot, kind)
            goal = landing[t][kind].at[image]
            arrival = recv.at[t, image, kind]
            here = (tile_row == row) & (tile_col == col)

            @pl.when(present & here)
            def _():
                pltpu.make_async_copy(part, goal, arrival).start()

            @pl.when(present & jnp.logical_not(here))
            def _():
                pltpu.make_async_remote_copy(
                    src_ref=part,
                    dst_ref=goal,
                    send_sem=send.at[t, slot, kind],
                    recv_sem=arrival,
                    device_id={"row": jnp.maximum(tile_row, 0), "col": jnp.maximum(tile_col, 0)},
                    device_id_type=MESH,
                ).start()

    def turn(w):
        source, goal = left_side[w], left_turned[w]

        def step(i, _):
            lanes = pl.ds(pl.multiple_of(i * 128, 128), 128)
            goal[lanes, :] = source[0:ROWS, lanes].T
            return 0

        lax.fori_loop(0, WHOLES[w][0] // 128, step, 0)

    def size(n):
        w, lo, hi = SUM_CHUNKS[n]
        return WHOLES[w][0] // 4, WHOLES[w][1] // 2, lo, hi - lo

    def block(n, rw, im, half=None):
        kb, nb, lo, width = size(n)
        cols = pl.ds(pl.multiple_of(im * nb + lo, 128), width)
        if half is None:
            return full[SUM_CHUNKS[n][0]].at[pl.ds(pl.multiple_of(rw * kb, kb), kb), cols]
        return full[SUM_CHUNKS[n][0]].at[pl.ds(pl.multiple_of(rw * kb + half * (kb // 2), kb // 2), kb // 2), cols]

    def push(n, k, src, dst, target):
        c = pltpu.make_async_remote_copy(
            src_ref=src, dst_ref=dst, send_sem=wsend.at[n, k], recv_sem=wrecv.at[n, k], device_id=target, device_id_type=MESH
        )
        c.start()
        copies.append(c)

    def arrive(n, k, ref):
        pltpu.make_async_copy(ref, ref, wrecv.at[n, k]).wait()

    def add(goal, part, rows):
        step_rows = 48

        def step(i, _):
            at = pl.ds(pl.multiple_of(i * step_rows, 16), step_rows)
            goal[at, :] = (goal[at, :].astype(F32) + part[at, :].astype(F32)).astype(BF)
            return 0

        lax.fori_loop(0, rows // step_rows, step, 0)

    def product(n, rw):
        w = SUM_CHUNKS[n][0]
        kb, nb, lo, width = size(n)
        rows = pl.ds(pl.multiple_of(rw * kb, kb), kb)
        for im in range(2):
            at = slice(im * nb + lo, im * nb + lo + width)
            full[w][rows, at] = jnp.dot(left_turned[w][rows, :], right_side[w][0:ROWS, at], preferred_element_type=F32).astype(BF)

    def pair_stage(n):
        land = lands[n][0]
        for j, rw in enumerate((core_row, core_y)):
            product(n, rw)
            for im in range(2):
                push(n, 2 * j + im, block(n, rw, im), land.at[j, im], {"row": core_row})
        for rw in (row, y_row):
            product(n, rw)

    def first(n):
        kb, nb, lo, width = size(n)
        for j, rw in enumerate((row, y_row)):
            for im in range(2):
                arrive(n, 2 * j + im, lands[n][0].at[j, im])
                add(block(n, rw, im), lands[n][0].at[j, im], kb)
        land = lands[n][1]
        for im in range(2):
            push(n, 4 + im, block(n, y_row, im, 0), land.at[im], {"row": y_row})
        land = lands[n][2]
        push(n, 6, block(n, row, other, 1), land.at[0], {"img": other})
        push(n, 7, block(n, y_row, other, 1), land.at[1], {"img": other})

    def second(n):
        kb, nb, lo, width = size(n)
        for im in range(2):
            arrive(n, 4 + im, lands[n][1].at[im])
            add(block(n, row, im, 0), lands[n][1].at[im], kb // 2)
        push(n, 8, block(n, row, other, 0), lands[n][3].at[0], {"img": other})
        for j, rw in enumerate((row, y_row)):
            arrive(n, 6 + j, lands[n][2].at[j])
            add(block(n, rw, img, 1), lands[n][2].at[j], kb // 2)
        push(n, 9, block(n, y_row, img, 1), lands[n][3].at[1], {"row": y_row})

    def shard(n, cl):
        kb, nb, lo, width = size(n)
        cols = pl.ds(pl.multiple_of(img * nb + lo, 128), width)
        return full[SUM_CHUNKS[n][0]].at[pl.ds(pl.multiple_of(row * kb + cl * (kb // 4), kb // 4), kb // 4), cols]

    def third(n):
        kb, nb, lo, width = size(n)
        for half in range(2):
            arrive(n, 8 + half, lands[n][3].at[half])
            add(block(n, row, img, half), lands[n][3].at[half], kb // 2)
        for d in range(1, 4):
            cl = lax.rem(col + d, 4)
            push(n, 9 + d, shard(n, cl), lands[n][4].at[d - 1], {"col": cl})

    def fourth(n):
        w, lo, hi = SUM_CHUNKS[n]
        for d in range(1, 4):
            arrive(n, 9 + d, lands[n][4].at[d - 1])
        mine = shard(n, col)

        def step(i, _):
            at = pl.ds(pl.multiple_of(i * 48, 16), 48)
            total = mine[at, :].astype(F32)
            for d in range(3):
                total = total + lands[n][4][d, at, :].astype(F32)
            grads[w][at, lo:hi] = total
            return 0

        lax.fori_loop(0, WHOLES[w][0] // 16 // 48, step, 0)

    def over_rows(values):
        return jnp.sum(values, axis=0, keepdims=True)

    small[0] = jnp.zeros((16, FEATURES), F32)
    lines = [bias_sums[0], bias_sums[1], sums[0], sums[1], norm_sums[0], norm_sums[1], sums[2], sums[3]]
    for i, values in enumerate(lines):
        small[0, i : i + 1, :] = over_rows(values)
    for i in range(4):
        small[0, 8 + i : 9 + i, :] = over_rows(up_sum[:, i * FEATURES : (i + 1) * FEATURES])
    exact = lax.Precision.HIGHEST
    total = jnp.zeros((64, 128), F32)
    for parity in range(2):
        for which in range(2):
            part = table_sums[64 * parity : 64 * parity + 64, 256 * parity + 128 * which : 256 * parity + 128 * which + 128]
            total = total + jnp.dot(part, taker[2 * parity + which], precision=exact, preferred_element_type=F32)
    table[0] = total
    hops = ({"row": core_row}, {"row": y_row}, {"img": other})

    def small_push(k, src, dst, target):
        c = pltpu.make_async_remote_copy(
            src_ref=src, dst_ref=dst, send_sem=ssend.at[k], recv_sem=srecv.at[k], device_id=target, device_id_type=MESH
        )
        c.start()
        copies.append(c)
        return c

    def small_step(i):
        if 0 < i <= 3:
            for k, (acc, land) in enumerate(((small, small_land), (table, table_land))):
                pltpu.make_async_copy(land.at[i - 1], land.at[i - 1], srecv.at[2 * (i - 1) + k]).wait()
                acc[i] = acc[i - 1] + land[i - 1]
        if i < 3:
            for k, (acc, land) in enumerate(((small, small_land), (table, table_land))):
                small_push(2 * i + k, acc.at[i], land.at[i], hops[i])
        if i == 3:
            small_z[col] = small[3]
            table_z[col] = table[3]
            for d in range(1, 4):
                cl = lax.rem(col + d, 4)
                small_push(4 + 2 * d, small.at[3], small_z.at[col], {"col": cl})
                small_push(5 + 2 * d, table.at[3], table_z.at[col], {"col": cl})
        if i == 4:
            for d in range(1, 4):
                cl = lax.rem(col + 4 - d, 4)
                pltpu.make_async_copy(small_z.at[cl], small_z.at[cl], srecv.at[4 + 2 * d]).wait()
                pltpu.make_async_copy(table_z.at[cl], table_z.at[cl], srecv.at[5 + 2 * d]).wait()
            small_out[...] = (small_z[0] + small_z[1]) + (small_z[2] + small_z[3])
            table_out[...] = (table_z[0] + table_z[1]) + (table_z[2] + table_z[3])

    turned = {0, 1}
    for n in range(chunks + 4):
        if n < chunks:
            w = SUM_CHUNKS[n][0]
            if w not in turned:
                turned.add(w)
                turn(w)
            pair_stage(n)
        if n < 5:
            small_step(n)
        if 0 <= n - 1 < chunks:
            first(n - 1)
        if 0 <= n - 2 < chunks:
            second(n - 2)
        if 0 <= n - 3 < chunks:
            third(n - 3)
        if 0 <= n - 4 < chunks:
            fourth(n - 4)

    for t in range(2):
        for image in range(2):
            pltpu.make_async_copy(owns[t].at[image], owns[t].at[image], own_sem.at[t, image]).wait()
            for kind in range(3):
                goal = landing[t][kind].at[image]
                pltpu.make_async_copy(goal, goal, recv.at[t, image, kind]).wait()
    places = lax.broadcasted_iota(jnp.int32, (16, 1), 0)
    left = places < 14 - 2 * col

    def rows16(values):
        return values.reshape(16, FEATURES).astype(F32)

    def right_half(values):
        low = values.reshape(8, FEATURES).astype(F32)
        return jnp.concatenate([low, low], axis=0)

    for image in range(2):

        def merge(tile_row, _):
            top = tile_row < 14 - 2 * row
            upper = jnp.minimum(tile_row, 13)
            lower = jnp.maximum(tile_row - 8, 0)
            for t, goal in ((0, out), (1, grad_out)):
                below, right, both = landing[t]
                own = jnp.where(top, rows16(owns[t][image, upper]), rows16(below[image, lower]))
                beside = jnp.where(top, right_half(right[image, upper]), right_half(both[image, lower]))
                goal[image, tile_row] = jnp.where(left, own, beside).astype(goal.dtype)
            return 0

        lax.fori_loop(0, 16, merge, 0)
    for t in range(2):
        for slot, kind, image, tile_row, tile_col, present in source_tiles(row, col):
            here = (tile_row == row) & (tile_col == col)

            @pl.when(present & jnp.logical_not(here))
            def _():
                pltpu.make_async_remote_copy(
                    src_ref=window_part(raws[t], slot, kind),
                    dst_ref=landing[t][kind].at[image],
                    send_sem=send.at[t, slot, kind],
                    recv_sem=recv.at[t, image, kind],
                    device_id={"row": jnp.maximum(tile_row, 0), "col": jnp.maximum(tile_col, 0)},
                    device_id_type=MESH,
                ).wait_send()

    for c in copies:
        c.wait_send()


def finish(n1, dqkv, o, da, n2, dh, g, dz, raw_r, raw_g, sums, up_sum, bias_sums, norm_sums, table_sums):
    vm = pl.BlockSpec(memory_space=pltpu.VMEM)
    an = pl.BlockSpec(memory_space=pl.ANY)
    shape = jax.ShapeDtypeStruct
    dma = pltpu.SemaphoreType.DMA
    pieces = [pltpu.VMEM((2, 8, 2, 8, FEATURES), BF), pltpu.VMEM((2, 14, 1, 8, FEATURES), BF), pltpu.VMEM((2, 8, 1, 8, FEATURES), BF)]
    lands = []
    for w, lo, hi in SUM_CHUNKS:
        kb, width = WHOLES[w][0] // 4, hi - lo
        lands += [
            pltpu.VMEM((2, 2, kb, width), BF),
            pltpu.VMEM((2, kb // 2, width), BF),
            pltpu.VMEM((2, kb // 2, width), BF),
            pltpu.VMEM((2, kb // 2, width), BF),
            pltpu.VMEM((3, kb // 4, width), BF),
        ]
    chunks = len(SUM_CHUNKS)
    return pl.pallas_call(
        finish_kernel,
        out_shape=[shape((2, 16, 16, FEATURES), BF), shape((2, 16, 16, FEATURES), F32)]
        + [shape((k // 16, n // 2), F32) for k, n in WHOLES]
        + [shape((16, FEATURES), F32), shape((64, 128), F32)],
        in_specs=[vm] * 8 + [an] * 2 + [vm] * 6,
        out_specs=[vm] * 8,
        scratch_shapes=pieces
        + pieces
        + [pltpu.VMEM((2, 14, 2, 8, FEATURES), BF)] * 2
        + [pltpu.VMEM((k, ROWS), BF) for k, _n in WHOLES[2:]]
        + [pltpu.VMEM(s, BF) for s in WHOLES]
        + [
            pltpu.VMEM((4, 16, FEATURES), F32),
            pltpu.VMEM((4, 64, 128), F32),
            pltpu.VMEM((3, 16, FEATURES), F32),
            pltpu.VMEM((3, 64, 128), F32),
            pltpu.VMEM((4, 16, FEATURES), F32),
            pltpu.VMEM((4, 64, 128), F32),
        ]
        + lands
        + [dma((2, 4, 3)), dma((2, 2, 3)), dma((2, 2)), dma((chunks, 13)), dma((chunks, 13)), dma((12,)), dma((12,))],
        compiler_params=pltpu.CompilerParams(collective_id=1, has_side_effects=True, vmem_limit_bytes=67043328),
    )(n1, dqkv, o, da, n2, dh, g, dz, raw_r, raw_g, sums, up_sum, bias_sums, norm_sums, table_sums, jnp.asarray(table_taker()))


def dot_rows(a, b):
    return lax.dot_general(a, b, (((0,), (0,)), ((), ())), preferred_element_type=F32)


def on_device(
    image_in,
    cotangent,
    qkv_weight,
    out_weight,
    up_weight,
    down_weight,
    query_bias,
    value_bias,
    out_bias,
    up_bias,
    down_bias,
    first_gain,
    first_shift,
    second_gain,
    second_shift,
    rows_table,
    cols_table,
):
    line = lambda v: v.reshape(1, -1)
    bias_all = line(jnp.concatenate([query_bias, jnp.zeros_like(query_bias), value_bias]))
    tab = table_operand(rows_table, cols_table, False)
    tab_back = table_operand(rows_table, cols_table, True)
    xw, cw, n1_turned, qkv, probs, o, o_turned, wq, wo, wu, wd = open_windows(
        image_in, cotangent, (qkv_weight, out_weight, up_weight, down_weight), line(first_gain), line(first_shift), bias_all, tab
    )
    result, n2, g, dh, da, do, dm, sums, up_sum = middle(
        o, xw, cw, wo, wu, wd, line(out_bias), line(up_bias), line(down_bias), line(second_gain), line(second_shift)
    )
    dqkv, raw_r, raw_g, bias_sums, norm_sums, table_sums = back(
        do, probs, qkv, o, xw, dm, result, wq, tab_back, bias_all, line(first_gain)
    )
    if lax.axis_size("img") == 2:
        *large, small, table = finish(n1_turned, dqkv, o_turned, da, n2, dh, g, cw, raw_r, raw_g, sums, up_sum, bias_sums, norm_sums, table_sums)
        return (
            *large,
            small[0],
            small[1],
            small[2],
            small[8:12].reshape(-1),
            *(small[i] for i in range(3, 8)),
            table[:, :27].T,
            table[:, 64:91].T,
        )
    image_out, image_grad = give_back(raw_r, raw_g)
    totals = (jnp.dot(n1_turned, dqkv, preferred_element_type=F32), jnp.dot(o_turned, da, preferred_element_type=F32), dot_rows(n2, dh), dot_rows(g, cw))
    shard_sums = []
    for total in totals:
        part = lax.psum_scatter(total.astype(BF), ("row", "col"), scatter_dimension=0, tiled=True)
        shard_sums.append(lax.psum_scatter(part, "img", scatter_dimension=1, tiled=True).astype(F32))
    rows_grad, cols_grad = table_grads(table_sums)
    small_sums = lax.psum(
        tuple(jnp.sum(bias_sums, axis=1))
        + (jnp.sum(sums[0], axis=0), jnp.sum(up_sum, axis=0), jnp.sum(sums[1], axis=0))
        + tuple(jnp.sum(norm_sums, axis=1))
        + (jnp.sum(sums[2], axis=0), jnp.sum(sums[3], axis=0), rows_grad, cols_grad),
        ("img", "row", "col"),
    )
    return (image_out, image_grad, *shard_sums, *small_sums)


def solution(mesh):
    tiles = P("img", "row", "col", None)
    shards = P(("row", "col"), "img")
    return jax.shard_map(
        on_device,
        mesh=mesh,
        in_specs=(tiles,) * 2 + (shards,) * 4 + (P(),) * 11,
        out_specs=(tiles,) * 2 + (shards,) * 4 + (P(),) * 11,
        check_vma=False,
    )
```

time: 915 us -> 331 us (0.36)
  Pallas kernels: 0 us -> 300 us
  matrix products: 282 us -> 4.42 us
  local copies, waits for them, and re-layouts: 241 us -> 19.6 us
  waiting for transfers between devices: 165 us -> 0 us
  other arithmetic: 105 us -> 2.09 us
  blocking collectives: 69.6 us -> 0 us
  starting transfers between devices: 27.7 us -> 0 us
  between operations: 15.7 us -> 0.79 us
    pallas_call x0 -> x4, Pallas kernels: none -> 300 us  [the longest x1 114 us: finish(): pl.pallas_call(finish_kernel, out_shape=[shape((2, 16, 16, FEATURES), BF)...]
    dot_general x30 -> x8, matrix products: 282 us -> 4.42 us  [table_operand(): lax.dot_general(table, take[parity, which], (((0,), (0,)), ((), ())), pre...]
    reshape x15 -> x8, local copies, waits for them, and re-layouts: 141 us -> 8.82 us  [the longest x7 8.21 us: on_device(): line = lambda v: v.reshape(1, -1)]
    reduce_scatter x5 -> x0, waiting for transfers between devices: 88.6 us -> none  [the longest x1 66.9 us: on_device(): lax.psum_scatter(total_up.astype(jnp.bfloat16), ('row', 'col'), scatter_d...]
    ppermute x8 -> x0, waiting for transfers between devices: 75.9 us -> none  [from_behind(): return lax.ppermute(block, axis, route)]
    psum x1 -> x0, blocking collectives: 41.7 us -> none  [on_device(): lax.psum((total_bias_all[:features], total_bias_all[2 * features:], total...]
    convert_element_type x9 -> x0, other arithmetic: 31.9 us -> none  [the longest x1 14.6 us: on_device(): (attention * (grad_attention - inner_sum)).astype(jnp.bfloat16)]
    all_gather x4 -> x0, blocking collectives: 27.9 us -> none  [the longest x1 8.64 us: gather_weights(): lax.all_gather(qkv_weight, 'img', axis=1, tiled=True)]
  transfers between devices with their start and end apart: 20 -> 0, of which waited for: 7 -> 0; matrix products, arithmetic and copies ran while one was open for 65% -> 0% of each run, Pallas kernels for 0% -> 0%
where the time goes in v1:
time: 331 us; the launch traced here: 327 us
  Pallas kernels  300 us (91%)
  local copies, waits for them, and re-layouts  19.6 us (6%)
  matrix products  4.42 us (1%)
    pallas_call x1, Pallas kernels, finish(): pl.pallas_call(finish_kernel, out_shape=[shape((2, 16, 16, FEATURES), BF)...  114 us
    pallas_call x1, Pallas kernels, open_windows(): pl.pallas_call(functools.partial(open_kernel, weights), out_shape=[shape(...  113 us
    pallas_call x1, Pallas kernels, middle(): pl.pallas_call(middle_kernel, grid=(ROWS // BLOCK,), out_shape=[shape((RO...  38.4 us
    pallas_call x1, Pallas kernels, back(): pl.pallas_call(back_kernel, out_shape=[shape((ROWS, 3 * FEATURES), BF), s...  34.4 us
    reshape x7, local copies, waits for them, and re-layouts, on_device(): line = lambda v: v.reshape(1, -1)  8.21 us
    unnamed x30, local copies, waits for them, and re-layouts  7.38 us

profile of v1, /device:TPU:0, one launch (start us, length us, event | category | flops | bytes accessed | tf_op | source)
XLA Modules:
  0.0 326.8 jit_solution(2244656227373301381)
XLA Ops:
  0.7 0.9 fusion
  1.6 0.9 fusion.1
  2.5 0.9 fusion.2
  3.4 0.9 fusion.3
  5.0 0.7 pad_maximum_fusion.2
  6.3 1.3 reshape.70.gain
  7.6 1.3 reshape.71.shift
  8.9 113.0 %shard_map.323 = (bf16[704,768]{1,0:T(8,128)(2,1)}, bf16[704,768]{1,0:T(8,128)(2,1)}, bf16[768,704]{1,0:T(8,128)(2,1)}, bf16[800,2304]{1,0:T(8,128)(2,1)}, bf16[...) custom-call(bf16[2,16,2,8,768]{4,3,2,1,0:T(8,128)(2,1)} %bitcast.39,, ...), custom_call_target="tpu_custom_call" | custom-call | tf_op jit(solution)/shard_map/pallas_call | solution.py:514
  121.8 1.3 reshape.73.out_bias
  123.1 1.3 reshape.75.down_bias
  124.4 1.3 reshape.76.gain
  125.7 1.3 reshape.77.shift
  127.0 38.4 %shard_map.324 = (bf16[704,768]{1,0:T(8,128)(2,1)}, bf16[704,768]{1,0:T(8,128)(2,1)}, bf16[704,3072]{1,0:T(8,128)(2,1)}, bf16[704,3072]{1,0:T(8,128)(2,1)}, bf16...) custom-call(bf16[800,768]{1,0:T(8,128)(2,1)} %get-tuple-element.52.o, ...), custom_call_target="tpu_custom_call" | custom-call | tf_op jit(solution)/shard_map/pallas_call | solution.py:609
  166.8 34.4 %shard_map.325 = (bf16[704,2304]{1,0:T(8,128)(2,1)}, bf16[4,22,3,8,768]{4,3,2,1,0:T(8,128)(2,1)}, bf16[4,22,3,8,768]{4,3,2,1,0:T(8,128)(2,1)}, f32[2,8,768]{2,1,...) custom-call(bf16[704,768]{1,0:T(8,128)(2,1)} %get-tuple-element.58.do, ...), custom_call_target="tpu_custom_call" | custom-call | tf_op jit(solution)/shard_map/pallas_call | solution.py:740
  201.2 114.2 %shard_map.326 = (bf16[2,16,16,768]{3,2,1,0:T(8,128)(2,1)}, f32[2,16,16,768]{3,2,1,0:T(8,128)}, f32[48,1152]{1,0:T(8,128)}, f32[48,384]{1,0:T(8,128)}, f32[48,15...) custom-call(bf16[768,704]{1,0:T(8,128)(2,1)} %get-tuple-element.51.turned_n1, ...), custom_call_target="tpu_custom_call" | custom-call | tf_op jit(solution)/shard_map/pallas_call | solution.py:1168
  315.4 1.0 slice_bitcast_fusion
  316.4 0.7 copy.37
  317.8 1.7 slice_reduce_fusion
  319.5 0.7 slice.68
  320.8 2.1 copy.45
  322.9 1.1 copy.46
  324.1 0.7 copy.47
  325.4 0.7 copy.49
  326.1 0.7 copy.50
  (35 shorter events, 4.7 us)
Async XLA Ops:
  126.9 38.4 %copy-start.5 = (bf16[27,64]{1,0:T(8,128)(2,1)S(1)}, bf16[27,64]{1,0:T(8,128)(2,1)}, u32[]{:S(2)}) copy-start(bf16[27,64]{1,0:T(8,128)(2,1)} %param.35) | copy-start | bytes 10372
  126.9 38.4 %copy-start.10 = (bf16[27,128]{1,0:T(8,128)(2,1)S(1)}, bf16[27,128]{1,0:T(8,128)(2,1)}, u32[]{:S(2)}) copy-start(bf16[27,128]{1,0:T(8,128)(2,1)} %constant.30) | copy-start | bytes 20740
  126.9 38.6 %copy-start.6 = (bf16[27,64]{1,0:T(8,128)(2,1)S(1)}, bf16[27,64]{1,0:T(8,128)(2,1)}, u32[]{:S(2)}) copy-start(bf16[27,64]{1,0:T(8,128)(2,1)} %param.36) | copy-start | bytes 10372
  126.9 38.6 %copy-start.9 = (bf16[27,128]{1,0:T(8,128)(2,1)S(1)}, bf16[27,128]{1,0:T(8,128)(2,1)}, u32[]{:S(2)}) copy-start(bf16[27,128]{1,0:T(8,128)(2,1)} %constant.32) | copy-start | bytes 20740
  126.9 38.8 %copy-start.8 = (bf16[27,128]{1,0:T(8,128)(2,1)S(1)}, bf16[27,128]{1,0:T(8,128)(2,1)}, u32[]{:S(2)}) copy-start(bf16[27,128]{1,0:T(8,128)(2,1)} %constant.34) | copy-start | bytes 20740
  126.9 39.0 %copy-start.7 = (bf16[27,128]{1,0:T(8,128)(2,1)S(1)}, bf16[27,128]{1,0:T(8,128)(2,1)}, u32[]{:S(2)}) copy-start(bf16[27,128]{1,0:T(8,128)(2,1)} %constant.36) | copy-start | bytes 20740
  315.4 7.5 %copy-start = (f32[2,16,16,768]{3,2,1,0:T(8,128)S(1)}, f32[2,16,16,768]{3,2,1,0:T(8,128)}, u32[]{:S(2)}) copy-start(f32[2,16,16,768]{3,2,1,0:T(8,128)} %get-tuple-element.134) | copy-start | bytes 4718596
  322.9 1.2 copy-start.3
  322.9 1.9 copy-start.4
  322.9 2.5 copy-start.2
  322.9 3.2 copy-start.1

commit v2 on v1

v2 whole, which is shorter than its diff:
```python
import functools

import jax
import jax.numpy as jnp
import numpy as np
from jax import lax
from jax.experimental import pallas as pl
from jax.experimental.pallas import tpu as pltpu
from jax.sharding import PartitionSpec as P

MESH = pl.DeviceIdType.MESH


def place():
    return lax.axis_index("img"), lax.axis_index("row"), lax.axis_index("col")


def side_owner(window_row, image):
    return lax.rem(window_row, 2), 3 - image - 2 * (window_row // 2)


def piece_target(kind, image, row, col):
    last_row, last_col = row == 3, col == 3
    side_row, side_col = side_owner(row, image)
    next_row, next_col = side_owner(lax.rem(row + 1, 4), image)
    if kind == 0:
        return (jnp.where(last_row, 3 - image, row + 1), col, jnp.where(last_row, 2, image))
    if kind == 1:
        return (jnp.where(last_col, side_row, row), jnp.where(last_col, side_col, col + 1), jnp.where(last_col, 2, image))
    target_row = jnp.where(last_row, 3 - image, jnp.where(last_col, next_row, row + 1))
    target_col = jnp.where(last_col, jnp.where(last_row, 3, next_col), col + 1)
    slot = jnp.where(last_row & last_col, 3, jnp.where(last_row | last_col, 2, image))
    return (target_row, target_col, slot)


def arrivals(row, col):
    wide = row >= 2
    side_row = row + 2 * (1 - col // 2)
    table = []
    for image in range(2):
        table.append((image, 0, row > 0))
        table.append((image, 1, col > 0))
        table.append((image, 2, (row > 0) & (col > 0)))
    table.append((2, 0, wide))
    table.append((2, 1, jnp.logical_not(wide)))
    table.append((2, 2, jnp.where(wide, col, side_row) > 0))
    table.append((3, 2, wide & (col == 3)))
    return table


def tile_part(ref, image, kind):
    if kind == 0:
        return ref.at[image, pl.ds(8, 8), pl.ds(0, 2)]
    if kind == 1:
        return ref.at[image, pl.ds(0, 14), pl.ds(1, 1)]
    return ref.at[image, pl.ds(8, 8), pl.ds(1, 1)]


def window_part(ref, slot, kind):
    if kind == 0:
        return ref.at[pl.ds(slot * 22, 8), pl.ds(1, 2)]
    if kind == 1:
        return ref.at[pl.ds(slot * 22 + 8, 14), pl.ds(0, 1)]
    return ref.at[pl.ds(slot * 22, 8), pl.ds(0, 1)]


def greet(img, row, col, pairs=True):
    barrier = pltpu.get_barrier_semaphore()
    for row_step in range(4):
        for col_step in range(4):
            if row_step or col_step:
                pl.semaphore_signal(
                    barrier,
                    inc=1,
                    device_id={"row": lax.rem(row + row_step, 4), "col": lax.rem(col + col_step, 4)},
                    device_id_type=MESH,
                )
    if pairs:
        pl.semaphore_signal(barrier, inc=1, device_id={"img": 1 - img}, device_id_type=MESH)
    pl.semaphore_wait(barrier, 16 if pairs else 15)


CHUNKS = ((0, 0, 640), (0, 640, 1152), (1, 0, 384), (2, 0, 768), (2, 768, 1536), (3, 0, 128), (3, 128, 384))


def links(shards, fulls, wsend, wrecv, wloc):
    img, row, col = place()
    y_row = lax.rem(row + 2, 4)
    core_row = row + 1 - 2 * lax.rem(row, 2)
    other = 1 - img
    sent = []

    def rows_of(w, rw, half=None):
        kb = fulls[w].shape[0] // 4
        if half is None:
            return pl.ds(pl.multiple_of(rw * kb, kb), kb)
        return pl.ds(pl.multiple_of(rw * kb + half * (kb // 2), kb // 2), kb // 2)

    def cols_of(n, im):
        w, lo, hi = CHUNKS[n]
        nb = fulls[w].shape[1] // 2
        return pl.ds(pl.multiple_of(im * nb + lo, 128), hi - lo)

    def block(n, rw, im, half=None):
        w = CHUNKS[n][0]
        return fulls[w].at[rows_of(w, rw, half), cols_of(n, im)]

    def slot(n, cl):
        w = CHUNKS[n][0]
        k16 = fulls[w].shape[0] // 16
        return fulls[w].at[pl.ds(pl.multiple_of((row * 4 + cl) * k16, k16), k16), cols_of(n, img)]

    def source(n):
        w, lo, hi = CHUNKS[n]
        return shards[w].at[:, pl.ds(lo, hi - lo)]

    def push(n, k, where, target, start=None):
        def copy():
            ref = block(n, *where)
            return pltpu.make_async_remote_copy(
                src_ref=source(n) if start else ref,
                dst_ref=slot(n, col) if start else ref,
                send_sem=wsend.at[n, k],
                recv_sem=wrecv.at[n, k],
                device_id=target(),
                device_id_type=MESH,
            )

        copy().start()
        sent.append(copy)

    def arrive(n, k, ref):
        pltpu.make_async_copy(ref, ref, wrecv.at[n, k]).wait()

    def along_col(n):
        pltpu.make_async_copy(source(n), slot(n, col), wloc.at[n]).start()
        for d in range(1, 4):
            push(n, d - 1, (row, img), lambda d=d: {"col": lax.rem(col + d, 4)}, True)

    def first(n):
        pltpu.make_async_copy(source(n), slot(n, col), wloc.at[n]).wait()
        for d in range(1, 4):
            arrive(n, d - 1, slot(n, lax.rem(col + 4 - d, 4)))
        push(n, 3, (row, img, 0), lambda: {"img": other})
        push(n, 4, (row, img, 1), lambda: {"row": y_row})
        push(n, 5, (row, img), lambda: {"row": core_row})

    def second(n):
        arrive(n, 3, block(n, row, other, 0))
        arrive(n, 4, block(n, y_row, img, 1))
        push(n, 6, (row, img, 0), lambda: {"row": y_row})
        push(n, 7, (row, other, 0), lambda: {"row": y_row})
        push(n, 8, (row, img, 1), lambda: {"img": other})
        push(n, 9, (y_row, img, 1), lambda: {"img": other})
        push(n, 10, (row, other, 0), lambda: {"row": core_row})
        push(n, 11, (y_row, img, 1), lambda: {"row": core_row})

    def third(n):
        arrive(n, 6, block(n, y_row, img, 0))
        arrive(n, 7, block(n, y_row, other, 0))
        arrive(n, 8, block(n, row, other, 1))
        arrive(n, 9, block(n, y_row, other, 1))
        push(n, 12, (y_row, img, 0), lambda: {"row": core_row})
        push(n, 13, (y_row, other, 0), lambda: {"row": core_row})
        push(n, 14, (row, other, 1), lambda: {"row": core_row})
        push(n, 15, (y_row, other, 1), lambda: {"row": core_row})

    def last(n):
        core_y = lax.rem(core_row + 2, 4)
        arrive(n, 5, block(n, core_row, img))
        arrive(n, 10, block(n, core_row, other, 0))
        arrive(n, 11, block(n, core_y, img, 1))
        arrive(n, 12, block(n, core_y, img, 0))
        arrive(n, 13, block(n, core_y, other, 0))
        arrive(n, 14, block(n, core_row, other, 1))
        arrive(n, 15, block(n, core_y, other, 1))

    return along_col, first, second, third, last, sent


def window_moves(tiles, raws, send, recv, loc):
    img, row, col = place()

    def each(t, act):
        for image in range(2):
            for kind in range(3):
                target_row, target_col, target_slot = piece_target(kind, image, row, col)
                here = (target_row == row) & (target_col == col)
                part = tile_part(tiles[t], image, kind)
                goal = window_part(raws[t], target_slot, kind)
                act(here, part, goal, send.at[t, image, kind], recv.at[t, target_slot, kind], target_row, target_col)

    def remote(part, goal, leave, arrival, target_row, target_col):
        return pltpu.make_async_remote_copy(
            src_ref=part,
            dst_ref=goal,
            send_sem=leave,
            recv_sem=arrival,
            device_id={"row": target_row, "col": target_col},
            device_id_type=MESH,
        )

    def own(t, image):
        return pltpu.make_async_copy(tiles[t].at[image, pl.ds(0, 14)], raws[t].at[pl.ds(image * 22 + 8, 14), pl.ds(1, 2)], loc.at[t, image])

    def start(t):
        for image in range(2):
            own(t, image).start()

        def act(here, part, goal, leave, arrival, target_row, target_col):
            @pl.when(here)
            def _():
                pltpu.make_async_copy(part, goal, arrival).start()

            @pl.when(jnp.logical_not(here))
            def _():
                remote(part, goal, leave, arrival, target_row, target_col).start()

        each(t, act)

    def arrived(t):
        for image in range(2):
            own(t, image).wait()
        for slot_index, kind, present in arrivals(row, col):
            part = window_part(raws[t], slot_index, kind)

            @pl.when(present)
            def _():
                pltpu.make_async_copy(part, part, recv.at[t, slot_index, kind]).wait()

    def left(t):
        def act(here, part, goal, leave, arrival, target_row, target_col):
            @pl.when(jnp.logical_not(here))
            def _():
                remote(part, goal, leave, arrival, target_row, target_col).wait_send()

        each(t, act)

    return start, arrived, left


BF = jnp.bfloat16
F32 = jnp.float32
ROWS = 704
SPAN = 800
FEATURES = 768
EPS = 1e-06


def row_params(step, row, col):
    wide = row >= 2
    side_row = row + 2 * (1 - col // 2)
    third_step = step - 28
    in_corner = wide & (third_step >= 8)
    slot = jnp.where(step < 14, 0, jnp.where(step < 28, 1, jnp.where(in_corner, 3, 2)))
    place_row = jnp.where(step < 14, step, jnp.where(step < 28, step - 14, jnp.where(in_corner, third_step - 8, third_step)))
    full = step < 28
    row_start = jnp.where(full, 8 - 2 * row, jnp.where(wide, 0, 8 - 2 * side_row))
    col_start = jnp.where(full, 8 - 2 * col, jnp.where(wide & jnp.logical_not(in_corner), 8 - 2 * col, 0))
    width = jnp.where(full, 14, jnp.where(wide & jnp.logical_not(in_corner), 14, 8))
    alive = jnp.where(full, True, jnp.where(in_corner, col == 3, jnp.where(wide, True, third_step < 14)))
    return slot, jnp.minimum(place_row + row_start, 21), col_start, jnp.where(alive, width, 0)


def window_params(window, row, col):
    wide = row >= 2
    start = jnp.where(window < 2, 14 * window, jnp.where(window == 2, 28, 36))
    tall = jnp.where(window < 2, 14, jnp.where((window == 2) & jnp.logical_not(wide), 14, 8))
    width = jnp.where(window < 2, 14, jnp.where((window == 2) & wide, 14, 8))
    return start, tall, width


def window_count(row, col):
    return jnp.where((row >= 2) & (col == 3), 4, 3)


def unit_of(values):
    center = values - jnp.mean(values, axis=-1, keepdims=True)
    inverse = lax.rsqrt(jnp.mean(center * center, axis=-1, keepdims=True) + EPS)
    return center * inverse, inverse


def relative_layout(backward):
    take = np.zeros((2, 2, 27, 128), np.float32)
    for parity in range(2):
        base = 64 if parity == 0 else 0
        for j in range(27):
            for copy in (0,) if backward else (0, 32):
                take[parity, 0, 26 - j, (base - 13 + j + copy) % 128] = 1
                if backward:
                    take[parity, 1, j, base + 16 + j] = 1
                else:
                    take[parity, 1, 26 - j, (base + 3 + j + copy) % 128] = 1
    return take


def table_operand(rows_table, cols_table, backward):
    take = jnp.asarray(relative_layout(backward), BF)
    parts = []
    for parity in range(2):
        both = []
        for which, table in ((0, rows_table), (1, cols_table)):
            both.append(lax.dot_general(table, take[parity, which], (((0,), (0,)), ((), ())), preferred_element_type=F32).astype(BF))
        block = jnp.concatenate(both, axis=1)
        zero = jnp.zeros_like(block)
        parts.append(jnp.concatenate([block, zero] if parity == 0 else [zero, block], axis=0))
    return jnp.concatenate(parts, axis=1)


def table_grads(sums):
    take = jnp.asarray(relative_layout(True), F32)
    grads = []
    for which in range(2):
        total = 0.0
        for parity in range(2):
            part = sums[64 * parity : 64 * parity + 64, 256 * parity + 128 * which : 256 * parity + 128 * which + 128]
            total = total + lax.dot_general(take[parity, which], part, (((1,), (1,)), ((), ())), precision=lax.Precision.HIGHEST)
        grads.append(total)
    return grads


def run_all(act):
    for i in range(0, len(act), 2):
        act[i](act[i + 1])


def open_kernel(weights, x_ref, c_ref, gain, shift, bias, tab, *refs):
    img, row, col = place()
    greet(img, row, col, weights)
    if weights:
        shards, refs = refs[:4], refs[4:]
    else:
        wq, refs = refs[0], refs[1:]
    xw, cw, n1_turned, qkv_s, probs, o, o_turned = refs[:7]
    refs = refs[7:]
    if weights:
        fulls, refs = refs[:4], refs[4:]
        wq = fulls[0]
    rawx, rawc, n1, send, recv, loc = refs[:6]
    if weights:
        along_col, first, second, third, last, sent = links(shards, fulls, *refs[6:])
    window_start, window_arrived, window_left = window_moves((x_ref, c_ref), (rawx, rawc), send, recv, loc)
    places = lax.broadcasted_iota(jnp.int32, (16, 1), 0)

    def cut_one(raw, step):
        slot, raw_row, col_start, width = row_params(step, row, col)
        wide_rows = raw[slot * 22 + raw_row].reshape(24, FEATURES).astype(F32)
        keep = places < width
        return keep, jnp.where(keep, pltpu.roll(wide_rows, lax.rem(24 - col_start, 24), 0)[:16], 0.0)

    def cut_x(step, _):
        at = pl.ds(pl.multiple_of(step * 16, 16), 16)
        keep, x = cut_one(rawx, step)
        xw[at, :] = x.astype(BF)
        unit, _inverse = unit_of(x)
        n1[at, :] = jnp.where(keep, unit * gain[...] + shift[...], 0.0).astype(BF)
        return 0

    def cut_c(step, _):
        at = pl.ds(pl.multiple_of(step * 16, 16), 16)
        _keep, c = cut_one(rawc, step)
        cw[at, :] = c.astype(BF)
        return 0

    def project(step, _):
        at = pl.ds(pl.multiple_of(step * 352, 32), 352)
        for part_index in range(3):
            lanes = slice(part_index * FEATURES, (part_index + 1) * FEATURES)
            part = jnp.dot(n1[at, :], wq[:, lanes], preferred_element_type=F32) + bias[:, lanes]
            qkv_s[at, lanes] = part.astype(BF)
        return 0

    def turn(source, goal):
        def step(i, _):
            lanes = pl.ds(pl.multiple_of(i * 128, 128), 128)
            goal[lanes, :] = source[0:ROWS, lanes].T
            return 0

        lax.fori_loop(0, FEATURES // 128, step, 0)

    if weights:
        along_col(0)
        along_col(1)
    else:
        window_start(0)
        window_start(1)
    o[...] = jnp.zeros_like(o)
    if weights:
        first(0)
        first(1)
        window_start(0)
        along_col(2)
        second(0)
        second(1)
        along_col(3)
    window_arrived(0)
    lax.fori_loop(0, 44, cut_x, 0)
    steps = []
    if weights:
        first(2)
        along_col(4)
        third(0)
        third(1)
        first(3)
        along_col(5)
        last(0)
        last(1)
        steps = [
            (second, 2),
            (first, 4, along_col, 6),
            (second, 3),
            (third, 2),
            (first, 5, window_start, 1),
            (second, 4),
            (third, 3),
            (first, 6),
            (second, 5),
            (third, 4),
            (second, 6),
            (third, 5),
            (third, 6),
        ]
    lax.fori_loop(0, 2, project, 0)
    row_of = lax.broadcasted_iota(jnp.int32, (224, 1), 0)
    lane = lax.broadcasted_iota(jnp.int32, (1, 128), 1)
    key_place = lax.broadcasted_iota(jnp.int32, (224, 128), 0)
    key_lane = lax.broadcasted_iota(jnp.int32, (224, 128), 1)
    key_a, key_b = key_place // 16, key_place % 16

    def pair(index, _):
        for turn_index, act in enumerate(steps):
            pl.when(index == turn_index)(functools.partial(run_all, act))
        window, pair_index = index // 6, index % 6
        start, tall, width = window_params(window, row, col)
        at = pl.ds(pl.multiple_of(start * 16, 16), 224)
        alive = (row_of // 16 < tall) & (row_of % 16 < width)
        lanes = lambda third: pl.ds(pl.multiple_of(third * FEATURES + pair_index * 128, 128), 128)
        q = jnp.where(alive, qkv_s[at, lanes(0)].astype(F32), 0.0)
        k = jnp.where(alive, qkv_s[at, lanes(1)].astype(F32), 0.0)
        v = jnp.where(alive, qkv_s[at, lanes(2)].astype(F32), bias[:, lanes(2)].astype(BF).astype(F32)).astype(BF)
        terms = jnp.dot(q.astype(BF), tab[...], preferred_element_type=F32)
        outs = []
        for parity in range(2):
            base = 64 if parity == 0 else 0
            own = (lane < 64) if parity == 0 else (lane >= 64)
            rel_rows = jnp.concatenate(
                [pltpu.roll(terms[16 * a : 16 * a + 16, 256 * parity : 256 * parity + 128], a, 1) for a in range(14)], axis=0
            )
            rel_cols = jnp.concatenate(
                [
                    pltpu.roll(terms[16 * a : 16 * a + 16, 256 * parity + 128 : 256 * parity + 256], 0, 1, stride=1, stride_axis=0)
                    for a in range(14)
                ],
                axis=0,
            )
            on = lane - base
            in_rows = ((on >= 0) & (on < 14)) | ((on >= 32) & (on < 46))
            in_cols = ((on >= 16) & (on < 30)) | ((on >= 48) & (on < 62))
            rel = jnp.where(in_rows, rel_rows, jnp.where(in_cols, rel_cols, 0.0))
            rough = rel.astype(BF).astype(F32)
            fine = jnp.where(on >= 32, rel - rough, rough)
            fine = jnp.where(on == 14, -1e30, fine)
            q_side = jnp.where(own, q * 0.125, fine).astype(BF)
            key_on = key_lane - base
            hot = jnp.where(
                key_on == 14,
                jnp.where(key_b >= 14, 1.0, 0.0),
                jnp.where(
                    (key_on % 32 < 14) & (key_a == key_on % 32),
                    1.0,
                    jnp.where((key_on % 32 >= 16) & (key_on % 32 < 30) & (key_b == key_on % 32 - 16), 1.0, 0.0),
                ),
            )
            k_side = jnp.where(own, k, hot).astype(BF)
            scores = lax.dot_general(q_side, k_side, (((1,), (1,)), ((), ())), preferred_element_type=F32)
            exponent = jnp.exp(scores - jnp.max(scores, axis=-1, keepdims=True))
            p = (exponent * (1.0 / jnp.sum(exponent, axis=-1, keepdims=True))).astype(BF)
            probs[window, 2 * pair_index + parity] = p
            outs.append(jnp.dot(p, v, preferred_element_type=F32))
        blended = jnp.where(lane < 64, outs[0], outs[1])
        out_lanes = pl.ds(pl.multiple_of(pair_index * 128, 128), 128)
        o_at = pl.ds(pl.multiple_of(start * 16, 16), 224)
        o[o_at, out_lanes] = jnp.where(alive, blended, 0.0).astype(BF)
        return 0

    lax.fori_loop(0, window_count(row, col) * 6, pair, 0)
    turn(n1, n1_turned)
    turn(o, o_turned)
    window_arrived(1)
    lax.fori_loop(0, 44, cut_c, 0)
    if weights:
        for n in range(2, len(CHUNKS)):
            last(n)
        for copy in sent:
            copy().wait_send()
    window_left(0)
    window_left(1)


def open_windows(x, c, shards, gain, shift, bias, tab):
    vm = pl.BlockSpec(memory_space=pltpu.VMEM)
    an = pl.BlockSpec(memory_space=pl.ANY)
    shape = jax.ShapeDtypeStruct
    dma = pltpu.SemaphoreType.DMA
    chunks = len(CHUNKS)
    weights = lax.axis_size("img") == 2
    if weights:
        given, wholes = list(shards), [(768, 2304), (768, 768), (768, 3072), (3072, 768)]
    else:
        widened = [lax.all_gather(w, "img", axis=1, tiled=True) for w in shards]
        gathered = [lax.all_gather(w, ("row", "col"), axis=0, tiled=True) for w in widened]
        given, wholes = gathered[:1], []
    raw = pltpu.VMEM((88, 3, 8, FEATURES), BF)
    outs = pl.pallas_call(
        functools.partial(open_kernel, weights),
        out_shape=[
            shape((ROWS, FEATURES), BF),
            shape((ROWS, FEATURES), BF),
            shape((FEATURES, ROWS), BF),
            shape((SPAN, 3 * FEATURES), BF),
            shape((4, 12, 224, 224), BF),
            shape((SPAN, FEATURES), BF),
            shape((FEATURES, ROWS), BF),
        ]
        + [shape(s, BF) for s in wholes],
        in_specs=[vm] * (6 + len(given)),
        out_specs=[vm] * 7 + ([vm, an, an, an] if weights else []),
        scratch_shapes=[raw, raw, pltpu.VMEM((ROWS, FEATURES), BF), dma((2, 2, 3)), dma((2, 4, 3)), dma((2, 2))]
        + ([dma((chunks, 16)), dma((chunks, 16)), dma((chunks,))] if weights else []),
        compiler_params=pltpu.CompilerParams(collective_id=0, has_side_effects=True, vmem_limit_bytes=67043328),
    )(x.reshape(2, 16, 2, 8, 768), c.reshape(2, 16, 2, 8, 768), gain, shift, bias, tab, *given)
    return list(outs) if weights else list(outs) + gathered


FF = 3072
CHUNK = 512
BLOCK = 176


def nt(a, b):
    return lax.dot_general(a, b, (((1,), (1,)), ((), ())), preferred_element_type=F32)


def norm_back(grad, unit, inverse, gain):
    scaled = grad * gain
    first_mean = jnp.mean(scaled, axis=-1, keepdims=True)
    second_mean = jnp.mean(scaled * unit, axis=-1, keepdims=True)
    return inverse * (scaled - first_mean - unit * second_mean)


def fold_rows(values):
    total = values[0:8]
    for i in range(1, values.shape[0] // 8):
        total = total + values[8 * i : 8 * i + 8]
    return total


def spread_rows(source, raw, row, col):
    def step(i, _):
        slot, raw_row, col_start, width = row_params(i, row, col)
        at = pl.ds(pl.multiple_of(i * 16, 16), 16)

        @pl.when(width > 0)
        def _():
            values = jnp.concatenate([source[at, :], jnp.zeros((8, FEATURES), F32)], axis=0)
            raw[slot * 22 + raw_row] = pltpu.roll(values, col_start, 0).astype(BF).reshape(3, 8, FEATURES)

        return 0

    lax.fori_loop(0, 44, step, 0)


def middle_kernel(
    o, xw, cw, wo, wu, wd, out_bias, up_bias, down_bias, gain, shift, raw_r, n2_turned, g_turned, dh, da, do, dm, sums, up_sum, n2, y_s, d_s, g_s
):
    step = pl.program_id(0)
    row, col = lax.axis_index("row"), lax.axis_index("col")
    blocks = [slice(i * BLOCK, (i + 1) * BLOCK) for i in range(ROWS // BLOCK)]

    def mid_of(at):
        return xw[at, :].astype(F32) + (jnp.dot(o[at, :], wo[...], preferred_element_type=F32) + out_bias[...])

    @pl.when(step == 0)
    def _():
        sums[...] = jnp.zeros_like(sums)
        d_s[...] = jnp.zeros_like(d_s)

        def begin(i, _):
            at = pl.ds(pl.multiple_of(i * BLOCK, 16), BLOCK)
            mid = mid_of(at)
            unit, _inverse = unit_of(mid)
            n2[at, :] = (unit * gain[...] + shift[...]).astype(BF)
            y_s[at, :] = mid + down_bias[...]
            dm[at, :] = mid
            return 0

        lax.fori_loop(0, ROWS // BLOCK, begin, 0)

        def turn(i, _):
            lanes = pl.ds(pl.multiple_of(i * 128, 128), 128)
            n2_turned[lanes, :] = n2[:, lanes].T
            return 0

        lax.fori_loop(0, FEATURES // 128, turn, 0)

    up_sum[...] = jnp.zeros_like(up_sum)
    for at in blocks:
        h = jnp.dot(n2[at, :], wu[...], preferred_element_type=F32) + up_bias[...]
        up = nt(cw[at, :], wd[...])
        phi = 0.5 * (1.0 + lax.erf(h * 0.7071067811865476))
        slope = phi + h * (jnp.exp(-0.5 * h * h) * 0.3989422804014327)
        active = (h * phi).astype(BF)
        back = (up * slope).astype(BF)
        g_s[at, :] = active
        dh[at, :] = back
        up_sum[...] += fold_rows(back.astype(F32))
        y_s[at, :] += jnp.dot(active, wd[...], preferred_element_type=F32)
        d_s[at, :] += nt(back, wu[...])
    for i in range(CHUNK // 128):
        g_turned[128 * i : 128 * i + 128, 0:ROWS] = g_s[:, 128 * i : 128 * i + 128].T

    @pl.when(step == FF // CHUNK - 1)
    def _():
        def end(i, _):
            at = pl.ds(pl.multiple_of(i * BLOCK, 16), BLOCK)
            unit, inverse = unit_of(dm[at, :])
            grad = d_s[at, :].astype(BF).astype(F32)
            up = cw[at, :].astype(F32)
            grad_mid = up + norm_back(grad, unit, inverse, gain[...])
            low_grad = grad_mid.astype(BF)
            dm[at, :] = grad_mid
            da[at, :] = low_grad
            do[at, :] = nt(low_grad, wo[...]).astype(BF)
            sums[0] += fold_rows(low_grad.astype(F32))
            sums[1] += fold_rows(up)
            sums[2] += fold_rows(grad * unit)
            sums[3] += fold_rows(grad)
            return 0

        lax.fori_loop(0, ROWS // BLOCK, end, 0)
        spread_rows(y_s, raw_r, row, col)


def middle(o, xw, cw, wo, wu, wd, out_bias, up_bias, down_bias, gain, shift):
    shape = jax.ShapeDtypeStruct
    once = lambda *s: pl.BlockSpec(s, lambda i: (0,) * len(s), pipeline_mode=pl.Buffered(1))
    return pl.pallas_call(
        middle_kernel,
        grid=(FF // CHUNK,),
        out_shape=[
            shape((88, 3, 8, FEATURES), BF),
            shape((FEATURES, ROWS), BF),
            shape((FF, FEATURES), BF),
            shape((ROWS, FF), BF),
            shape((ROWS, FEATURES), BF),
            shape((SPAN, FEATURES), BF),
            shape((ROWS, FEATURES), F32),
            shape((4, 8, FEATURES), F32),
            shape((8, FF), F32),
        ],
        in_specs=[
            once(SPAN, FEATURES),
            once(ROWS, FEATURES),
            once(ROWS, FEATURES),
            once(FEATURES, FEATURES),
            pl.BlockSpec((FEATURES, CHUNK), lambda i: (0, i)),
            pl.BlockSpec((CHUNK, FEATURES), lambda i: (i, 0)),
            once(1, FEATURES),
            pl.BlockSpec((1, CHUNK), lambda i: (0, i)),
            once(1, FEATURES),
            once(1, FEATURES),
            once(1, FEATURES),
        ],
        out_specs=[
            once(88, 3, 8, FEATURES),
            once(FEATURES, ROWS),
            pl.BlockSpec((CHUNK, FEATURES), lambda i: (i, 0)),
            pl.BlockSpec((ROWS, CHUNK), lambda i: (0, i)),
            once(ROWS, FEATURES),
            once(SPAN, FEATURES),
            once(ROWS, FEATURES),
            once(4, 8, FEATURES),
            pl.BlockSpec((8, CHUNK), lambda i: (0, i)),
        ],
        scratch_shapes=[
            pltpu.VMEM((ROWS, FEATURES), BF),
            pltpu.VMEM((ROWS, FEATURES), F32),
            pltpu.VMEM((ROWS, FEATURES), F32),
            pltpu.VMEM((ROWS, CHUNK), BF),
        ],
        compiler_params=pltpu.CompilerParams(vmem_limit_bytes=62 << 20),
    )(o, xw, cw, wo, wu, wd, out_bias, up_bias, down_bias, gain, shift)


def attention_back(window, pair_index, probs_of, do, qkv, o, tab, bias, bias_sums, table_sums, row, col):
    row_of = lax.broadcasted_iota(jnp.int32, (224, 1), 0)
    lane = lax.broadcasted_iota(jnp.int32, (1, 128), 1)
    key_place = lax.broadcasted_iota(jnp.int32, (224, 128), 0)
    key_lane = lax.broadcasted_iota(jnp.int32, (224, 128), 1)
    key_a, key_b = key_place // 16, key_place % 16
    start, tall, width = window_params(window, row, col)
    at = pl.ds(pl.multiple_of(start * 16, 16), 224)
    inside = row_of // 16 < tall
    alive = inside & (row_of % 16 < width)
    lanes = lambda third: pl.ds(pl.multiple_of(third * FEATURES + pair_index * 128, 128), 128)
    old = [qkv[at, lanes(third)].astype(F32) for third in range(3)]
    q = jnp.where(alive, old[0], 0.0)
    k = jnp.where(alive, old[1], 0.0)
    v = jnp.where(alive, old[2], bias[:, lanes(2)].astype(BF).astype(F32))
    grad = jnp.where(alive, do[at, lanes(0)].astype(F32), 0.0)
    product = grad * jnp.where(alive, o[at, lanes(0)].astype(F32), 0.0)
    q_turned = q.T.astype(BF)
    grad_turned = grad.T.astype(BF)
    value_parts, key_parts, query_parts, table_parts = [], [], [], []
    for parity in range(2):
        base = 64 if parity == 0 else 0
        own = (lane < 64) if parity == 0 else (lane >= 64)
        half = slice(64 * parity, 64 * parity + 64)
        inner = jnp.sum(jnp.where(own, product, 0.0), axis=-1, keepdims=True)
        rough = inner.astype(BF).astype(F32)
        on = lane - base
        grad_side = jnp.where(own, grad, jnp.where(on == 0, rough, jnp.where(on == 1, inner - rough, 0.0))).astype(BF)
        v_side = jnp.where(own, v, jnp.where((on == 0) | (on == 1), -1.0, 0.0)).astype(BF)
        centered = nt(grad_side, v_side)
        p = probs_of(parity)
        ds = (p.astype(F32) * centered).astype(BF)
        value_parts.append(jnp.dot(grad_turned[half], p, preferred_element_type=F32))
        key_parts.append(jnp.dot(q_turned[half], ds, preferred_element_type=F32))
        key_on = key_lane - base
        hot = jnp.where(
            (key_on >= 0) & (key_on < 14) & (key_a == key_on),
            1.0,
            jnp.where((key_on >= 16) & (key_on < 30) & (key_b == 29 - key_on), 1.0, 0.0),
        )
        k_side = jnp.where(own, k * 0.125, hot).astype(BF)
        wide = jnp.dot(ds, k_side, preferred_element_type=F32)
        query_parts.append(wide)
        by_rows = jnp.where((on >= 0) & (on < 14), wide, 0.0)
        by_cols = jnp.where((on >= 16) & (on < 30), wide, 0.0)
        table_parts.append(jnp.concatenate([pltpu.roll(by_rows[16 * a : 16 * a + 16], (128 - a) % 128, 1) for a in range(14)], axis=0))
        table_parts.append(
            jnp.concatenate([pltpu.roll(by_cols[16 * a : 16 * a + 16], 0, 1, stride=1, stride_axis=0) for a in range(14)], axis=0)
        )
    turned = jnp.concatenate(table_parts, axis=1).astype(BF)
    dq = jnp.where(lane < 64, query_parts[0], query_parts[1]) + nt(turned, tab[...])
    table_sums[...] += jnp.dot(q_turned, turned, preferred_element_type=F32)
    dk = jnp.concatenate(key_parts, axis=0).T * 0.125
    dv = jnp.concatenate(value_parts, axis=0).T.astype(BF).astype(F32)
    dq = jnp.where(alive, dq, 0.0).astype(BF).astype(F32)
    bias_sums[0, :, lanes(0)] += fold_rows(dq)
    bias_sums[1, :, lanes(0)] += fold_rows(dv)
    for third, new in enumerate((dq, dk, dv)):
        qkv[at, lanes(third)] = jnp.where(alive, new, jnp.where(inside, 0.0, old[third])).astype(BF)


def clear_idle(qkv, row, col):
    wide = row >= 2
    limit = jnp.where(wide, jnp.where(col == 3, 44, 36), 42)
    for a in range(36, 44):

        @pl.when(a >= limit)
        def _():
            qkv[16 * a : 16 * a + 16, :] = jnp.zeros((16, 3 * FEATURES), BF)


def plain_back_kernel(do, probs, qkv, o, tab, bias, dqkv, bias_sums, table_sums):
    row, col = lax.axis_index("row"), lax.axis_index("col")
    dqkv[...] = qkv[...]
    clear_idle(dqkv, row, col)
    bias_sums[...] = jnp.zeros_like(bias_sums)
    table_sums[...] = jnp.zeros_like(table_sums)

    def pair(index, _):
        window, pair_index = index // 6, index % 6
        attention_back(
            window,
            pair_index,
            lambda parity: probs[window, 2 * pair_index + parity],
            do,
            dqkv,
            o,
            tab,
            bias,
            bias_sums,
            table_sums,
            row,
            col,
        )
        return 0

    lax.fori_loop(0, window_count(row, col) * 6, pair, 0)


def plain_back(do, probs, qkv, o, tab, bias):
    vm = pl.BlockSpec(memory_space=pltpu.VMEM)
    shape = jax.ShapeDtypeStruct
    return pl.pallas_call(
        plain_back_kernel,
        out_shape=[shape((SPAN, 3 * FEATURES), BF), shape((2, 8, FEATURES), F32), shape((128, 512), F32)],
        in_specs=[vm] * 6,
        out_specs=[vm] * 3,
        compiler_params=pltpu.CompilerParams(vmem_limit_bytes=62 << 20),
    )(do, probs, qkv, o, tab, bias)


WHOLES = ((768, 2304), (768, 768), (768, 3072), (3072, 768))
SUM_CHUNKS = ((1, 0, 384), (3, 0, 128), (3, 128, 384), (2, 0, 768), (2, 768, 1536), (0, 0, 384), (0, 384, 768), (0, 768, 1152))


def pair_lanes(j, im):
    if im == 0:
        return (128 * j, FEATURES + 128 * j, 128 * (j + 3))
    return (2 * FEATURES + 128 * j, FEATURES + 128 * (j + 3), 2 * FEATURES + 128 * (j + 3))


def land_shapes(chunks):
    lands = []
    for w, lo, hi in chunks:
        kb, width = WHOLES[w][0] // 4, hi - lo
        lands += [
            pltpu.VMEM((2, 2, kb, width), BF),
            pltpu.VMEM((2, kb // 2, width), BF),
            pltpu.VMEM((2, kb // 2, width), BF),
            pltpu.VMEM((2, kb // 2, width), BF),
            pltpu.VMEM((3, kb // 4, width), BF),
        ]
    return lands


def reducers(chunks, full, left_turned, right_side, grads, land_refs, wsend, wrecv):
    img, row, col = place()
    y_row = lax.rem(row + 2, 4)
    core_row = row + 1 - 2 * lax.rem(row, 2)
    core_y = lax.rem(core_row + 2, 4)
    other = 1 - img
    lands = [land_refs[5 * n : 5 * n + 5] for n in range(len(chunks))]
    sent = []

    def size(n):
        w, lo, hi = chunks[n]
        return WHOLES[w][0] // 4, WHOLES[w][1] // 2, lo, hi - lo

    def block(n, rw, im, half=None):
        kb, nb, lo, width = size(n)
        cols = pl.ds(pl.multiple_of(im * nb + lo, 128), width)
        if half is None:
            return full[chunks[n][0]].at[pl.ds(pl.multiple_of(rw * kb, kb), kb), cols]
        return full[chunks[n][0]].at[pl.ds(pl.multiple_of(rw * kb + half * (kb // 2), kb // 2), kb // 2), cols]

    def shard(n, cl):
        kb, nb, lo, width = size(n)
        cols = pl.ds(pl.multiple_of(img * nb + lo, 128), width)
        return full[chunks[n][0]].at[pl.ds(pl.multiple_of(row * kb + cl * (kb // 4), kb // 4), kb // 4), cols]

    def push(n, k, src, dst, target):
        def copy():
            return pltpu.make_async_remote_copy(
                src_ref=src(), dst_ref=dst(), send_sem=wsend.at[n, k], recv_sem=wrecv.at[n, k], device_id=target(), device_id_type=MESH
            )

        copy().start()
        sent.append(copy)

    def arrive(n, k, ref):
        pltpu.make_async_copy(ref, ref, wrecv.at[n, k]).wait()

    def add(goal, part, rows):
        def step(i, _):
            at = pl.ds(pl.multiple_of(i * 48, 16), 48)
            goal[at, :] = (goal[at, :].astype(F32) + part[at, :].astype(F32)).astype(BF)
            return 0

        lax.fori_loop(0, rows // 48, step, 0)

    def product(n, rw):
        w = chunks[n][0]
        kb, nb, lo, width = size(n)
        rows = pl.ds(pl.multiple_of(rw * kb, kb), kb)
        for im in range(2):
            at = slice(im * nb + lo, im * nb + lo + width)
            if w == 0:
                right = jnp.concatenate([right_side[0][0:ROWS, p : p + 128] for p in pair_lanes(lo // 384, im)], axis=1)
            else:
                right = right_side[w][0:ROWS, at]
            full[w][rows, at] = jnp.dot(left_turned[w](rw, kb), right, preferred_element_type=F32).astype(BF)

    def pair_stage(n):
        land = lands[n][0]
        for j, rw in enumerate((core_row, core_y)):
            product(n, rw)
            for im in range(2):
                push(n, 2 * j + im, functools.partial(block, n, rw, im), lambda j=j, im=im: land.at[j, im], lambda: {"row": core_row})
        for rw in (row, y_row):
            product(n, rw)

    def first(n):
        kb, nb, lo, width = size(n)
        for j, rw in enumerate((row, y_row)):
            for im in range(2):
                arrive(n, 2 * j + im, lands[n][0].at[j, im])
                add(block(n, rw, im), lands[n][0].at[j, im], kb)
        for im in range(2):
            push(n, 4 + im, functools.partial(block, n, y_row, im, 0), lambda im=im: lands[n][1].at[im], lambda: {"row": y_row})
        push(n, 6, functools.partial(block, n, row, other, 1), lambda: lands[n][2].at[0], lambda: {"img": other})
        push(n, 7, functools.partial(block, n, y_row, other, 1), lambda: lands[n][2].at[1], lambda: {"img": other})

    def second(n):
        kb, nb, lo, width = size(n)
        for im in range(2):
            arrive(n, 4 + im, lands[n][1].at[im])
            add(block(n, row, im, 0), lands[n][1].at[im], kb // 2)
        push(n, 8, functools.partial(block, n, row, other, 0), lambda: lands[n][3].at[0], lambda: {"img": other})
        for j, rw in enumerate((row, y_row)):
            arrive(n, 6 + j, lands[n][2].at[j])
            add(block(n, rw, img, 1), lands[n][2].at[j], kb // 2)
        push(n, 9, functools.partial(block, n, y_row, img, 1), lambda: lands[n][3].at[1], lambda: {"row": y_row})

    def third(n):
        kb, nb, lo, width = size(n)
        for half in range(2):
            arrive(n, 8 + half, lands[n][3].at[half])
            add(block(n, row, img, half), lands[n][3].at[half], kb // 2)
        for d in range(1, 4):

            def src(d=d):
                return shard(n, lax.rem(col + d, 4))

            push(n, 9 + d, src, lambda d=d: lands[n][4].at[d - 1], lambda d=d: {"col": lax.rem(col + d, 4)})

    def fourth(n):
        w, lo, hi = chunks[n]
        for d in range(1, 4):
            arrive(n, 9 + d, lands[n][4].at[d - 1])
        mine = shard(n, col)

        def step(part, _):
            at = pl.ds(pl.multiple_of(part * 48, 16), 48)
            total = mine[at, :].astype(F32)
            for d in range(3):
                total = total + lands[n][4][d, at, :].astype(F32)
            if w > 0:
                grads[w][at, lo:hi] = total
            else:
                for im in range(2):

                    @pl.when(img == im)
                    def _():
                        for i, p in enumerate(pair_lanes(lo // 384, im)):
                            lane = p - 1152 * im
                            grads[0][at, lane : lane + 128] = total[:, 128 * i : 128 * i + 128]

            return 0

        lax.fori_loop(0, WHOLES[w][0] // 16 // 48, step, 0)

    return pair_stage, first, second, third, fourth, sent


def table_taker():
    take = relative_layout(True)
    out = np.zeros((4, 128, 128), np.float32)
    for parity in range(2):
        for which in range(2):
            out[2 * parity + which, :, 64 * which : 64 * which + 27] = take[parity, which].T
    return out


def source_tiles(row, col):
    wide = row >= 2
    side_row = row + 2 * (1 - col // 2)
    table = []
    for image in range(2):
        table.append((image, 0, image, row - 1, col, row > 0))
        table.append((image, 1, image, row, col - 1, col > 0))
        table.append((image, 2, image, row - 1, col - 1, (row > 0) & (col > 0)))
    third_image = jnp.where(wide, 3 - row, 1 - lax.rem(col, 2))
    table.append((2, 0, third_image, 3, col, wide))
    table.append((2, 1, third_image, side_row, 3, jnp.logical_not(wide)))
    table.append((2, 2, third_image, jnp.where(wide, 3, side_row - 1), jnp.where(wide, col - 1, 3), jnp.where(wide, col, side_row) > 0))
    table.append((3, 2, 3 - row, 3, 3, wide & (col == 3)))
    return table


def returns(raws, landing, send, recv, row, col):
    def each(t, act):
        for slot, kind, image, tile_row, tile_col, present in source_tiles(row, col):
            here = (tile_row == row) & (tile_col == col)
            act(slot, kind, image, tile_row, tile_col, present & here, present & jnp.logical_not(here))

    def start(t):
        def act(slot, kind, image, tile_row, tile_col, local, remote):
            @pl.when(local)
            def _():
                pltpu.make_async_copy(
                    window_part(raws[t], slot, kind), landing[t][kind].at[image], recv.at[t, image, kind]
                ).start()

            @pl.when(remote)
            def _():
                hop(t, slot, kind, image, tile_row, tile_col).start()

        each(t, act)

    def hop(t, slot, kind, image, tile_row, tile_col):
        return pltpu.make_async_remote_copy(
            src_ref=window_part(raws[t], slot, kind),
            dst_ref=landing[t][kind].at[image],
            send_sem=send.at[t, slot, kind],
            recv_sem=recv.at[t, image, kind],
            device_id={"row": jnp.maximum(tile_row, 0), "col": jnp.maximum(tile_col, 0)},
            device_id_type=MESH,
        )

    def arrived(t):
        for image in range(2):
            for kind in range(3):
                goal = landing[t][kind].at[image]
                pltpu.make_async_copy(goal, goal, recv.at[t, image, kind]).wait()

    def left(t):
        def act(slot, kind, image, tile_row, tile_col, local, remote):
            @pl.when(remote)
            def _():
                hop(t, slot, kind, image, tile_row, tile_col).wait_send()

        each(t, act)

    return start, arrived, left


def merge_tiles(owns, landing, goals, row, col):
    places = lax.broadcasted_iota(jnp.int32, (16, 1), 0)
    in_left = places < 14 - 2 * col

    def rows16(values):
        return values.reshape(16, FEATURES).astype(F32)

    def right_half(values):
        low = values.reshape(8, FEATURES).astype(F32)
        return jnp.concatenate([low, low], axis=0)

    for image in range(2):

        def merge(tile_row, _):
            top = tile_row < 14 - 2 * row
            upper = jnp.minimum(tile_row, 13)
            lower = jnp.maximum(tile_row - 8, 0)
            for own, (below, right, both), goal in zip(owns, landing, goals):
                stacked = jnp.where(top, rows16(own(image, upper)), rows16(below[image, lower]))
                beside = jnp.where(top, right_half(right[image, upper]), right_half(both[image, lower]))
                goal[image, tile_row] = jnp.where(in_left, stacked, beside).astype(goal.dtype)
            return 0

        lax.fori_loop(0, 16, merge, 0)


def input_grad(at, dqkv, wq, xw, image_grad, gain, norm_sums):
    grad = nt(dqkv[at, :], wq).astype(BF).astype(F32)
    unit, inverse = unit_of(xw[at, :].astype(F32))
    image_grad[at, :] += norm_back(grad, unit, inverse, gain[...])
    norm_sums[0] += fold_rows(grad * unit)
    norm_sums[1] += fold_rows(grad)


def plain_close_kernel(dqkv, xw, dm, raw_r, wq, gain, out, grad_out, norm_sums, image_grad, raw_g, *refs):
    img, row, col = place()
    landing, (send, recv) = (refs[:3], refs[3:6]), refs[6:]
    greet(img, row, col, False)
    start, arrived, left = returns((raw_r, raw_g), landing, send, recv, row, col)
    start(0)
    norm_sums[...] = jnp.zeros_like(norm_sums)
    image_grad[...] = dm[...]

    def step(i, _):
        input_grad(pl.ds(pl.multiple_of(i * BLOCK, 16), BLOCK), dqkv, wq[...], xw, image_grad, gain, norm_sums)
        return 0

    lax.fori_loop(0, ROWS // BLOCK, step, 0)
    spread_rows(image_grad, raw_g, row, col)
    start(1)
    for t in range(2):
        arrived(t)
    owns = [lambda image, upper, raw=raw: raw[image * 22 + 8 + upper, 1:3] for raw in (raw_r, raw_g)]
    merge_tiles(owns, landing, (out, grad_out), row, col)
    for t in range(2):
        left(t)


PIECES = [(2, 8, 2, 8, FEATURES), (2, 14, 1, 8, FEATURES), (2, 8, 1, 8, FEATURES)]


def plain_close(dqkv, xw, dm, raw_r, wq, gain):
    vm = pl.BlockSpec(memory_space=pltpu.VMEM)
    shape = jax.ShapeDtypeStruct
    dma = pltpu.SemaphoreType.DMA
    pieces = [pltpu.VMEM(s, BF) for s in PIECES]
    return pl.pallas_call(
        plain_close_kernel,
        out_shape=[shape((2, 16, 16, FEATURES), BF), shape((2, 16, 16, FEATURES), F32), shape((2, 8, FEATURES), F32)],
        in_specs=[vm] * 6,
        out_specs=[vm] * 3,
        scratch_shapes=[pltpu.VMEM((ROWS, FEATURES), F32), pltpu.VMEM((88, 3, 8, FEATURES), BF)]
        + pieces
        + pieces
        + [dma((2, 4, 3)), dma((2, 2, 3))],
        compiler_params=pltpu.CompilerParams(collective_id=2, has_side_effects=True, vmem_limit_bytes=67043328),
    )(dqkv, xw, dm, raw_r, wq, gain)


def back_kernel(
    do, o, tab, bias, o_turned, da, n2_turned, cw, xw, n1_turned, gain, sums, up_sum, taker, probs, qkv_in, dh_in, g_in, dm_in, wq_in, raw_r, *refs
):
    out, grad_out, gq, go, gu, gd, small_out, table_out = refs[:8]
    qkv, probs_s, image_grad, shared_h, shared_g, own_r = refs[8:14]
    bias_sums, table_sums, norm_sums = refs[14:17]
    landing = (refs[17:20], refs[20:23])
    full = refs[23:27]
    small, table, small_land, table_land, small_z, table_z = refs[27:33]
    count = len(SUM_CHUNKS)
    lands = refs[33 : 33 + 5 * count]
    send, recv, load_sem, probs_sem, wsend, wrecv, ssend, srecv = refs[33 + 5 * count :]
    img, row, col = place()
    y_row = lax.rem(row + 2, 4)
    core_row = row + 1 - 2 * lax.rem(row, 2)
    other = 1 - img
    copies = []

    def load(i):
        pairs = (
            (dh_in, shared_h.at[pl.ds(0, ROWS)]),
            (g_in, shared_g),
            (qkv_in, qkv),
            (dm_in, image_grad),
            (wq_in, shared_h.at[:, pl.ds(0, 3 * FEATURES)]),
            (raw_r.at[pl.ds(8, 14), pl.ds(1, 2)], own_r.at[0]),
            (raw_r.at[pl.ds(30, 14), pl.ds(1, 2)], own_r.at[1]),
        )
        return pltpu.make_async_copy(pairs[i][0], pairs[i][1], load_sem.at[i])

    for i in (2, 1, 0, 3, 5, 6):
        load(i).start()
    windows = window_count(row, col)

    def fetch(k, window, slot):
        pair_index = lax.rem(k, 2) * 3 + k // 2
        return pltpu.make_async_copy(probs.at[window, pl.ds(2 * pair_index, 2)], probs_s.at[slot], probs_sem.at[slot])

    fetch(0, 0, 0).start()
    greet(img, row, col)
    start, arrived, left = returns((raw_r, shared_g), landing, send, recv, row, col)
    start(0)

    def turned_rows(ref):
        return lambda rw, kb: ref[pl.ds(pl.multiple_of(rw * kb, kb), kb), :]

    def turned_g(rw, kb):
        return shared_g[pl.ds(pl.multiple_of(rw * 32, 32), 32)].reshape(FEATURES, FEATURES)[:, 0:ROWS]

    pair_stage, first, second, third, fourth, sent = reducers(
        SUM_CHUNKS,
        full,
        (turned_rows(n1_turned), turned_rows(o_turned), turned_rows(n2_turned), turned_g),
        (qkv, da, shared_h, cw),
        (gq, go, gu, gd),
        lands,
        wsend,
        wrecv,
    )
    bias_sums[...] = jnp.zeros_like(bias_sums)
    table_sums[...] = jnp.zeros_like(table_sums)
    norm_sums[...] = jnp.zeros_like(norm_sums)
    pair_stage(0)
    load(2).wait()
    clear_idle(qkv, row, col)
    load(1).wait()
    load(0).wait()
    steps = [
        (pair_stage, 1),
        (first, 0),
        (pair_stage, 2),
        (first, 1, second, 0),
        (pair_stage, 3),
        (first, 2, third, 0),
        (pair_stage, 5, second, 1),
        (first, 3),
        (pair_stage, 4),
        (third, 1, second, 2),
        (first, 5, fourth, 0),
        (second, 3),
        (pair_stage, 6, third, 2),
        (first, 4),
        (second, 5, fourth, 1),
        (third, 3),
        (first, 6, second, 4),
        (third, 5, fourth, 2),
    ]

    def head_pair(k, _):
        pair_index = lax.rem(k, 2) * 3 + k // 2

        def each(window, _):
            for i, act in enumerate(steps):
                pl.when((k == i // 3) & (window == i % 3))(functools.partial(run_all, act))
            turn_count = k * windows + window
            slot = lax.rem(turn_count, 2)
            fetch(k, window, slot).wait()
            wrap = window + 1 == windows
            next_k = jnp.where(wrap, k + 1, k)

            @pl.when(next_k < 6)
            def _():
                fetch(next_k, jnp.where(wrap, 0, window + 1), 1 - slot).start()

            attention_back(
                window,
                pair_index,
                lambda parity: probs_s[slot, parity],
                do,
                qkv,
                o,
                tab,
                bias,
                bias_sums,
                table_sums,
                row,
                col,
            )
            return 0

        lax.fori_loop(0, windows, each, 0)
        return 0

    lax.fori_loop(0, 6, head_pair, 0)
    load(4).start()
    pair_stage(7)
    load(3).wait()
    load(4).wait()

    def grad_rows(i):
        input_grad(pl.ds(i * BLOCK, BLOCK), qkv, shared_h[:, 0 : 3 * FEATURES], xw, image_grad, gain, norm_sums)

    grad_rows(0)
    first(7)
    grad_rows(1)
    second(6)
    third(4)
    grad_rows(2)
    fourth(3)
    second(7)
    grad_rows(3)
    spread_rows(image_grad, shared_g, row, col)
    start(1)
    third(6)
    def over_rows(values):
        return jnp.sum(values, axis=0, keepdims=True)

    small[0] = jnp.zeros((16, FEATURES), F32)
    lines = [bias_sums[0], bias_sums[1], sums[0], sums[1], norm_sums[0], norm_sums[1], sums[2], sums[3]]
    for i, values in enumerate(lines):
        small[0, i : i + 1, :] = over_rows(values)
    for i in range(4):
        small[0, 8 + i : 9 + i, :] = over_rows(up_sum[:, i * FEATURES : (i + 1) * FEATURES])
    exact = lax.Precision.HIGHEST
    total = jnp.zeros((64, 128), F32)
    for parity in range(2):
        for which in range(2):
            part = table_sums[64 * parity : 64 * parity + 64, 256 * parity + 128 * which : 256 * parity + 128 * which + 128]
            total = total + jnp.dot(part, taker[2 * parity + which], precision=exact, preferred_element_type=F32)
    table[0] = total
    hops = ({"row": core_row}, {"row": y_row}, {"img": other})

    def small_push(k, src, dst, target):
        c = pltpu.make_async_remote_copy(
            src_ref=src, dst_ref=dst, send_sem=ssend.at[k], recv_sem=srecv.at[k], device_id=target, device_id_type=MESH
        )
        c.start()
        copies.append(c)
        return c

    def small_step(i):
        if 0 < i <= 3:
            for k, (acc, land) in enumerate(((small, small_land), (table, table_land))):
                pltpu.make_async_copy(land.at[i - 1], land.at[i - 1], srecv.at[2 * (i - 1) + k]).wait()
                acc[i] = acc[i - 1] + land[i - 1]
        if i < 3:
            for k, (acc, land) in enumerate(((small, small_land), (table, table_land))):
                small_push(2 * i + k, acc.at[i], land.at[i], hops[i])
        if i == 3:
            small_z[col] = small[3]
            table_z[col] = table[3]
            for d in range(1, 4):
                cl = lax.rem(col + d, 4)
                small_push(4 + 2 * d, small.at[3], small_z.at[col], {"col": cl})
                small_push(5 + 2 * d, table.at[3], table_z.at[col], {"col": cl})
        if i == 4:
            for d in range(1, 4):
                cl = lax.rem(col + 4 - d, 4)
                pltpu.make_async_copy(small_z.at[cl], small_z.at[cl], srecv.at[4 + 2 * d]).wait()
                pltpu.make_async_copy(table_z.at[cl], table_z.at[cl], srecv.at[5 + 2 * d]).wait()
            small_out[...] = (small_z[0] + small_z[1]) + (small_z[2] + small_z[3])
            table_out[...] = (table_z[0] + table_z[1]) + (table_z[2] + table_z[3])

    small_step(0)
    third(7)
    fourth(4)
    small_step(1)
    fourth(5)
    small_step(2)
    arrived(0)
    load(5).wait()
    load(6).wait()
    merge_tiles([lambda image, upper: own_r[image, upper]], landing[:1], (out,), row, col)
    small_step(3)
    fourth(6)
    fourth(7)
    small_step(4)
    arrived(1)
    merge_tiles([lambda image, upper: shared_g[image * 22 + 8 + upper, 1:3]], landing[1:], (grad_out,), row, col)
    left(0)
    left(1)
    for c in copies:
        c.wait_send()
    for copy in sent:
        copy().wait_send()


def back(do, o, tab, bias, o_turned, da, n2_turned, cw, xw, n1_turned, gain, sums, up_sum, probs, qkv, dh, g, dm, wq, raw_r):
    vm = pl.BlockSpec(memory_space=pltpu.VMEM)
    an = pl.BlockSpec(memory_space=pl.ANY)
    shape = jax.ShapeDtypeStruct
    dma = pltpu.SemaphoreType.DMA
    pieces = [pltpu.VMEM(s, BF) for s in PIECES]
    count = len(SUM_CHUNKS)
    return pl.pallas_call(
        back_kernel,
        out_shape=[shape((2, 16, 16, FEATURES), BF), shape((2, 16, 16, FEATURES), F32)]
        + [shape((k // 16, n // 2), F32) for k, n in WHOLES]
        + [shape((16, FEATURES), F32), shape((64, 128), F32)],
        in_specs=[vm] * 14 + [an] * 7,
        out_specs=[vm] * 8,
        scratch_shapes=[
            pltpu.VMEM((SPAN, 3 * FEATURES), BF),
            pltpu.VMEM((2, 2, 224, 224), BF),
            pltpu.VMEM((ROWS, FEATURES), F32),
            pltpu.VMEM((FEATURES, 4 * FEATURES), BF),
            pltpu.VMEM((128, 3, 8, FEATURES), BF),
            pltpu.VMEM((2, 14, 2, 8, FEATURES), BF),
            pltpu.VMEM((2, 8, FEATURES), F32),
            pltpu.VMEM((128, 512), F32),
            pltpu.VMEM((2, 8, FEATURES), F32),
        ]
        + pieces
        + pieces
        + [pltpu.VMEM(s, BF) for s in WHOLES]
        + [
            pltpu.VMEM((4, 16, FEATURES), F32),
            pltpu.VMEM((4, 64, 128), F32),
            pltpu.VMEM((3, 16, FEATURES), F32),
            pltpu.VMEM((3, 64, 128), F32),
            pltpu.VMEM((4, 16, FEATURES), F32),
            pltpu.VMEM((4, 64, 128), F32),
        ]
        + land_shapes(SUM_CHUNKS)
        + [dma((2, 4, 3)), dma((2, 2, 3)), dma((7,)), dma((2,)), dma((count, 13)), dma((count, 13)), dma((12,)), dma((12,))],
        compiler_params=pltpu.CompilerParams(collective_id=1, has_side_effects=True, vmem_limit_bytes=67043328),
    )(
        do, o, tab, bias, o_turned, da, n2_turned, cw, xw, n1_turned, gain, sums, up_sum, jnp.asarray(table_taker()),
        probs, qkv, dh, g.reshape(128, 3, 8, FEATURES), dm, wq, raw_r,
    )


def on_device(
    image_in,
    cotangent,
    qkv_weight,
    out_weight,
    up_weight,
    down_weight,
    query_bias,
    value_bias,
    out_bias,
    up_bias,
    down_bias,
    first_gain,
    first_shift,
    second_gain,
    second_shift,
    rows_table,
    cols_table,
):
    line = lambda v: v.reshape(1, -1)
    bias_all = line(jnp.concatenate([query_bias, jnp.zeros_like(query_bias), value_bias]))
    tab = table_operand(rows_table, cols_table, False)
    tab_back = table_operand(rows_table, cols_table, True)
    xw, cw, n1_turned, qkv, probs, o, o_turned, wq, wo, wu, wd = open_windows(
        image_in, cotangent, (qkv_weight, out_weight, up_weight, down_weight), line(first_gain), line(first_shift), bias_all, tab
    )
    raw_r, n2_turned, g_turned, dh, da, do, dm, sums, up_sum = middle(
        o, xw, cw, wo, wu, wd, line(out_bias), line(up_bias), line(down_bias), line(second_gain), line(second_shift)
    )
    if lax.axis_size("img") == 2:
        *large, small, table = back(
            do, o, tab_back, bias_all, o_turned, da, n2_turned, cw, xw, n1_turned, line(first_gain), sums, up_sum,
            probs, qkv, dh, g_turned, dm, wq, raw_r,
        )
        return (
            *large,
            small[0],
            small[1],
            small[2],
            small[8:12].reshape(-1),
            *(small[i] for i in range(3, 8)),
            table[:, :27].T,
            table[:, 64:91].T,
        )
    dqkv, bias_sums, table_sums = plain_back(do, probs, qkv, o, tab_back, bias_all)
    image_out, image_grad, norm_sums = plain_close(dqkv, xw, dm, raw_r, wq, line(first_gain))
    dot = lambda a, b: jnp.dot(a, b, preferred_element_type=F32)
    totals = (dot(n1_turned, dqkv[:ROWS]), dot(o_turned, da), dot(n2_turned, dh), dot(g_turned[:, :ROWS], cw))
    shard_sums = []
    for total in totals:
        part = lax.psum_scatter(total.astype(BF), ("row", "col"), scatter_dimension=0, tiled=True)
        shard_sums.append(lax.psum_scatter(part, "img", scatter_dimension=1, tiled=True).astype(F32))
    rows_grad, cols_grad = table_grads(table_sums)
    small_sums = lax.psum(
        tuple(jnp.sum(bias_sums, axis=1))
        + (jnp.sum(sums[0], axis=0), jnp.sum(up_sum, axis=0), jnp.sum(sums[1], axis=0))
        + tuple(jnp.sum(norm_sums, axis=1))
        + (jnp.sum(sums[2], axis=0), jnp.sum(sums[3], axis=0), rows_grad, cols_grad),
        ("img", "row", "col"),
    )
    return (image_out, image_grad, *shard_sums, *small_sums)


def solution(mesh):
    tiles = P("img", "row", "col", None)
    shards = P(("row", "col"), "img")
    return jax.shard_map(
        on_device,
        mesh=mesh,
        in_specs=(tiles,) * 2 + (shards,) * 4 + (P(),) * 11,
        out_specs=(tiles,) * 2 + (shards,) * 4 + (P(),) * 11,
        check_vma=False,
    )
```

time: 331 us -> 289 us (0.87)
  Pallas kernels: 300 us -> 257 us
    pallas_call x3 -> x2, Pallas kernels: 187 us -> 149 us  [the longest x1 113 us: back(): pl.pallas_call(back_kernel, out_shape=[shape((2, 16, 16, FEATURES), BF),...]
    pallas_call x1, Pallas kernels: 113 us -> 108 us  [open_windows(): pl.pallas_call(functools.partial(open_kernel, weights), out_shape=[shape(...]
where the time goes in v2:
time: 289 us; the launch traced here: 284 us
  Pallas kernels  257 us (89%)
  local copies, waits for them, and re-layouts  19.6 us (7%)
  matrix products  4.42 us (2%)
    pallas_call x1, Pallas kernels, back(): pl.pallas_call(back_kernel, out_shape=[shape((2, 16, 16, FEATURES), BF),...  113 us
    pallas_call x1, Pallas kernels, open_windows(): pl.pallas_call(functools.partial(open_kernel, weights), out_shape=[shape(...  108 us
    pallas_call x1, Pallas kernels, middle(): pl.pallas_call(middle_kernel, grid=(FF // CHUNK,), out_shape=[shape((88,...  36.2 us
    reshape x7, local copies, waits for them, and re-layouts, on_device(): line = lambda v: v.reshape(1, -1)  8.21 us
    unnamed x30, local copies, waits for them, and re-layouts  7.38 us

profile of v2, /device:TPU:0, one launch (start us, length us, event | category | flops | bytes accessed | tf_op | source)
XLA Modules:
  0.0 283.9 jit_solution(7056936911654808196)
XLA Ops:
  0.7 0.9 fusion
  1.6 0.9 fusion.1
  2.5 0.9 fusion.2
  3.4 0.9 fusion.3
  5.0 0.7 pad_maximum_fusion.2
  6.3 1.3 reshape.73.gain
  7.6 1.3 reshape.74.shift
  8.8 108.0 %shard_map.323 = (bf16[704,768]{1,0:T(8,128)(2,1)}, bf16[704,768]{1,0:T(8,128)(2,1)}, bf16[768,704]{1,0:T(8,128)(2,1)}, bf16[800,2304]{1,0:T(8,128)(2,1)}, bf16[...) custom-call(bf16[2,16,2,8,768]{4,3,2,1,0:T(8,128)(2,1)} %bitcast.41,, ...), custom_call_target="tpu_custom_call" | custom-call | tf_op jit(solution)/shard_map/pallas_call | solution.py:514
  116.8 1.3 reshape.76.out_bias
  118.1 1.3 reshape.78.down_bias
  119.4 1.3 reshape.79.gain
  120.6 1.3 reshape.80.shift
  121.9 36.2 %shard_map.324 = (bf16[88,3,8,768]{3,2,1,0:T(8,128)(2,1)}, bf16[768,704]{1,0:T(8,128)(2,1)}, bf16[3072,768]{1,0:T(8,128)(2,1)}, bf16[704,3072]{1,0:T(8,128)(2,1)...) custom-call(bf16[800,768]{1,0:T(8,128)(2,1)} %get-tuple-element.45.o, ...), custom_call_target="tpu_custom_call" | custom-call | tf_op jit(solution)/shard_map/pallas_call | solution.py:647
  159.7 112.8 %shard_map.325 = (bf16[2,16,16,768]{3,2,1,0:T(8,128)(2,1)}, f32[2,16,16,768]{3,2,1,0:T(8,128)}, f32[48,1152]{1,0:T(8,128)}, f32[48,384]{1,0:T(8,128)}, f32[48,15...) custom-call(bf16[800,768]{1,0:T(8,128)(2,1)} %get-tuple-element.51.do, ...), custom_call_target="tpu_custom_call" | custom-call | tf_op jit(solution)/shard_map/pallas_call | solution.py:1334
  272.5 1.0 slice_bitcast_fusion
  273.5 0.7 copy.37
  274.2 0.7 copy.38
  274.9 1.7 slice_reduce_fusion
  276.6 0.7 slice.68
  277.9 2.1 copy.45
  280.0 1.1 copy.46
  281.2 0.7 copy.47
  282.5 0.7 copy.49
  283.2 0.7 copy.50
  (34 shorter events, 4.0 us)
Async XLA Ops:
  121.9 36.3 %copy-start.5 = (bf16[27,64]{1,0:T(8,128)(2,1)S(1)}, bf16[27,64]{1,0:T(8,128)(2,1)}, u32[]{:S(2)}) copy-start(bf16[27,64]{1,0:T(8,128)(2,1)} %param.35) | copy-start | bytes 10372
  121.9 36.3 %copy-start.10 = (bf16[27,128]{1,0:T(8,128)(2,1)S(1)}, bf16[27,128]{1,0:T(8,128)(2,1)}, u32[]{:S(2)}) copy-start(bf16[27,128]{1,0:T(8,128)(2,1)} %constant.30) | copy-start | bytes 20740
  121.9 36.5 %copy-start.6 = (bf16[27,64]{1,0:T(8,128)(2,1)S(1)}, bf16[27,64]{1,0:T(8,128)(2,1)}, u32[]{:S(2)}) copy-start(bf16[27,64]{1,0:T(8,128)(2,1)} %param.36) | copy-start | bytes 10372
  121.9 36.5 %copy-start.9 = (bf16[27,128]{1,0:T(8,128)(2,1)S(1)}, bf16[27,128]{1,0:T(8,128)(2,1)}, u32[]{:S(2)}) copy-start(bf16[27,128]{1,0:T(8,128)(2,1)} %constant.32) | copy-start | bytes 20740
  121.9 36.7 %copy-start.8 = (bf16[27,128]{1,0:T(8,128)(2,1)S(1)}, bf16[27,128]{1,0:T(8,128)(2,1)}, u32[]{:S(2)}) copy-start(bf16[27,128]{1,0:T(8,128)(2,1)} %constant.34) | copy-start | bytes 20740
  121.9 36.9 %copy-start.7 = (bf16[27,128]{1,0:T(8,128)(2,1)S(1)}, bf16[27,128]{1,0:T(8,128)(2,1)}, u32[]{:S(2)}) copy-start(bf16[27,128]{1,0:T(8,128)(2,1)} %constant.36) | copy-start | bytes 20740
  272.5 7.5 %copy-start = (f32[2,16,16,768]{3,2,1,0:T(8,128)S(1)}, f32[2,16,16,768]{3,2,1,0:T(8,128)}, u32[]{:S(2)}) copy-start(f32[2,16,16,768]{3,2,1,0:T(8,128)} %get-tuple-element.122) | copy-start | bytes 4718596
  280.0 1.2 copy-start.3
  280.0 1.9 copy-start.4
  280.0 2.5 copy-start.2
  280.0 3.2 %copy-start.1 = (f32[192,384]{1,0:T(8,128)S(1)}, f32[192,384]{1,0:T(8,128)}, u32[]{:S(2)}) copy-start(f32[192,384]{1,0:T(8,128)} %get-tuple-element.126) | copy-start | bytes 884740

commit v3 on v2

--- a/solution.py
+++ b/solution.py
@@ -294,17 +294,38 @@
     return take
 
 
-def table_operand(rows_table, cols_table, backward):
-    take = jnp.asarray(relative_layout(backward), BF)
-    parts = []
+def takers(backward):
+    return jnp.asarray(relative_layout(backward).reshape(4, 27, 128), BF)
+
+
+def build_table(tab, rows_table, cols_table, take):
+    tab[...] = jnp.zeros_like(tab)
     for parity in range(2):
-        both = []
         for which, table in ((0, rows_table), (1, cols_table)):
-            both.append(lax.dot_general(table, take[parity, which], (((0,), (0,)), ((), ())), preferred_element_type=F32).astype(BF))
-        block = jnp.concatenate(both, axis=1)
-        zero = jnp.zeros_like(block)
-        parts.append(jnp.concatenate([block, zero] if parity == 0 else [zero, block], axis=0))
-    return jnp.concatenate(parts, axis=1)
+            block = lax.dot_general(table[...], take[2 * parity + which], (((0,), (0,)), ((), ())), preferred_element_type=F32)
+            lane = 256 * parity + 128 * which
+            tab[64 * parity : 64 * parity + 64, lane : lane + 128] = block.astype(BF)
+
+
+def as_row(ref):
+    return ref[...].reshape(1, -1)
+
+
+def run_all(acts):
+    for act in acts:
+        act[0](*act[1:])
+
+
+def plan_slots(plan, acts):
+    slots = [[]]
+    for name in plan:
+        if name == "|":
+            slots.append([])
+        elif name in acts:
+            slots[-1].append((acts[name],))
+        else:
+            slots[-1].append((acts[name[0]], int(name[1:])))
+    return slots
 
 
 def table_grads(sums):
@@ -319,26 +340,25 @@
     return grads
 
 
-def run_all(act):
-    for i in range(0, len(act), 2):
-        act[i](act[i + 1])
-
-
-def open_kernel(weights, x_ref, c_ref, gain, shift, bias, tab, *refs):
+OPEN_PLAN = ("a0", "a1", "11", "a5", "a3", "10", "21", "20", "a6", "15", "13", "31", "25", "Wx", "30", "L0", "16", "23", "35", "a4", "X", "26", "L1", "P", "|", "|", "a2", "|", "|", "14", "|", "|", "|", "12", "|", "Wc", "L5", "|", "36", "|", "|", "|", "24", "|", "|", "L6", "|", "|", "33", "|", "|", "22", "T", "34", "32", "K", "L2", "L3", "L4")
+
+
+def open_kernel(weights, x_ref, c_ref, gain, shift, query_bias, value_bias, rows_table, cols_table, take, *refs):
     img, row, col = place()
     greet(img, row, col, weights)
     if weights:
         shards, refs = refs[:4], refs[4:]
     else:
         wq, refs = refs[0], refs[1:]
-    xw, cw, n1_turned, qkv_s, probs, o, o_turned = refs[:7]
+    xw, cw, n1_turned, qkv_out, probs_out, o, o_turned = refs[:7]
     refs = refs[7:]
     if weights:
         fulls, refs = refs[:4], refs[4:]
-        wq = fulls[0]
-    rawx, rawc, n1, send, recv, loc = refs[:6]
+    rawx, rawc, n1, tab, row_bias, qkv_s, probs, out_sem, probs_sem, send, recv, loc = refs[:12]
+    refs = refs[12:]
     if weights:
-        along_col, first, second, third, last, sent = links(shards, fulls, *refs[6:])
+        wq, wq_out = refs[0], fulls[0]
+        along_col, first, second, third, last, sent = links(shards, (wq, *fulls[1:]), *refs[1:])
     window_start, window_arrived, window_left = window_moves((x_ref, c_ref), (rawx, rawc), send, recv, loc)
     places = lax.broadcasted_iota(jnp.int32, (16, 1), 0)
 
@@ -353,7 +373,7 @@
         keep, x = cut_one(rawx, step)
         xw[at, :] = x.astype(BF)
         unit, _inverse = unit_of(x)
-        n1[at, :] = jnp.where(keep, unit * gain[...] + shift[...], 0.0).astype(BF)
+        n1[at, :] = jnp.where(keep, unit * as_row(gain) + as_row(shift), 0.0).astype(BF)
         return 0
 
     def cut_c(step, _):
@@ -366,7 +386,9 @@
         at = pl.ds(pl.multiple_of(step * 352, 32), 352)
         for part_index in range(3):
             lanes = slice(part_index * FEATURES, (part_index + 1) * FEATURES)
-            part = jnp.dot(n1[at, :], wq[:, lanes], preferred_element_type=F32) + bias[:, lanes]
+            part = jnp.dot(n1[at, :], wq[:, lanes], preferred_element_type=F32)
+            if part_index != 1:
+                part = part + row_bias[part_index // 2]
             qkv_s[at, lanes] = part.astype(BF)
         return 0
 
@@ -378,58 +400,52 @@
 
         lax.fori_loop(0, FEATURES // 128, step, 0)
 
+    def cut_windows():
+        window_arrived(0)
+        lax.fori_loop(0, 44, cut_x, 0)
+
+    def cut_cotangent():
+        window_arrived(1)
+        lax.fori_loop(0, 44, cut_c, 0)
+
+    def project_all():
+        lax.fori_loop(0, 2, project, 0)
+        pltpu.make_async_copy(qkv_s, qkv_out, out_sem.at[0]).start()
+        if weights:
+            pltpu.make_async_copy(wq, wq_out, out_sem.at[1]).start()
+
+    def turn_all():
+        turn(n1, n1_turned)
+        turn(o, o_turned)
+
+    acts = {"X": cut_windows, "P": project_all, "T": turn_all, "K": cut_cotangent}
+    acts["Wx"] = functools.partial(window_start, 0)
+    acts["Wc"] = functools.partial(window_start, 1)
     if weights:
-        along_col(0)
-        along_col(1)
+        acts.update({"a": along_col, "1": first, "2": second, "3": third, "L": last})
+        slots = plan_slots(OPEN_PLAN, acts)
     else:
-        window_start(0)
-        window_start(1)
+        slots = plan_slots(("Wx", "Wc", "X", "P", *("|",) * 18, "T", "K"), acts)
     o[...] = jnp.zeros_like(o)
-    if weights:
-        first(0)
-        first(1)
-        window_start(0)
-        along_col(2)
-        second(0)
-        second(1)
-        along_col(3)
-    window_arrived(0)
-    lax.fori_loop(0, 44, cut_x, 0)
-    steps = []
-    if weights:
-        first(2)
-        along_col(4)
-        third(0)
-        third(1)
-        first(3)
-        along_col(5)
-        last(0)
-        last(1)
-        steps = [
-            (second, 2),
-            (first, 4, along_col, 6),
-            (second, 3),
-            (third, 2),
-            (first, 5, window_start, 1),
-            (second, 4),
-            (third, 3),
-            (first, 6),
-            (second, 5),
-            (third, 4),
-            (second, 6),
-            (third, 5),
-            (third, 6),
-        ]
-    lax.fori_loop(0, 2, project, 0)
+    build_table(tab, rows_table, cols_table, take)
+    row_bias[0] = as_row(query_bias)
+    row_bias[1] = as_row(value_bias)
+    run_all(slots[0])
     row_of = lax.broadcasted_iota(jnp.int32, (224, 1), 0)
     lane = lax.broadcasted_iota(jnp.int32, (1, 128), 1)
     key_place = lax.broadcasted_iota(jnp.int32, (224, 128), 0)
     key_lane = lax.broadcasted_iota(jnp.int32, (224, 128), 1)
     key_a, key_b = key_place // 16, key_place % 16
 
+    def probs_copy(index):
+        window, pair_index = index // 6, index % 6
+        part = pl.ds(2 * pair_index, 2)
+        return pltpu.make_async_copy(probs.at[window, part], probs_out.at[window, part], probs_sem.at[window, pair_index])
+
     def pair(index, _):
-        for turn_index, act in enumerate(steps):
-            pl.when(index == turn_index)(functools.partial(run_all, act))
+        for i, slot_acts in enumerate(slots[1:-1]):
+            if slot_acts:
+                pl.when(index == i + 1)(functools.partial(run_all, slot_acts))
         window, pair_index = index // 6, index % 6
         start, tall, width = window_params(window, row, col)
         at = pl.ds(pl.multiple_of(start * 16, 16), 224)
@@ -437,7 +453,7 @@
         lanes = lambda third: pl.ds(pl.multiple_of(third * FEATURES + pair_index * 128, 128), 128)
         q = jnp.where(alive, qkv_s[at, lanes(0)].astype(F32), 0.0)
         k = jnp.where(alive, qkv_s[at, lanes(1)].astype(F32), 0.0)
-        v = jnp.where(alive, qkv_s[at, lanes(2)].astype(F32), bias[:, lanes(2)].astype(BF).astype(F32)).astype(BF)
+        v = jnp.where(alive, qkv_s[at, lanes(2)].astype(F32), row_bias[1, :, lanes(0)].astype(BF).astype(F32)).astype(BF)
         terms = jnp.dot(q.astype(BF), tab[...], preferred_element_type=F32)
         outs = []
         for parity in range(2):
@@ -481,23 +497,23 @@
         out_lanes = pl.ds(pl.multiple_of(pair_index * 128, 128), 128)
         o_at = pl.ds(pl.multiple_of(start * 16, 16), 224)
         o[o_at, out_lanes] = jnp.where(alive, blended, 0.0).astype(BF)
+        probs_copy(index).start()
         return 0
 
-    lax.fori_loop(0, window_count(row, col) * 6, pair, 0)
-    turn(n1, n1_turned)
-    turn(o, o_turned)
-    window_arrived(1)
-    lax.fori_loop(0, 44, cut_c, 0)
+    pairs = window_count(row, col) * 6
+    lax.fori_loop(0, pairs, pair, 0)
+    run_all(slots[-1])
+    pltpu.make_async_copy(qkv_s, qkv_out, out_sem.at[0]).wait()
     if weights:
-        for n in range(2, len(CHUNKS)):
-            last(n)
+        pltpu.make_async_copy(wq, wq_out, out_sem.at[1]).wait()
         for copy in sent:
             copy().wait_send()
+    lax.fori_loop(0, pairs, lambda index, _: (probs_copy(index).wait(), 0)[1], 0)
     window_left(0)
     window_left(1)
 
 
-def open_windows(x, c, shards, gain, shift, bias, tab):
+def open_windows(x, c, shards, gain, shift, query_bias, value_bias, rows_table, cols_table):
     vm = pl.BlockSpec(memory_space=pltpu.VMEM)
     an = pl.BlockSpec(memory_space=pl.ANY)
     shape = jax.ShapeDtypeStruct
@@ -523,12 +539,25 @@
             shape((FEATURES, ROWS), BF),
         ]
         + [shape(s, BF) for s in wholes],
-        in_specs=[vm] * (6 + len(given)),
-        out_specs=[vm] * 7 + ([vm, an, an, an] if weights else []),
-        scratch_shapes=[raw, raw, pltpu.VMEM((ROWS, FEATURES), BF), dma((2, 2, 3)), dma((2, 4, 3)), dma((2, 2))]
-        + ([dma((chunks, 16)), dma((chunks, 16)), dma((chunks,))] if weights else []),
+        in_specs=[vm] * (9 + len(given)),
+        out_specs=[vm, vm, vm, an, an, vm, vm] + [an] * len(wholes),
+        scratch_shapes=[
+            raw,
+            raw,
+            pltpu.VMEM((ROWS, FEATURES), BF),
+            pltpu.VMEM((128, 512), BF),
+            pltpu.VMEM((2, 1, FEATURES), F32),
+            pltpu.VMEM((SPAN, 3 * FEATURES), BF),
+            pltpu.VMEM((4, 12, 224, 224), BF),
+            dma((2,)),
+            dma((4, 6)),
+            dma((2, 2, 3)),
+            dma((2, 4, 3)),
+            dma((2, 2)),
+        ]
+        + ([pltpu.VMEM((768, 2304), BF), dma((chunks, 16)), dma((chunks, 16)), dma((chunks,))] if weights else []),
         compiler_params=pltpu.CompilerParams(collective_id=0, has_side_effects=True, vmem_limit_bytes=67043328),
-    )(x.reshape(2, 16, 2, 8, 768), c.reshape(2, 16, 2, 8, 768), gain, shift, bias, tab, *given)
+    )(x.reshape(2, 16, 2, 8, 768), c.reshape(2, 16, 2, 8, 768), gain, shift, query_bias, value_bias, rows_table, cols_table, takers(False), *given)
     return list(outs) if weights else list(outs) + gathered
 
 
@@ -578,7 +607,7 @@
     blocks = [slice(i * BLOCK, (i + 1) * BLOCK) for i in range(ROWS // BLOCK)]
 
     def mid_of(at):
-        return xw[at, :].astype(F32) + (jnp.dot(o[at, :], wo[...], preferred_element_type=F32) + out_bias[...])
+        return xw[at, :].astype(F32) + (jnp.dot(o[at, :], wo[...], preferred_element_type=F32) + as_row(out_bias))
 
     @pl.when(step == 0)
     def _():
@@ -589,8 +618,8 @@
             at = pl.ds(pl.multiple_of(i * BLOCK, 16), BLOCK)
             mid = mid_of(at)
             unit, _inverse = unit_of(mid)
-            n2[at, :] = (unit * gain[...] + shift[...]).astype(BF)
-            y_s[at, :] = mid + down_bias[...]
+            n2[at, :] = (unit * as_row(gain) + as_row(shift)).astype(BF)
+            y_s[at, :] = mid + as_row(down_bias)
             dm[at, :] = mid
             return 0
 
@@ -626,7 +655,7 @@
             unit, inverse = unit_of(dm[at, :])
             grad = d_s[at, :].astype(BF).astype(F32)
             up = cw[at, :].astype(F32)
-            grad_mid = up + norm_back(grad, unit, inverse, gain[...])
+            grad_mid = up + norm_back(grad, unit, inverse, as_row(gain))
             low_grad = grad_mid.astype(BF)
             dm[at, :] = grad_mid
             da[at, :] = low_grad
@@ -665,11 +694,11 @@
             once(FEATURES, FEATURES),
             pl.BlockSpec((FEATURES, CHUNK), lambda i: (0, i)),
             pl.BlockSpec((CHUNK, FEATURES), lambda i: (i, 0)),
-            once(1, FEATURES),
+            once(FEATURES),
             pl.BlockSpec((1, CHUNK), lambda i: (0, i)),
-            once(1, FEATURES),
-            once(1, FEATURES),
-            once(1, FEATURES),
+            once(FEATURES),
+            once(FEATURES),
+            once(FEATURES),
         ],
         out_specs=[
             once(88, 3, 8, FEATURES),
@@ -692,7 +721,7 @@
     )(o, xw, cw, wo, wu, wd, out_bias, up_bias, down_bias, gain, shift)
 
 
-def attention_back(window, pair_index, probs_of, do, qkv, o, tab, bias, bias_sums, table_sums, row, col):
+def attention_back(window, pair_index, probs_of, do, qkv, o, tab, value_bias, bias_sums, table_sums, row, col):
     row_of = lax.broadcasted_iota(jnp.int32, (224, 1), 0)
     lane = lax.broadcasted_iota(jnp.int32, (1, 128), 1)
     key_place = lax.broadcasted_iota(jnp.int32, (224, 128), 0)
@@ -706,7 +735,7 @@
     old = [qkv[at, lanes(third)].astype(F32) for third in range(3)]
     q = jnp.where(alive, old[0], 0.0)
     k = jnp.where(alive, old[1], 0.0)
-    v = jnp.where(alive, old[2], bias[:, lanes(2)].astype(BF).astype(F32))
+    v = jnp.where(alive, old[2], value_bias[:, lanes(0)].astype(BF).astype(F32))
     grad = jnp.where(alive, do[at, lanes(0)].astype(F32), 0.0)
     product = grad * jnp.where(alive, o[at, lanes(0)].astype(F32), 0.0)
     q_turned = q.T.astype(BF)
@@ -763,8 +792,10 @@
             qkv[16 * a : 16 * a + 16, :] = jnp.zeros((16, 3 * FEATURES), BF)
 
 
-def plain_back_kernel(do, probs, qkv, o, tab, bias, dqkv, bias_sums, table_sums):
+def plain_back_kernel(do, probs, qkv, o, value_bias, rows_table, cols_table, take, dqkv, bias_sums, table_sums, tab, row_bias):
     row, col = lax.axis_index("row"), lax.axis_index("col")
+    build_table(tab, rows_table, cols_table, take)
+    row_bias[...] = as_row(value_bias)
     dqkv[...] = qkv[...]
     clear_idle(dqkv, row, col)
     bias_sums[...] = jnp.zeros_like(bias_sums)
@@ -780,7 +811,7 @@
             dqkv,
             o,
             tab,
-            bias,
+            row_bias,
             bias_sums,
             table_sums,
             row,
@@ -791,16 +822,17 @@
     lax.fori_loop(0, window_count(row, col) * 6, pair, 0)
 
 
-def plain_back(do, probs, qkv, o, tab, bias):
+def plain_back(do, probs, qkv, o, value_bias, rows_table, cols_table):
     vm = pl.BlockSpec(memory_space=pltpu.VMEM)
     shape = jax.ShapeDtypeStruct
     return pl.pallas_call(
         plain_back_kernel,
         out_shape=[shape((SPAN, 3 * FEATURES), BF), shape((2, 8, FEATURES), F32), shape((128, 512), F32)],
-        in_specs=[vm] * 6,
+        in_specs=[vm] * 8,
         out_specs=[vm] * 3,
+        scratch_shapes=[pltpu.VMEM((128, 512), BF), pltpu.VMEM((1, FEATURES), F32)],
         compiler_params=pltpu.CompilerParams(vmem_limit_bytes=62 << 20),
-    )(do, probs, qkv, o, tab, bias)
+    )(do, probs, qkv, o, value_bias, rows_table, cols_table, takers(True))
 
 
 WHOLES = ((768, 2304), (768, 768), (768, 3072), (3072, 768))
@@ -981,6 +1013,9 @@
     return table
 
 
+CLOSE_PLAN = ("p1", "|", "p0", "11", "p2", "10", "p3", "12", "|", "21", "20", "|", "|", "|", "|", "p4", "|", "13", "|", "|", "31", "22", "|", "|", "30", "p5", "|", "|", "|", "15", "|", "32", "|", "23", "|", "|", "25", "G0", "14", "33", "G1", "p7", "41", "G2", "35", "40", "17", "G3", "s0", "S", "24", "s1", "27", "37", "43", "34", "p6", "s2", "16", "42", "s3", "26", "36", "44", "46", "47", "45", "s4")
+
+
 def returns(raws, landing, send, recv, row, col):
     def each(t, act):
         for slot, kind, image, tile_row, tile_col, present in source_tiles(row, col):
@@ -1057,7 +1092,7 @@
 def input_grad(at, dqkv, wq, xw, image_grad, gain, norm_sums):
     grad = nt(dqkv[at, :], wq).astype(BF).astype(F32)
     unit, inverse = unit_of(xw[at, :].astype(F32))
-    image_grad[at, :] += norm_back(grad, unit, inverse, gain[...])
+    image_grad[at, :] += norm_back(grad, unit, inverse, as_row(gain))
     norm_sums[0] += fold_rows(grad * unit)
     norm_sums[1] += fold_rows(grad)
 
@@ -1108,17 +1143,17 @@
 
 
 def back_kernel(
-    do, o, tab, bias, o_turned, da, n2_turned, cw, xw, n1_turned, gain, sums, up_sum, taker, probs, qkv_in, dh_in, g_in, dm_in, wq_in, raw_r, *refs
+    do, o, value_bias, rows_table, cols_table, take, o_turned, da, n2_turned, cw, xw, n1_turned, gain, sums, up_sum, taker, probs, qkv_in, dh_in, g_in, dm_in, wq_in, raw_r, *refs
 ):
     out, grad_out, gq, go, gu, gd, small_out, table_out = refs[:8]
     qkv, probs_s, image_grad, shared_h, shared_g, own_r = refs[8:14]
-    bias_sums, table_sums, norm_sums = refs[14:17]
-    landing = (refs[17:20], refs[20:23])
-    full = refs[23:27]
-    small, table, small_land, table_land, small_z, table_z = refs[27:33]
+    bias_sums, table_sums, norm_sums, tab, row_bias = refs[14:19]
+    landing = (refs[19:22], refs[22:25])
+    full = refs[25:29]
+    small, table, small_land, table_land, small_z, table_z = refs[29:35]
     count = len(SUM_CHUNKS)
-    lands = refs[33 : 33 + 5 * count]
-    send, recv, load_sem, probs_sem, wsend, wrecv, ssend, srecv = refs[33 + 5 * count :]
+    lands = refs[35 : 35 + 5 * count]
+    send, recv, load_sem, probs_sem, wsend, wrecv, ssend, srecv = refs[35 + 5 * count :]
     img, row, col = place()
     y_row = lax.rem(row + 2, 4)
     core_row = row + 1 - 2 * lax.rem(row, 2)
@@ -1169,104 +1204,42 @@
     bias_sums[...] = jnp.zeros_like(bias_sums)
     table_sums[...] = jnp.zeros_like(table_sums)
     norm_sums[...] = jnp.zeros_like(norm_sums)
-    pair_stage(0)
+    build_table(tab, rows_table, cols_table, take)
+    row_bias[...] = as_row(value_bias)
     load(2).wait()
     clear_idle(qkv, row, col)
     load(1).wait()
     load(0).wait()
-    steps = [
-        (pair_stage, 1),
-        (first, 0),
-        (pair_stage, 2),
-        (first, 1, second, 0),
-        (pair_stage, 3),
-        (first, 2, third, 0),
-        (pair_stage, 5, second, 1),
-        (first, 3),
-        (pair_stage, 4),
-        (third, 1, second, 2),
-        (first, 5, fourth, 0),
-        (second, 3),
-        (pair_stage, 6, third, 2),
-        (first, 4),
-        (second, 5, fourth, 1),
-        (third, 3),
-        (first, 6, second, 4),
-        (third, 5, fourth, 2),
-    ]
-
-    def head_pair(k, _):
-        pair_index = lax.rem(k, 2) * 3 + k // 2
-
-        def each(window, _):
-            for i, act in enumerate(steps):
-                pl.when((k == i // 3) & (window == i % 3))(functools.partial(run_all, act))
-            turn_count = k * windows + window
-            slot = lax.rem(turn_count, 2)
-            fetch(k, window, slot).wait()
-            wrap = window + 1 == windows
-            next_k = jnp.where(wrap, k + 1, k)
-
-            @pl.when(next_k < 6)
-            def _():
-                fetch(next_k, jnp.where(wrap, 0, window + 1), 1 - slot).start()
-
-            attention_back(
-                window,
-                pair_index,
-                lambda parity: probs_s[slot, parity],
-                do,
-                qkv,
-                o,
-                tab,
-                bias,
-                bias_sums,
-                table_sums,
-                row,
-                col,
-            )
-            return 0
-
-        lax.fori_loop(0, windows, each, 0)
-        return 0
-
-    lax.fori_loop(0, 6, head_pair, 0)
-    load(4).start()
-    pair_stage(7)
-    load(3).wait()
-    load(4).wait()
 
     def grad_rows(i):
+        if i == 0:
+            load(4).start()
+            load(3).wait()
+            load(4).wait()
         input_grad(pl.ds(i * BLOCK, BLOCK), qkv, shared_h[:, 0 : 3 * FEATURES], xw, image_grad, gain, norm_sums)
 
-    grad_rows(0)
-    first(7)
-    grad_rows(1)
-    second(6)
-    third(4)
-    grad_rows(2)
-    fourth(3)
-    second(7)
-    grad_rows(3)
-    spread_rows(image_grad, shared_g, row, col)
-    start(1)
-    third(6)
+    def send_grad():
+        spread_rows(image_grad, shared_g, row, col)
+        start(1)
+
     def over_rows(values):
         return jnp.sum(values, axis=0, keepdims=True)
 
-    small[0] = jnp.zeros((16, FEATURES), F32)
-    lines = [bias_sums[0], bias_sums[1], sums[0], sums[1], norm_sums[0], norm_sums[1], sums[2], sums[3]]
-    for i, values in enumerate(lines):
-        small[0, i : i + 1, :] = over_rows(values)
-    for i in range(4):
-        small[0, 8 + i : 9 + i, :] = over_rows(up_sum[:, i * FEATURES : (i + 1) * FEATURES])
-    exact = lax.Precision.HIGHEST
-    total = jnp.zeros((64, 128), F32)
-    for parity in range(2):
-        for which in range(2):
-            part = table_sums[64 * parity : 64 * parity + 64, 256 * parity + 128 * which : 256 * parity + 128 * which + 128]
-            total = total + jnp.dot(part, taker[2 * parity + which], precision=exact, preferred_element_type=F32)
-    table[0] = total
+    def gather_small():
+        small[0] = jnp.zeros((16, FEATURES), F32)
+        lines = [bias_sums[0], bias_sums[1], sums[0], sums[1], norm_sums[0], norm_sums[1], sums[2], sums[3]]
+        for i, values in enumerate(lines):
+            small[0, i : i + 1, :] = over_rows(values)
+        for i in range(4):
+            small[0, 8 + i : 9 + i, :] = over_rows(up_sum[:, i * FEATURES : (i + 1) * FEATURES])
+        exact = lax.Precision.HIGHEST
+        total = jnp.zeros((64, 128), F32)
+        for parity in range(2):
+            for which in range(2):
+                part = table_sums[64 * parity : 64 * parity + 64, 256 * parity + 128 * which : 256 * parity + 128 * which + 128]
+                total = total + jnp.dot(part, taker[2 * parity + which], precision=exact, preferred_element_type=F32)
+        table[0] = total
+
     hops = ({"row": core_row}, {"row": y_row}, {"img": other})
 
     def small_push(k, src, dst, target):
@@ -1278,6 +1251,8 @@
         return c
 
     def small_step(i):
+        if i == 0:
+            gather_small()
         if 0 < i <= 3:
             for k, (acc, land) in enumerate(((small, small_land), (table, table_land))):
                 pltpu.make_async_copy(land.at[i - 1], land.at[i - 1], srecv.at[2 * (i - 1) + k]).wait()
@@ -1300,20 +1275,52 @@
             small_out[...] = (small_z[0] + small_z[1]) + (small_z[2] + small_z[3])
             table_out[...] = (table_z[0] + table_z[1]) + (table_z[2] + table_z[3])
 
-    small_step(0)
-    third(7)
-    fourth(4)
-    small_step(1)
-    fourth(5)
-    small_step(2)
+    acts = {"p": pair_stage, "1": first, "2": second, "3": third, "4": fourth, "G": grad_rows, "s": small_step, "S": send_grad}
+    slots = plan_slots(CLOSE_PLAN, acts)
+    run_all(slots[0])
+
+    def head_pair(k, _):
+        pair_index = lax.rem(k, 2) * 3 + k // 2
+
+        def each(window, _):
+            for i, slot_acts in enumerate(slots[1:-1]):
+                if slot_acts:
+                    pl.when((k == (i + 1) // 3) & (window == (i + 1) % 3))(functools.partial(run_all, slot_acts))
+            turn_count = k * windows + window
+            slot = lax.rem(turn_count, 2)
+            fetch(k, window, slot).wait()
+            wrap = window + 1 == windows
+            next_k = jnp.where(wrap, k + 1, k)
+
+            @pl.when(next_k < 6)
+            def _():
+                fetch(next_k, jnp.where(wrap, 0, window + 1), 1 - slot).start()
+
+            attention_back(
+                window,
+                pair_index,
+                lambda parity: probs_s[slot, parity],
+                do,
+                qkv,
+                o,
+                tab,
+                row_bias,
+                bias_sums,
+                table_sums,
+                row,
+                col,
+            )
+            return 0
+
+        lax.fori_loop(0, windows, each, 0)
+        return 0
+
+    lax.fori_loop(0, 6, head_pair, 0)
+    run_all(slots[-1])
     arrived(0)
     load(5).wait()
     load(6).wait()
     merge_tiles([lambda image, upper: own_r[image, upper]], landing[:1], (out,), row, col)
-    small_step(3)
-    fourth(6)
-    fourth(7)
-    small_step(4)
     arrived(1)
     merge_tiles([lambda image, upper: shared_g[image * 22 + 8 + upper, 1:3]], landing[1:], (grad_out,), row, col)
     left(0)
@@ -1324,7 +1331,7 @@
         copy().wait_send()
 
 
-def back(do, o, tab, bias, o_turned, da, n2_turned, cw, xw, n1_turned, gain, sums, up_sum, probs, qkv, dh, g, dm, wq, raw_r):
+def back(do, o, value_bias, rows_table, cols_table, o_turned, da, n2_turned, cw, xw, n1_turned, gain, sums, up_sum, probs, qkv, dh, g, dm, wq, raw_r):
     vm = pl.BlockSpec(memory_space=pltpu.VMEM)
     an = pl.BlockSpec(memory_space=pl.ANY)
     shape = jax.ShapeDtypeStruct
@@ -1333,10 +1340,10 @@
     count = len(SUM_CHUNKS)
     return pl.pallas_call(
         back_kernel,
-        out_shape=[shape((2, 16, 16, FEATURES), BF), shape((2, 16, 16, FEATURES), F32)]
+        out_shape=[shape((2, 16, 16, FEATURES), BF), shape((2, 16, 16, FEATURES), BF)]
         + [shape((k // 16, n // 2), F32) for k, n in WHOLES]
         + [shape((16, FEATURES), F32), shape((64, 128), F32)],
-        in_specs=[vm] * 14 + [an] * 7,
+        in_specs=[vm] * 16 + [an] * 7,
         out_specs=[vm] * 8,
         scratch_shapes=[
             pltpu.VMEM((SPAN, 3 * FEATURES), BF),
@@ -1348,6 +1355,8 @@
             pltpu.VMEM((2, 8, FEATURES), F32),
             pltpu.VMEM((128, 512), F32),
             pltpu.VMEM((2, 8, FEATURES), F32),
+            pltpu.VMEM((128, 512), BF),
+            pltpu.VMEM((1, FEATURES), F32),
         ]
         + pieces
         + pieces
@@ -1364,9 +1373,39 @@
         + [dma((2, 4, 3)), dma((2, 2, 3)), dma((7,)), dma((2,)), dma((count, 13)), dma((count, 13)), dma((12,)), dma((12,))],
         compiler_params=pltpu.CompilerParams(collective_id=1, has_side_effects=True, vmem_limit_bytes=67043328),
     )(
-        do, o, tab, bias, o_turned, da, n2_turned, cw, xw, n1_turned, gain, sums, up_sum, jnp.asarray(table_taker()),
+        do, o, value_bias, rows_table, cols_table, takers(True), o_turned, da, n2_turned, cw, xw, n1_turned, gain, sums, up_sum, jnp.asarray(table_taker()),
         probs, qkv, dh, g.reshape(128, 3, 8, FEATURES), dm, wq, raw_r,
     )
+
+
+def deliver_kernel(out_in, grad_in, *refs):
+    sums_in, (small, table), outs = refs[:4], refs[4:6], refs[6:]
+    outs[0][...] = out_in[...]
+
+    def widen(i, _):
+        outs[1][i // 16, i % 16] = grad_in[i // 16, i % 16].astype(F32)
+        return 0
+
+    lax.fori_loop(0, 32, widen, 0)
+    for given, goal in zip(sums_in, outs[2:6]):
+        goal[...] = given[...]
+    for i, goal in zip((0, 1, 2, None, 3, 4, 5, 6, 7), outs[6:15]):
+        if i is None:
+            goal[...] = jnp.concatenate([small[8 + j : 9 + j, :] for j in range(4)], axis=1).reshape(4 * FEATURES)
+        else:
+            goal[...] = small[i : i + 1, :].reshape(FEATURES)
+    turned = table[...].T
+    outs[15][...] = turned[0:27, :]
+    outs[16][...] = turned[64:91, :]
+
+
+def deliver(*given):
+    vm = pl.BlockSpec(memory_space=pltpu.VMEM)
+    shape = jax.ShapeDtypeStruct
+    lengths = [FEATURES] * 3 + [4 * FEATURES] + [FEATURES] * 5
+    outs = [shape((2, 16, 16, FEATURES), BF), shape((2, 16, 16, FEATURES), F32)] + [shape((k // 16, n // 2), F32) for k, n in WHOLES]
+    outs += [shape((n,), F32) for n in lengths] + [shape((27, 64), F32)] * 2
+    return pl.pallas_call(deliver_kernel, out_shape=outs, in_specs=[vm] * 8, out_specs=[vm] * len(outs))(*given)
 
 
 def on_device(
@@ -1389,32 +1428,23 @@
     cols_table,
 ):
     line = lambda v: v.reshape(1, -1)
-    bias_all = line(jnp.concatenate([query_bias, jnp.zeros_like(query_bias), value_bias]))
-    tab = table_operand(rows_table, cols_table, False)
-    tab_back = table_operand(rows_table, cols_table, True)
     xw, cw, n1_turned, qkv, probs, o, o_turned, wq, wo, wu, wd = open_windows(
-        image_in, cotangent, (qkv_weight, out_weight, up_weight, down_weight), line(first_gain), line(first_shift), bias_all, tab
+        image_in, cotangent, (qkv_weight, out_weight, up_weight, down_weight), first_gain, first_shift, query_bias, value_bias, rows_table, cols_table
     )
     raw_r, n2_turned, g_turned, dh, da, do, dm, sums, up_sum = middle(
-        o, xw, cw, wo, wu, wd, line(out_bias), line(up_bias), line(down_bias), line(second_gain), line(second_shift)
+        o, xw, cw, wo, wu, wd, out_bias, line(up_bias), down_bias, second_gain, second_shift
     )
     if lax.axis_size("img") == 2:
-        *large, small, table = back(
-            do, o, tab_back, bias_all, o_turned, da, n2_turned, cw, xw, n1_turned, line(first_gain), sums, up_sum,
-            probs, qkv, dh, g_turned, dm, wq, raw_r,
+        return tuple(
+            deliver(
+                *back(
+                    do, o, value_bias, rows_table, cols_table, o_turned, da, n2_turned, cw, xw, n1_turned, first_gain, sums, up_sum,
+                    probs, qkv, dh, g_turned, dm, wq, raw_r,
+                )
+            )
         )
-        return (
-            *large,
-            small[0],
-            small[1],
-            small[2],
-            small[8:12].reshape(-1),
-            *(small[i] for i in range(3, 8)),
-            table[:, :27].T,
-            table[:, 64:91].T,
-        )
-    dqkv, bias_sums, table_sums = plain_back(do, probs, qkv, o, tab_back, bias_all)
-    image_out, image_grad, norm_sums = plain_close(dqkv, xw, dm, raw_r, wq, line(first_gain))
+    dqkv, bias_sums, table_sums = plain_back(do, probs, qkv, o, value_bias, rows_table, cols_table)
+    image_out, image_grad, norm_sums = plain_close(dqkv, xw, dm, raw_r, wq, first_gain)
     dot = lambda a, b: jnp.dot(a, b, preferred_element_type=F32)
     totals = (dot(n1_turned, dqkv[:ROWS]), dot(o_turned, da), dot(n2_turned, dh), dot(g_turned[:, :ROWS], cw))
     shard_sums = []

time: 289 us -> 252 us (0.87); the launches traced: 284 us -> 252 us
  local copies, waits for them, and re-layouts: 19.6 us -> 0 us
  Pallas kernels: 257 us -> 251 us
  matrix products: 4.42 us -> 0 us
    reshape x8 -> x0, local copies, waits for them, and re-layouts: 8.82 us -> none  [the longest x7 8.21 us: on_device(): line = lambda v: v.reshape(1, -1)]
    unnamed x30 -> x0, local copies, waits for them, and re-layouts: 7.38 us -> none
    pallas_call x1, Pallas kernels: 108 us -> 101 us  [open_windows(): pl.pallas_call(functools.partial(open_kernel, weights), out_shape=[shape(...]
    dot_general x8 -> x0, matrix products: 4.42 us -> none  [table_operand(): lax.dot_general(table, take[parity, which], (((0,), (0,)), ((), ())), pre...]
    pallas_call x0 -> x1, Pallas kernels: none -> 3.87 us  [deliver(): pl.pallas_call(deliver_kernel, out_shape=outs, in_specs=[vm] * 8, out_spe...]
    pallas_call x1, Pallas kernels: 113 us -> 110 us  [back(): pl.pallas_call(back_kernel, out_shape=[shape((2, 16, 16, FEATURES), BF),...]
where the time goes in v3:
time: 252 us
  Pallas kernels  251 us (100%)
    pallas_call x1, Pallas kernels, back(): pl.pallas_call(back_kernel, out_shape=[shape((2, 16, 16, FEATURES), BF),...  110 us
    pallas_call x1, Pallas kernels, open_windows(): pl.pallas_call(functools.partial(open_kernel, weights), out_shape=[shape(...  101 us
    pallas_call x1, Pallas kernels, middle(): pl.pallas_call(middle_kernel, grid=(FF // CHUNK,), out_shape=[shape((88,...  36.2 us

profile of v3, /device:TPU:0, one launch (start us, length us, event | category | flops | bytes accessed | tf_op | source)
XLA Modules:
  0.0 251.6 jit_solution(16946132579389820280)
XLA Ops:
  0.7 101.0 %shard_map.323 = (bf16[704,768]{1,0:T(8,128)(2,1)}, bf16[704,768]{1,0:T(8,128)(2,1)}, bf16[768,704]{1,0:T(8,128)(2,1)}, bf16[800,2304]{1,0:T(8,128)(2,1)}, bf16[...) custom-call(bf16[2,16,2,8,768]{4,3,2,1,0:T(8,128)(2,1)} %bitcast.5, ...), custom_call_target="tpu_custom_call" | custom-call | tf_op jit(solution)/shard_map/pallas_call | solution.py:530
  101.6 36.2 %shard_map.324 = (bf16[88,3,8,768]{3,2,1,0:T(8,128)(2,1)}, bf16[768,704]{1,0:T(8,128)(2,1)}, bf16[3072,768]{1,0:T(8,128)(2,1)}, bf16[704,3072]{1,0:T(8,128)(2,1)...) custom-call(bf16[800,768]{1,0:T(8,128)(2,1)} %get-tuple-element.45.o, ...), custom_call_target="tpu_custom_call" | custom-call | tf_op jit(solution)/shard_map/pallas_call | solution.py:676
  137.9 109.6 %shard_map.325 = (bf16[2,16,16,768]{3,2,1,0:T(8,128)(2,1)}, bf16[2,16,16,768]{3,2,1,0:T(8,128)(2,1)}, f32[48,1152]{1,0:T(8,128)}, f32[48,384]{1,0:T(8,128)}, f32...) custom-call(bf16[800,768]{1,0:T(8,128)(2,1)} %get-tuple-element.51.do, ...), custom_call_target="tpu_custom_call" | custom-call | tf_op jit(solution)/shard_map/pallas_call | solution.py:1341
  247.5 3.9 %shard_map.326 = (bf16[2,16,16,768]{3,2,1,0:T(8,128)(2,1)}, f32[2,16,16,768]{3,2,1,0:T(8,128)}, f32[48,1152]{1,0:T(8,128)}, f32[48,384]{1,0:T(8,128)}, f32[48,15...) custom-call(bf16[2,16,16,768]{3,2,1,0:T(8,128)(2,1)} %get-tuple-elem, ...), custom_call_target="tpu_custom_call" | custom-call | tf_op jit(solution)/shard_map/pallas_call | solution.py:1408

commit v4 on v3

--- a/solution.py
+++ b/solution.py
@@ -116,10 +116,10 @@
 
     def push(n, k, where, target, start=None):
         def copy():
-            ref = block(n, *where)
+            ref = slot(n, where) if start else block(n, *where)
             return pltpu.make_async_remote_copy(
-                src_ref=source(n) if start else ref,
-                dst_ref=slot(n, col) if start else ref,
+                src_ref=source(n) if start and where is col else ref,
+                dst_ref=ref,
                 send_sem=wsend.at[n, k],
                 recv_sem=wrecv.at[n, k],
                 device_id=target(),
@@ -132,15 +132,21 @@
     def arrive(n, k, ref):
         pltpu.make_async_copy(ref, ref, wrecv.at[n, k]).wait()
 
+    far_col, near_col = lax.rem(col + 2, 4), col + 1 - 2 * lax.rem(col, 2)
+
     def along_col(n):
         pltpu.make_async_copy(source(n), slot(n, col), wloc.at[n]).start()
-        for d in range(1, 4):
-            push(n, d - 1, (row, img), lambda d=d: {"col": lax.rem(col + d, 4)}, True)
+        push(n, 0, col, lambda: {"col": far_col}, True)
+
+    def near_by(n):
+        pltpu.make_async_copy(source(n), slot(n, col), wloc.at[n]).wait()
+        push(n, 1, col, lambda: {"col": near_col}, True)
+        arrive(n, 0, slot(n, far_col))
+        push(n, 2, far_col, lambda: {"col": near_col}, True)
 
     def first(n):
-        pltpu.make_async_copy(source(n), slot(n, col), wloc.at[n]).wait()
-        for d in range(1, 4):
-            arrive(n, d - 1, slot(n, lax.rem(col + 4 - d, 4)))
+        arrive(n, 1, slot(n, near_col))
+        arrive(n, 2, slot(n, 3 - col))
         push(n, 3, (row, img, 0), lambda: {"img": other})
         push(n, 4, (row, img, 1), lambda: {"row": y_row})
         push(n, 5, (row, img), lambda: {"row": core_row})
@@ -175,7 +181,7 @@
         arrive(n, 14, block(n, core_row, other, 1))
         arrive(n, 15, block(n, core_y, other, 1))
 
-    return along_col, first, second, third, last, sent
+    return along_col, near_by, first, second, third, last, sent
 
 
 def window_moves(tiles, raws, send, recv, loc):
@@ -340,25 +346,65 @@
     return grads
 
 
-OPEN_PLAN = ("a0", "a1", "11", "a5", "a3", "10", "21", "20", "a6", "15", "13", "31", "25", "Wx", "30", "L0", "16", "23", "35", "a4", "X", "26", "L1", "P", "|", "|", "a2", "|", "|", "14", "|", "|", "|", "12", "|", "Wc", "L5", "|", "36", "|", "|", "|", "24", "|", "|", "L6", "|", "|", "33", "|", "|", "22", "T", "34", "32", "K", "L2", "L3", "L4")
-
-
-def open_kernel(weights, x_ref, c_ref, gain, shift, query_bias, value_bias, rows_table, cols_table, take, *refs):
+FF = 3072
+CHUNK = 512
+BLOCK = 176
+
+
+def nt(a, b):
+    return lax.dot_general(a, b, (((1,), (1,)), ((), ())), preferred_element_type=F32)
+
+
+def norm_back(grad, unit, inverse, gain):
+    scaled = grad * gain
+    first_mean = jnp.mean(scaled, axis=-1, keepdims=True)
+    second_mean = jnp.mean(scaled * unit, axis=-1, keepdims=True)
+    return inverse * (scaled - first_mean - unit * second_mean)
+
+
+def fold_rows(values):
+    total = values[0:8]
+    for i in range(1, values.shape[0] // 8):
+        total = total + values[8 * i : 8 * i + 8]
+    return total
+
+
+def spread_rows(source, raw, row, col):
+    def step(i, _):
+        slot, raw_row, col_start, width = row_params(i, row, col)
+        at = pl.ds(pl.multiple_of(i * 16, 16), 16)
+
+        @pl.when(width > 0)
+        def _():
+            values = jnp.concatenate([source[at, :], jnp.zeros((8, FEATURES), F32)], axis=0)
+            raw[slot * 22 + raw_row] = pltpu.roll(values, col_start, 0).astype(BF).reshape(3, 8, FEATURES)
+
+        return 0
+
+    lax.fori_loop(0, 44, step, 0)
+
+
+OPEN_PLAN = ("a2", "a1", "a0", "a5", "b2", "b1", "a3", "12", "b0", "Wx", "11", "10", "21", "22", "b5", "20", "32", "b3", "a6", "31", "15", "13", "30", "b6", "a4", "25", "X", "L1", "Wc", "L2", "L0", "P", "|", "|", "|", "16", "35", "|", "|", "|", "23", "|", "|", "|", "|", "|", "b4", "26", "|", "|", "|", "|", "|", "|", "33", "|", "14", "L5", "T", "M", "36", "K", "24", "L6", "L3", "|", "34", "|", "L4", "|", "|")
+
+
+def open_kernel(weights, x_ref, c_ref, gain, shift, query_bias, value_bias, rows_table, cols_table, take, out_bias, up_bias, down_bias, gain2, shift2, *refs):
     img, row, col = place()
     greet(img, row, col, weights)
     if weights:
         shards, refs = refs[:4], refs[4:]
     else:
-        wq, refs = refs[0], refs[1:]
+        wq, wo, wu, wd = refs[:4]
+        refs = refs[4:]
     xw, cw, n1_turned, qkv_out, probs_out, o, o_turned = refs[:7]
-    refs = refs[7:]
+    raw_out, n2_turned, g_out, dh_out, da, do, dm, sums, up_sum = refs[7:16]
+    refs = refs[16:]
     if weights:
-        fulls, refs = refs[:4], refs[4:]
-    rawx, rawc, n1, tab, row_bias, qkv_s, probs, out_sem, probs_sem, send, recv, loc = refs[:12]
-    refs = refs[12:]
+        wq_out, refs = refs[0], refs[1:]
+    rawx, rawc, n1, tab, row_bias, qkv_s, probs, y_s, d_s, g_s, g_chunk, dh_chunk, out_sem, probs_sem, send, recv, loc = refs[:17]
+    refs = refs[17:]
     if weights:
-        wq, wq_out = refs[0], fulls[0]
-        along_col, first, second, third, last, sent = links(shards, (wq, *fulls[1:]), *refs[1:])
+        wq, wo, wu, wd = refs[:4]
+        along_col, near_by, first, second, third, last, sent = links(shards, refs[:4], *refs[4:])
     window_start, window_arrived, window_left = window_moves((x_ref, c_ref), (rawx, rawc), send, recv, loc)
     places = lax.broadcasted_iota(jnp.int32, (16, 1), 0)
 
@@ -418,14 +464,92 @@
         turn(n1, n1_turned)
         turn(o, o_turned)
 
-    acts = {"X": cut_windows, "P": project_all, "T": turn_all, "K": cut_cotangent}
+    blocks = (slice(0, 352), slice(352, 704))
+
+    def middle_begin():
+        sums[...] = jnp.zeros_like(sums)
+        up_sum[...] = jnp.zeros_like(up_sum)
+        d_s[...] = jnp.zeros_like(d_s)
+
+        def begin(i, _):
+            at = pl.ds(pl.multiple_of(i * BLOCK, 16), BLOCK)
+            mid = xw[at, :].astype(F32) + (jnp.dot(o[at, :], wo[...], preferred_element_type=F32) + as_row(out_bias))
+            unit, _inverse = unit_of(mid)
+            n1[at, :] = (unit * as_row(gain2) + as_row(shift2)).astype(BF)
+            y_s[at, :] = mid + as_row(down_bias)
+            dm[at, :] = mid
+            return 0
+
+        lax.fori_loop(0, ROWS // BLOCK, begin, 0)
+        turn(n1, n2_turned)
+
+    def chunk_out(which, step):
+        lanes = pl.ds(pl.multiple_of(step * FEATURES, FEATURES), FEATURES)
+        if which == 0:
+            return pltpu.make_async_copy(g_chunk, g_out.at[lanes, :], out_sem.at[2])
+        return pltpu.make_async_copy(dh_chunk, dh_out.at[:, lanes], out_sem.at[3])
+
+    def middle_step(turn_index, _):
+        for i, slot_acts in enumerate(middle_slots):
+            if slot_acts:
+                pl.when(turn_index == i)(functools.partial(run_all, slot_acts))
+        step = lax.rem(turn_index, 2) * 2 + turn_index // 2
+        lanes = pl.ds(pl.multiple_of(step * FEATURES, FEATURES), FEATURES)
+
+        @pl.when(turn_index > 0)
+        def _():
+            chunk_out(0, 0).wait()
+            chunk_out(1, 0).wait()
+
+        for at in blocks:
+            h = jnp.dot(n1[at, :], wu[:, lanes], preferred_element_type=F32) + up_bias[:, lanes]
+            up = nt(cw[at, :], wd[lanes, :])
+            phi = 0.5 * (1.0 + lax.erf(h * 0.7071067811865476))
+            slope = phi + h * (jnp.exp(-0.5 * h * h) * 0.3989422804014327)
+            active = (h * phi).astype(BF)
+            back = (up * slope).astype(BF)
+            g_s[at, :] = active
+            dh_chunk[at, :] = back
+            up_sum[:, lanes] += fold_rows(back.astype(F32))
+            y_s[at, :] += jnp.dot(active, wd[lanes, :], preferred_element_type=F32)
+            d_s[at, :] += nt(back, wu[:, lanes])
+        for i in range(FEATURES // 128):
+            g_chunk[128 * i : 128 * i + 128, 0:ROWS] = g_s[:, 128 * i : 128 * i + 128].T
+        chunk_out(0, step).start()
+        chunk_out(1, step).start()
+        return 0
+
+    def middle_end():
+        def end(i, _):
+            at = pl.ds(pl.multiple_of(i * BLOCK, 16), BLOCK)
+            unit, inverse = unit_of(dm[at, :])
+            grad = d_s[at, :].astype(BF).astype(F32)
+            up = cw[at, :].astype(F32)
+            grad_mid = up + norm_back(grad, unit, inverse, as_row(gain2))
+            low_grad = grad_mid.astype(BF)
+            dm[at, :] = grad_mid
+            da[at, :] = low_grad
+            do[at, :] = nt(low_grad, wo[...]).astype(BF)
+            sums[0] += fold_rows(low_grad.astype(F32))
+            sums[1] += fold_rows(up)
+            sums[2] += fold_rows(grad * unit)
+            sums[3] += fold_rows(grad)
+            return 0
+
+        spread_rows(y_s, rawx, row, col)
+        raw_copy = pltpu.make_async_copy(rawx, raw_out, out_sem.at[4])
+        raw_copy.start()
+        lax.fori_loop(0, ROWS // BLOCK, end, 0)
+        raw_copy.wait()
+
+    acts = {"X": cut_windows, "P": project_all, "T": turn_all, "K": cut_cotangent, "M": middle_begin}
     acts["Wx"] = functools.partial(window_start, 0)
     acts["Wc"] = functools.partial(window_start, 1)
     if weights:
-        acts.update({"a": along_col, "1": first, "2": second, "3": third, "L": last})
+        acts.update({"a": along_col, "b": near_by, "1": first, "2": second, "3": third, "L": last})
         slots = plan_slots(OPEN_PLAN, acts)
     else:
-        slots = plan_slots(("Wx", "Wc", "X", "P", *("|",) * 18, "T", "K"), acts)
+        slots = plan_slots(("Wx", "Wc", "X", "P", *("|",) * 18, "T", "K", "M", *("|",) * 4), acts)
     o[...] = jnp.zeros_like(o)
     build_table(tab, rows_table, cols_table, take)
     row_bias[0] = as_row(query_bias)
@@ -443,7 +567,7 @@
         return pltpu.make_async_copy(probs.at[window, part], probs_out.at[window, part], probs_sem.at[window, pair_index])
 
     def pair(index, _):
-        for i, slot_acts in enumerate(slots[1:-1]):
+        for i, slot_acts in enumerate(slots[1:18]):
             if slot_acts:
                 pl.when(index == i + 1)(functools.partial(run_all, slot_acts))
         window, pair_index = index // 6, index % 6
@@ -502,7 +626,13 @@
 
     pairs = window_count(row, col) * 6
     lax.fori_loop(0, pairs, pair, 0)
-    run_all(slots[-1])
+    run_all(slots[18])
+    middle_slots = [[], *slots[19:22]]
+    lax.fori_loop(0, 4, middle_step, 0)
+    run_all(slots[22])
+    middle_end()
+    chunk_out(0, 0).wait()
+    chunk_out(1, 0).wait()
     pltpu.make_async_copy(qkv_s, qkv_out, out_sem.at[0]).wait()
     if weights:
         pltpu.make_async_copy(wq, wq_out, out_sem.at[1]).wait()
@@ -513,7 +643,7 @@
     window_left(1)
 
 
-def open_windows(x, c, shards, gain, shift, query_bias, value_bias, rows_table, cols_table):
+def open_windows(x, c, shards, gain, shift, query_bias, value_bias, rows_table, cols_table, out_bias, up_bias, down_bias, gain2, shift2):
     vm = pl.BlockSpec(memory_space=pltpu.VMEM)
     an = pl.BlockSpec(memory_space=pl.ANY)
     shape = jax.ShapeDtypeStruct
@@ -521,11 +651,11 @@
     chunks = len(CHUNKS)
     weights = lax.axis_size("img") == 2
     if weights:
-        given, wholes = list(shards), [(768, 2304), (768, 768), (768, 3072), (3072, 768)]
+        given = list(shards)
     else:
         widened = [lax.all_gather(w, "img", axis=1, tiled=True) for w in shards]
         gathered = [lax.all_gather(w, ("row", "col"), axis=0, tiled=True) for w in widened]
-        given, wholes = gathered[:1], []
+        given = gathered
     raw = pltpu.VMEM((88, 3, 8, FEATURES), BF)
     outs = pl.pallas_call(
         functools.partial(open_kernel, weights),
@@ -538,145 +668,7 @@
             shape((SPAN, FEATURES), BF),
             shape((FEATURES, ROWS), BF),
         ]
-        + [shape(s, BF) for s in wholes],
-        in_specs=[vm] * (9 + len(given)),
-        out_specs=[vm, vm, vm, an, an, vm, vm] + [an] * len(wholes),
-        scratch_shapes=[
-            raw,
-            raw,
-            pltpu.VMEM((ROWS, FEATURES), BF),
-            pltpu.VMEM((128, 512), BF),
-            pltpu.VMEM((2, 1, FEATURES), F32),
-            pltpu.VMEM((SPAN, 3 * FEATURES), BF),
-            pltpu.VMEM((4, 12, 224, 224), BF),
-            dma((2,)),
-            dma((4, 6)),
-            dma((2, 2, 3)),
-            dma((2, 4, 3)),
-            dma((2, 2)),
-        ]
-        + ([pltpu.VMEM((768, 2304), BF), dma((chunks, 16)), dma((chunks, 16)), dma((chunks,))] if weights else []),
-        compiler_params=pltpu.CompilerParams(collective_id=0, has_side_effects=True, vmem_limit_bytes=67043328),
-    )(x.reshape(2, 16, 2, 8, 768), c.reshape(2, 16, 2, 8, 768), gain, shift, query_bias, value_bias, rows_table, cols_table, takers(False), *given)
-    return list(outs) if weights else list(outs) + gathered
-
-
-FF = 3072
-CHUNK = 512
-BLOCK = 176
-
-
-def nt(a, b):
-    return lax.dot_general(a, b, (((1,), (1,)), ((), ())), preferred_element_type=F32)
-
-
-def norm_back(grad, unit, inverse, gain):
-    scaled = grad * gain
-    first_mean = jnp.mean(scaled, axis=-1, keepdims=True)
-    second_mean = jnp.mean(scaled * unit, axis=-1, keepdims=True)
-    return inverse * (scaled - first_mean - unit * second_mean)
-
-
-def fold_rows(values):
-    total = values[0:8]
-    for i in range(1, values.shape[0] // 8):
-        total = total + values[8 * i : 8 * i + 8]
-    return total
-
-
-def spread_rows(source, raw, row, col):
-    def step(i, _):
-        slot, raw_row, col_start, width = row_params(i, row, col)
-        at = pl.ds(pl.multiple_of(i * 16, 16), 16)
-
-        @pl.when(width > 0)
-        def _():
-            values = jnp.concatenate([source[at, :], jnp.zeros((8, FEATURES), F32)], axis=0)
-            raw[slot * 22 + raw_row] = pltpu.roll(values, col_start, 0).astype(BF).reshape(3, 8, FEATURES)
-
-        return 0
-
-    lax.fori_loop(0, 44, step, 0)
-
-
-def middle_kernel(
-    o, xw, cw, wo, wu, wd, out_bias, up_bias, down_bias, gain, shift, raw_r, n2_turned, g_turned, dh, da, do, dm, sums, up_sum, n2, y_s, d_s, g_s
-):
-    step = pl.program_id(0)
-    row, col = lax.axis_index("row"), lax.axis_index("col")
-    blocks = [slice(i * BLOCK, (i + 1) * BLOCK) for i in range(ROWS // BLOCK)]
-
-    def mid_of(at):
-        return xw[at, :].astype(F32) + (jnp.dot(o[at, :], wo[...], preferred_element_type=F32) + as_row(out_bias))
-
-    @pl.when(step == 0)
-    def _():
-        sums[...] = jnp.zeros_like(sums)
-        d_s[...] = jnp.zeros_like(d_s)
-
-        def begin(i, _):
-            at = pl.ds(pl.multiple_of(i * BLOCK, 16), BLOCK)
-            mid = mid_of(at)
-            unit, _inverse = unit_of(mid)
-            n2[at, :] = (unit * as_row(gain) + as_row(shift)).astype(BF)
-            y_s[at, :] = mid + as_row(down_bias)
-            dm[at, :] = mid
-            return 0
-
-        lax.fori_loop(0, ROWS // BLOCK, begin, 0)
-
-        def turn(i, _):
-            lanes = pl.ds(pl.multiple_of(i * 128, 128), 128)
-            n2_turned[lanes, :] = n2[:, lanes].T
-            return 0
-
-        lax.fori_loop(0, FEATURES // 128, turn, 0)
-
-    up_sum[...] = jnp.zeros_like(up_sum)
-    for at in blocks:
-        h = jnp.dot(n2[at, :], wu[...], preferred_element_type=F32) + up_bias[...]
-        up = nt(cw[at, :], wd[...])
-        phi = 0.5 * (1.0 + lax.erf(h * 0.7071067811865476))
-        slope = phi + h * (jnp.exp(-0.5 * h * h) * 0.3989422804014327)
-        active = (h * phi).astype(BF)
-        back = (up * slope).astype(BF)
-        g_s[at, :] = active
-        dh[at, :] = back
-        up_sum[...] += fold_rows(back.astype(F32))
-        y_s[at, :] += jnp.dot(active, wd[...], preferred_element_type=F32)
-        d_s[at, :] += nt(back, wu[...])
-    for i in range(CHUNK // 128):
-        g_turned[128 * i : 128 * i + 128, 0:ROWS] = g_s[:, 128 * i : 128 * i + 128].T
-
-    @pl.when(step == FF // CHUNK - 1)
-    def _():
-        def end(i, _):
-            at = pl.ds(pl.multiple_of(i * BLOCK, 16), BLOCK)
-            unit, inverse = unit_of(dm[at, :])
-            grad = d_s[at, :].astype(BF).astype(F32)
-            up = cw[at, :].astype(F32)
-            grad_mid = up + norm_back(grad, unit, inverse, as_row(gain))
-            low_grad = grad_mid.astype(BF)
-            dm[at, :] = grad_mid
-            da[at, :] = low_grad
-            do[at, :] = nt(low_grad, wo[...]).astype(BF)
-            sums[0] += fold_rows(low_grad.astype(F32))
-            sums[1] += fold_rows(up)
-            sums[2] += fold_rows(grad * unit)
-            sums[3] += fold_rows(grad)
-            return 0
-
-        lax.fori_loop(0, ROWS // BLOCK, end, 0)
-        spread_rows(y_s, raw_r, row, col)
-
-
-def middle(o, xw, cw, wo, wu, wd, out_bias, up_bias, down_bias, gain, shift):
-    shape = jax.ShapeDtypeStruct
-    once = lambda *s: pl.BlockSpec(s, lambda i: (0,) * len(s), pipeline_mode=pl.Buffered(1))
-    return pl.pallas_call(
-        middle_kernel,
-        grid=(FF // CHUNK,),
-        out_shape=[
+        + [
             shape((88, 3, 8, FEATURES), BF),
             shape((FEATURES, ROWS), BF),
             shape((FF, FEATURES), BF),
@@ -686,39 +678,33 @@
             shape((ROWS, FEATURES), F32),
             shape((4, 8, FEATURES), F32),
             shape((8, FF), F32),
-        ],
-        in_specs=[
-            once(SPAN, FEATURES),
-            once(ROWS, FEATURES),
-            once(ROWS, FEATURES),
-            once(FEATURES, FEATURES),
-            pl.BlockSpec((FEATURES, CHUNK), lambda i: (0, i)),
-            pl.BlockSpec((CHUNK, FEATURES), lambda i: (i, 0)),
-            once(FEATURES),
-            pl.BlockSpec((1, CHUNK), lambda i: (0, i)),
-            once(FEATURES),
-            once(FEATURES),
-            once(FEATURES),
-        ],
-        out_specs=[
-            once(88, 3, 8, FEATURES),
-            once(FEATURES, ROWS),
-            pl.BlockSpec((CHUNK, FEATURES), lambda i: (i, 0)),
-            pl.BlockSpec((ROWS, CHUNK), lambda i: (0, i)),
-            once(ROWS, FEATURES),
-            once(SPAN, FEATURES),
-            once(ROWS, FEATURES),
-            once(4, 8, FEATURES),
-            pl.BlockSpec((8, CHUNK), lambda i: (0, i)),
-        ],
+        ]
+        + ([shape((768, 2304), BF)] if weights else []),
+        in_specs=[vm] * (14 + len(given)),
+        out_specs=[vm, vm, vm, an, an, vm, vm, an, vm, an, an, vm, vm, vm, vm, vm] + ([an] if weights else []),
         scratch_shapes=[
+            raw,
+            raw,
             pltpu.VMEM((ROWS, FEATURES), BF),
+            pltpu.VMEM((128, 512), BF),
+            pltpu.VMEM((2, 1, FEATURES), F32),
+            pltpu.VMEM((SPAN, 3 * FEATURES), BF),
+            pltpu.VMEM((4, 12, 224, 224), BF),
             pltpu.VMEM((ROWS, FEATURES), F32),
             pltpu.VMEM((ROWS, FEATURES), F32),
-            pltpu.VMEM((ROWS, CHUNK), BF),
-        ],
-        compiler_params=pltpu.CompilerParams(vmem_limit_bytes=62 << 20),
-    )(o, xw, cw, wo, wu, wd, out_bias, up_bias, down_bias, gain, shift)
+            pltpu.VMEM((ROWS, FEATURES), BF),
+            pltpu.VMEM((FEATURES, FEATURES), BF),
+            pltpu.VMEM((ROWS, FEATURES), BF),
+            dma((5,)),
+            dma((4, 6)),
+            dma((2, 2, 3)),
+            dma((2, 4, 3)),
+            dma((2, 2)),
+        ]
+        + ([pltpu.VMEM(s, BF) for s in WHOLES] + [dma((chunks, 16)), dma((chunks, 16)), dma((chunks,))] if weights else []),
+        compiler_params=pltpu.CompilerParams(collective_id=0, has_side_effects=True, vmem_limit_bytes=67043328),
+    )(x.reshape(2, 16, 2, 8, 768), c.reshape(2, 16, 2, 8, 768), gain, shift, query_bias, value_bias, rows_table, cols_table, takers(False), out_bias, up_bias, down_bias, gain2, shift2, *given)
+    return list(outs) if weights else list(outs) + gathered[:1]
 
 
 def attention_back(window, pair_index, probs_of, do, qkv, o, tab, value_bias, bias_sums, table_sums, row, col):
@@ -865,6 +851,7 @@
     core_row = row + 1 - 2 * lax.rem(row, 2)
     core_y = lax.rem(core_row + 2, 4)
     other = 1 - img
+    far_col, near_col = lax.rem(col + 2, 4), col + 1 - 2 * lax.rem(col, 2)
     lands = [land_refs[5 * n : 5 * n + 5] for n in range(len(chunks))]
     sent = []
 
@@ -952,24 +939,24 @@
         for half in range(2):
             arrive(n, 8 + half, lands[n][3].at[half])
             add(block(n, row, img, half), lands[n][3].at[half], kb // 2)
-        for d in range(1, 4):
-
-            def src(d=d):
-                return shard(n, lax.rem(col + d, 4))
-
-            push(n, 9 + d, src, lambda d=d: lands[n][4].at[d - 1], lambda d=d: {"col": lax.rem(col + d, 4)})
+        push(n, 10, lambda: shard(n, near_col), lambda: lands[n][4].at[0], lambda: {"col": near_col})
+        push(n, 11, lambda: shard(n, 3 - col), lambda: lands[n][4].at[1], lambda: {"col": near_col})
 
     def fourth(n):
+        kb = size(n)[0]
+        arrive(n, 11, lands[n][4].at[1])
+        add(shard(n, far_col), lands[n][4].at[1], kb // 4)
+        push(n, 12, lambda: shard(n, far_col), lambda: lands[n][4].at[2], lambda: {"col": far_col})
+
+    def fifth(n):
         w, lo, hi = chunks[n]
-        for d in range(1, 4):
-            arrive(n, 9 + d, lands[n][4].at[d - 1])
+        arrive(n, 10, lands[n][4].at[0])
+        arrive(n, 12, lands[n][4].at[2])
         mine = shard(n, col)
 
         def step(part, _):
             at = pl.ds(pl.multiple_of(part * 48, 16), 48)
-            total = mine[at, :].astype(F32)
-            for d in range(3):
-                total = total + lands[n][4][d, at, :].astype(F32)
+            total = mine[at, :].astype(F32) + lands[n][4][0, at, :].astype(F32) + lands[n][4][2, at, :].astype(F32)
             if w > 0:
                 grads[w][at, lo:hi] = total
             else:
@@ -985,7 +972,7 @@
 
         lax.fori_loop(0, WHOLES[w][0] // 16 // 48, step, 0)
 
-    return pair_stage, first, second, third, fourth, sent
+    return pair_stage, first, second, third, fourth, fifth, sent
 
 
 def table_taker():
@@ -1013,7 +1000,7 @@
     return table
 
 
-CLOSE_PLAN = ("p1", "|", "p0", "11", "p2", "10", "p3", "12", "|", "21", "20", "|", "|", "|", "|", "p4", "|", "13", "|", "|", "31", "22", "|", "|", "30", "p5", "|", "|", "|", "15", "|", "32", "|", "23", "|", "|", "25", "G0", "14", "33", "G1", "p7", "41", "G2", "35", "40", "17", "G3", "s0", "S", "24", "s1", "27", "37", "43", "34", "p6", "s2", "16", "42", "s3", "26", "36", "44", "46", "47", "45", "s4")
+CLOSE_PLAN = ("p1", "p2", "11", "|", "|", "12", "p4", "|", "|", "14", "21", "|", "p0", "|", "|", "p3", "|", "22", "|", "p5", "24", "|", "10", "31", "|", "|", "|", "|", "|", "|", "|", "13", "|", "32", "41", "15", "34", "G0", "G1", "G2", "42", "p7", "G3", "S", "p6", "23", "s0", "25", "20", "17", "16", "30", "s1", "44", "35", "27", "40", "52", "33", "26", "s2", "45", "37", "51", "50", "36", "s3", "43", "54", "47", "46", "53", "57", "55", "56", "s4")
 
 
 def returns(raws, landing, send, recv, row, col):
@@ -1172,7 +1159,7 @@
         )
         return pltpu.make_async_copy(pairs[i][0], pairs[i][1], load_sem.at[i])
 
-    for i in (2, 1, 0, 3, 5, 6):
+    for i in (1, 2, 0, 3, 5, 6):
         load(i).start()
     windows = window_count(row, col)
 
@@ -1191,7 +1178,7 @@
     def turned_g(rw, kb):
         return shared_g[pl.ds(pl.multiple_of(rw * 32, 32), 32)].reshape(FEATURES, FEATURES)[:, 0:ROWS]
 
-    pair_stage, first, second, third, fourth, sent = reducers(
+    pair_stage, first, second, third, fourth, fifth, sent = reducers(
         SUM_CHUNKS,
         full,
         (turned_rows(n1_turned), turned_rows(o_turned), turned_rows(n2_turned), turned_g),
@@ -1206,10 +1193,7 @@
     norm_sums[...] = jnp.zeros_like(norm_sums)
     build_table(tab, rows_table, cols_table, take)
     row_bias[...] = as_row(value_bias)
-    load(2).wait()
-    clear_idle(qkv, row, col)
     load(1).wait()
-    load(0).wait()
 
     def grad_rows(i):
         if i == 0:
@@ -1275,9 +1259,12 @@
             small_out[...] = (small_z[0] + small_z[1]) + (small_z[2] + small_z[3])
             table_out[...] = (table_z[0] + table_z[1]) + (table_z[2] + table_z[3])
 
-    acts = {"p": pair_stage, "1": first, "2": second, "3": third, "4": fourth, "G": grad_rows, "s": small_step, "S": send_grad}
+    acts = {"p": pair_stage, "1": first, "2": second, "3": third, "4": fourth, "5": fifth, "G": grad_rows, "s": small_step, "S": send_grad}
     slots = plan_slots(CLOSE_PLAN, acts)
     run_all(slots[0])
+    load(2).wait()
+    clear_idle(qkv, row, col)
+    load(0).wait()
 
     def head_pair(k, _):
         pair_index = lax.rem(k, 2) * 3 + k // 2
@@ -1428,11 +1415,21 @@
     cols_table,
 ):
     line = lambda v: v.reshape(1, -1)
-    xw, cw, n1_turned, qkv, probs, o, o_turned, wq, wo, wu, wd = open_windows(
-        image_in, cotangent, (qkv_weight, out_weight, up_weight, down_weight), first_gain, first_shift, query_bias, value_bias, rows_table, cols_table
-    )
-    raw_r, n2_turned, g_turned, dh, da, do, dm, sums, up_sum = middle(
-        o, xw, cw, wo, wu, wd, out_bias, line(up_bias), down_bias, second_gain, second_shift
+    xw, cw, n1_turned, qkv, probs, o, o_turned, raw_r, n2_turned, g_turned, dh, da, do, dm, sums, up_sum, wq = open_windows(
+        image_in,
+        cotangent,
+        (qkv_weight, out_weight, up_weight, down_weight),
+        first_gain,
+        first_shift,
+        query_bias,
+        value_bias,
+        rows_table,
+        cols_table,
+        out_bias,
+        line(up_bias),
+        down_bias,
+        second_gain,
+        second_shift,
     )
     if lax.axis_size("img") == 2:
         return tuple(

time: 252 us -> 237 us (0.940)
  Pallas kernels: 251 us -> 236 us
    pallas_call x1 -> x0, Pallas kernels: 36.2 us -> none  [middle(): pl.pallas_call(middle_kernel, grid=(FF // CHUNK,), out_shape=[shape((88,...]
    pallas_call x1, Pallas kernels: 101 us -> 122 us  [open_windows(): pl.pallas_call(functools.partial(open_kernel, weights), out_shape=[shape(...]
where the time goes in v4:
time: 237 us; the launch traced here: 236 us
  Pallas kernels  236 us (100%)
    pallas_call x1, Pallas kernels, open_windows(): pl.pallas_call(functools.partial(open_kernel, weights), out_shape=[shape(...  122 us
    pallas_call x1, Pallas kernels, back(): pl.pallas_call(back_kernel, out_shape=[shape((2, 16, 16, FEATURES), BF),...  110 us

profile of v4, /device:TPU:0, one launch (start us, length us, event | category | flops | bytes accessed | tf_op | source)
XLA Modules:
  0.0 236.4 jit_solution(13266412808572534613)
XLA Ops:
  0.7 121.9 %shard_map.323 = (bf16[704,768]{1,0:T(8,128)(2,1)}, bf16[704,768]{1,0:T(8,128)(2,1)}, bf16[768,704]{1,0:T(8,128)(2,1)}, bf16[800,2304]{1,0:T(8,128)(2,1)}, bf16[...) custom-call(bf16[2,16,2,8,768]{4,3,2,1,0:T(8,128)(2,1)} %bitcast.5, ...), custom_call_target="tpu_custom_call" | custom-call | tf_op jit(solution)/shard_map/pallas_call | solution.py:660
  122.6 109.8 %shard_map.324 = (bf16[2,16,16,768]{3,2,1,0:T(8,128)(2,1)}, bf16[2,16,16,768]{3,2,1,0:T(8,128)(2,1)}, f32[48,1152]{1,0:T(8,128)}, f32[48,384]{1,0:T(8,128)}, f32...) custom-call(bf16[800,768]{1,0:T(8,128)(2,1)} %get-tuple-element.42.do, ...), custom_call_target="tpu_custom_call" | custom-call | tf_op jit(solution)/shard_map/pallas_call | solution.py:1328
  232.4 3.9 %shard_map.325 = (bf16[2,16,16,768]{3,2,1,0:T(8,128)(2,1)}, f32[2,16,16,768]{3,2,1,0:T(8,128)}, f32[48,1152]{1,0:T(8,128)}, f32[48,384]{1,0:T(8,128)}, f32[48,15...) custom-call(bf16[2,16,16,768]{3,2,1,0:T(8,128)(2,1)} %get-tuple-elem, ...), custom_call_target="tpu_custom_call" | custom-call | tf_op jit(solution)/shard_map/pallas_call | solution.py:1395

commit v5 on v4

--- a/solution.py
+++ b/solution.py
@@ -384,7 +384,7 @@
     lax.fori_loop(0, 44, step, 0)
 
 
-OPEN_PLAN = ("a2", "a1", "a0", "a5", "b2", "b1", "a3", "12", "b0", "Wx", "11", "10", "21", "22", "b5", "20", "32", "b3", "a6", "31", "15", "13", "30", "b6", "a4", "25", "X", "L1", "Wc", "L2", "L0", "P", "|", "|", "|", "16", "35", "|", "|", "|", "23", "|", "|", "|", "|", "|", "b4", "26", "|", "|", "|", "|", "|", "|", "33", "|", "14", "L5", "T", "M", "36", "K", "24", "L6", "L3", "|", "34", "|", "L4", "|", "|")
+OPEN_PLAN = ("a0", "a2", "a1", "b0", "b2", "a6", "10", "b1", "a5", "Wx", "11", "b5", "b6", "12", "20", "22", "21", "15", "a3", "X", "16", "a4", "b3", "31", "30", "25", "L1", "L0", "P", "32", "13", "b4", "26", "|", "|", "L2", "|", "|", "Wc", "|", "|", "|", "|", "|", "|", "|", "35", "|", "|", "|", "|", "23", "14", "|", "36", "|", "U", "|", "M", "K", "T", "33", "24", "L3", "L5", "L6", "|", "34", "|", "L4", "|", "|")
 
 
 def open_kernel(weights, x_ref, c_ref, gain, shift, query_bias, value_bias, rows_table, cols_table, take, out_bias, up_bias, down_bias, gain2, shift2, *refs):
@@ -395,13 +395,18 @@
     else:
         wq, wo, wu, wd = refs[:4]
         refs = refs[4:]
-    xw, cw, n1_turned, qkv_out, probs_out, o, o_turned = refs[:7]
-    raw_out, n2_turned, g_out, dh_out, da, do, dm, sums, up_sum = refs[7:16]
+    xw_out, cw_out, n1_out, qkv_out, probs_out, o_out, o_turned_out = refs[:7]
+    raw_out, n2_out, g_out, dh_out, da, do, dm, sums, up_sum = refs[7:16]
     refs = refs[16:]
     if weights:
         wq_out, refs = refs[0], refs[1:]
-    rawx, rawc, n1, tab, row_bias, qkv_s, probs, y_s, d_s, g_s, g_chunk, dh_chunk, out_sem, probs_sem, send, recv, loc = refs[:17]
-    refs = refs[17:]
+    rawx, rawc, n1, tab, row_bias, qkv_s, probs, y_s, d_s, g_s, g_chunk, dh_chunk, xw, cw, n1_turned, o, o_turned, n2_turned, hot, out_sem, probs_sem, send, recv, loc = refs[:24]
+    refs = refs[24:]
+    flushes = ((xw, xw_out), (cw, cw_out), (n1_turned, n1_out), (o, o_out), (o_turned, o_turned_out), (n2_turned, n2_out))
+
+    def flush(i):
+        return pltpu.make_async_copy(flushes[i][0], flushes[i][1], out_sem.at[5 + i])
+
     if weights:
         wq, wo, wu, wd = refs[:4]
         along_col, near_by, first, second, third, last, sent = links(shards, refs[:4], *refs[4:])
@@ -449,10 +454,12 @@
     def cut_windows():
         window_arrived(0)
         lax.fori_loop(0, 44, cut_x, 0)
+        flush(0).start()
 
     def cut_cotangent():
         window_arrived(1)
         lax.fori_loop(0, 44, cut_c, 0)
+        flush(1).start()
 
     def project_all():
         lax.fori_loop(0, 2, project, 0)
@@ -461,8 +468,13 @@
             pltpu.make_async_copy(wq, wq_out, out_sem.at[1]).start()
 
     def turn_all():
+        turn(o, o_turned)
+        flush(3).start()
+        flush(4).start()
+
+    def turn_first():
         turn(n1, n1_turned)
-        turn(o, o_turned)
+        flush(2).start()
 
     blocks = (slice(0, 352), slice(352, 704))
 
@@ -482,6 +494,7 @@
 
         lax.fori_loop(0, ROWS // BLOCK, begin, 0)
         turn(n1, n2_turned)
+        flush(5).start()
 
     def chunk_out(which, step):
         lanes = pl.ds(pl.multiple_of(step * FEATURES, FEATURES), FEATURES)
@@ -542,14 +555,14 @@
         lax.fori_loop(0, ROWS // BLOCK, end, 0)
         raw_copy.wait()
 
-    acts = {"X": cut_windows, "P": project_all, "T": turn_all, "K": cut_cotangent, "M": middle_begin}
+    acts = {"X": cut_windows, "P": project_all, "T": turn_all, "U": turn_first, "K": cut_cotangent, "M": middle_begin}
     acts["Wx"] = functools.partial(window_start, 0)
     acts["Wc"] = functools.partial(window_start, 1)
     if weights:
         acts.update({"a": along_col, "b": near_by, "1": first, "2": second, "3": third, "L": last})
         slots = plan_slots(OPEN_PLAN, acts)
     else:
-        slots = plan_slots(("Wx", "Wc", "X", "P", *("|",) * 18, "T", "K", "M", *("|",) * 4), acts)
+        slots = plan_slots(("Wx", "Wc", "X", "P", *("|",) * 18, "T", "U", "K", "M", *("|",) * 4), acts)
     o[...] = jnp.zeros_like(o)
     build_table(tab, rows_table, cols_table, take)
     row_bias[0] = as_row(query_bias)
@@ -560,40 +573,45 @@
     key_place = lax.broadcasted_iota(jnp.int32, (224, 128), 0)
     key_lane = lax.broadcasted_iota(jnp.int32, (224, 128), 1)
     key_a, key_b = key_place // 16, key_place % 16
+    for parity in range(2):
+        key_on = key_lane - (64 if parity == 0 else 0)
+        hot[parity] = jnp.where(
+            key_on == 14,
+            jnp.where(key_b >= 14, 1.0, 0.0),
+            jnp.where(
+                (key_on % 32 < 14) & (key_a == key_on % 32),
+                1.0,
+                jnp.where((key_on % 32 >= 16) & (key_on % 32 < 30) & (key_b == key_on % 32 - 16), 1.0, 0.0),
+            ),
+        )
 
     def probs_copy(index):
         window, pair_index = index // 6, index % 6
         part = pl.ds(2 * pair_index, 2)
         return pltpu.make_async_copy(probs.at[window, part], probs_out.at[window, part], probs_sem.at[window, pair_index])
 
-    def pair(index, _):
-        for i, slot_acts in enumerate(slots[1:18]):
-            if slot_acts:
-                pl.when(index == i + 1)(functools.partial(run_all, slot_acts))
-        window, pair_index = index // 6, index % 6
+    def attend(window, pair_index, rows):
         start, tall, width = window_params(window, row, col)
         at = pl.ds(pl.multiple_of(start * 16, 16), 224)
+        q_at = pl.ds(pl.multiple_of(start * 16, 16), rows)
         alive = (row_of // 16 < tall) & (row_of % 16 < width)
         lanes = lambda third: pl.ds(pl.multiple_of(third * FEATURES + pair_index * 128, 128), 128)
-        q = jnp.where(alive, qkv_s[at, lanes(0)].astype(F32), 0.0)
+        q = jnp.where(alive[:rows], qkv_s[q_at, lanes(0)].astype(F32), 0.0)
         k = jnp.where(alive, qkv_s[at, lanes(1)].astype(F32), 0.0)
         v = jnp.where(alive, qkv_s[at, lanes(2)].astype(F32), row_bias[1, :, lanes(0)].astype(BF).astype(F32)).astype(BF)
         terms = jnp.dot(q.astype(BF), tab[...], preferred_element_type=F32)
+        lines = [slice(16 * a, 16 * a + 16) for a in range(rows // 16)]
         outs = []
         for parity in range(2):
-            base = 64 if parity == 0 else 0
             own = (lane < 64) if parity == 0 else (lane >= 64)
+            first_lane = 256 * parity
             rel_rows = jnp.concatenate(
-                [pltpu.roll(terms[16 * a : 16 * a + 16, 256 * parity : 256 * parity + 128], a, 1) for a in range(14)], axis=0
+                [pltpu.roll(terms[at_a, first_lane : first_lane + 128], a, 1) for a, at_a in enumerate(lines)], axis=0
             )
             rel_cols = jnp.concatenate(
-                [
-                    pltpu.roll(terms[16 * a : 16 * a + 16, 256 * parity + 128 : 256 * parity + 256], 0, 1, stride=1, stride_axis=0)
-                    for a in range(14)
-                ],
-                axis=0,
+                [pltpu.roll(terms[at_a, first_lane + 128 : first_lane + 256], 0, 1, stride=1, stride_axis=0) for at_a in lines], axis=0
             )
-            on = lane - base
+            on = lane - (64 if parity == 0 else 0)
             in_rows = ((on >= 0) & (on < 14)) | ((on >= 32) & (on < 46))
             in_cols = ((on >= 16) & (on < 30)) | ((on >= 48) & (on < 62))
             rel = jnp.where(in_rows, rel_rows, jnp.where(in_cols, rel_cols, 0.0))
@@ -601,26 +619,25 @@
             fine = jnp.where(on >= 32, rel - rough, rough)
             fine = jnp.where(on == 14, -1e30, fine)
             q_side = jnp.where(own, q * 0.125, fine).astype(BF)
-            key_on = key_lane - base
-            hot = jnp.where(
-                key_on == 14,
-                jnp.where(key_b >= 14, 1.0, 0.0),
-                jnp.where(
-                    (key_on % 32 < 14) & (key_a == key_on % 32),
-                    1.0,
-                    jnp.where((key_on % 32 >= 16) & (key_on % 32 < 30) & (key_b == key_on % 32 - 16), 1.0, 0.0),
-                ),
-            )
-            k_side = jnp.where(own, k, hot).astype(BF)
+            k_side = jnp.where(own, k, hot[parity]).astype(BF)
             scores = lax.dot_general(q_side, k_side, (((1,), (1,)), ((), ())), preferred_element_type=F32)
             exponent = jnp.exp(scores - jnp.max(scores, axis=-1, keepdims=True))
             p = (exponent * (1.0 / jnp.sum(exponent, axis=-1, keepdims=True))).astype(BF)
-            probs[window, 2 * pair_index + parity] = p
+            probs[window, 2 * pair_index + parity, 0:rows, :] = p
+            if rows < 224:
+                probs[window, 2 * pair_index + parity, rows:224, :] = jnp.zeros((224 - rows, 224), BF)
             outs.append(jnp.dot(p, v, preferred_element_type=F32))
         blended = jnp.where(lane < 64, outs[0], outs[1])
-        out_lanes = pl.ds(pl.multiple_of(pair_index * 128, 128), 128)
-        o_at = pl.ds(pl.multiple_of(start * 16, 16), 224)
-        o[o_at, out_lanes] = jnp.where(alive, blended, 0.0).astype(BF)
+        o[q_at, lanes(0)] = jnp.where(alive[:rows], blended, 0.0).astype(BF)
+
+    def pair(index, _):
+        for i, slot_acts in enumerate(slots[1:18]):
+            if slot_acts:
+                pl.when(index == i + 1)(functools.partial(run_all, slot_acts))
+        window, pair_index = index // 6, index % 6
+        short = (window >= 2) & (row >= 2)
+        pl.when(short)(functools.partial(attend, window, pair_index, 128))
+        pl.when(jnp.logical_not(short))(functools.partial(attend, window, pair_index, 224))
         probs_copy(index).start()
         return 0
 
@@ -639,6 +656,8 @@
         for copy in sent:
             copy().wait_send()
     lax.fori_loop(0, pairs, lambda index, _: (probs_copy(index).wait(), 0)[1], 0)
+    for i in range(6):
+        flush(i).wait()
     window_left(0)
     window_left(1)
 
@@ -681,7 +700,7 @@
         ]
         + ([shape((768, 2304), BF)] if weights else []),
         in_specs=[vm] * (14 + len(given)),
-        out_specs=[vm, vm, vm, an, an, vm, vm, an, vm, an, an, vm, vm, vm, vm, vm] + ([an] if weights else []),
+        out_specs=[an] * 11 + [vm] * 5 + ([an] if weights else []),
         scratch_shapes=[
             raw,
             raw,
@@ -695,7 +714,14 @@
             pltpu.VMEM((ROWS, FEATURES), BF),
             pltpu.VMEM((FEATURES, FEATURES), BF),
             pltpu.VMEM((ROWS, FEATURES), BF),
-            dma((5,)),
+            pltpu.VMEM((ROWS, FEATURES), BF),
+            pltpu.VMEM((ROWS, FEATURES), BF),
+            pltpu.VMEM((FEATURES, ROWS), BF),
+            pltpu.VMEM((SPAN, FEATURES), BF),
+            pltpu.VMEM((FEATURES, ROWS), BF),
+            pltpu.VMEM((FEATURES, ROWS), BF),
+            pltpu.VMEM((2, 224, 128), F32),
+            dma((11,)),
             dma((4, 6)),
             dma((2, 2, 3)),
             dma((2, 4, 3)),
@@ -707,12 +733,22 @@
     return list(outs) if weights else list(outs) + gathered[:1]
 
 
-def attention_back(window, pair_index, probs_of, do, qkv, o, tab, value_bias, bias_sums, table_sums, row, col):
-    row_of = lax.broadcasted_iota(jnp.int32, (224, 1), 0)
-    lane = lax.broadcasted_iota(jnp.int32, (1, 128), 1)
+def key_marks(hot):
     key_place = lax.broadcasted_iota(jnp.int32, (224, 128), 0)
     key_lane = lax.broadcasted_iota(jnp.int32, (224, 128), 1)
     key_a, key_b = key_place // 16, key_place % 16
+    for parity in range(2):
+        key_on = key_lane - (64 if parity == 0 else 0)
+        hot[parity] = jnp.where(
+            (key_on >= 0) & (key_on < 14) & (key_a == key_on),
+            1.0,
+            jnp.where((key_on >= 16) & (key_on < 30) & (key_b == 29 - key_on), 1.0, 0.0),
+        )
+
+
+def attention_back(window, pair_index, probs_of, do, qkv, o, tab, hot, value_bias, bias_sums, table_sums, row, col):
+    row_of = lax.broadcasted_iota(jnp.int32, (224, 1), 0)
+    lane = lax.broadcasted_iota(jnp.int32, (1, 128), 1)
     start, tall, width = window_params(window, row, col)
     at = pl.ds(pl.multiple_of(start * 16, 16), 224)
     inside = row_of // 16 < tall
@@ -741,13 +777,7 @@
         ds = (p.astype(F32) * centered).astype(BF)
         value_parts.append(jnp.dot(grad_turned[half], p, preferred_element_type=F32))
         key_parts.append(jnp.dot(q_turned[half], ds, preferred_element_type=F32))
-        key_on = key_lane - base
-        hot = jnp.where(
-            (key_on >= 0) & (key_on < 14) & (key_a == key_on),
-            1.0,
-            jnp.where((key_on >= 16) & (key_on < 30) & (key_b == 29 - key_on), 1.0, 0.0),
-        )
-        k_side = jnp.where(own, k * 0.125, hot).astype(BF)
+        k_side = jnp.where(own, k * 0.125, hot[parity]).astype(BF)
         wide = jnp.dot(ds, k_side, preferred_element_type=F32)
         query_parts.append(wide)
         by_rows = jnp.where((on >= 0) & (on < 14), wide, 0.0)
@@ -778,10 +808,11 @@
             qkv[16 * a : 16 * a + 16, :] = jnp.zeros((16, 3 * FEATURES), BF)
 
 
-def plain_back_kernel(do, probs, qkv, o, value_bias, rows_table, cols_table, take, dqkv, bias_sums, table_sums, tab, row_bias):
+def plain_back_kernel(do, probs, qkv, o, value_bias, rows_table, cols_table, take, dqkv, bias_sums, table_sums, tab, row_bias, hot):
     row, col = lax.axis_index("row"), lax.axis_index("col")
     build_table(tab, rows_table, cols_table, take)
     row_bias[...] = as_row(value_bias)
+    key_marks(hot)
     dqkv[...] = qkv[...]
     clear_idle(dqkv, row, col)
     bias_sums[...] = jnp.zeros_like(bias_sums)
@@ -797,6 +828,7 @@
             dqkv,
             o,
             tab,
+            hot,
             row_bias,
             bias_sums,
             table_sums,
@@ -816,7 +848,7 @@
         out_shape=[shape((SPAN, 3 * FEATURES), BF), shape((2, 8, FEATURES), F32), shape((128, 512), F32)],
         in_specs=[vm] * 8,
         out_specs=[vm] * 3,
-        scratch_shapes=[pltpu.VMEM((128, 512), BF), pltpu.VMEM((1, FEATURES), F32)],
+        scratch_shapes=[pltpu.VMEM((128, 512), BF), pltpu.VMEM((1, FEATURES), F32), pltpu.VMEM((2, 224, 128), F32)],
         compiler_params=pltpu.CompilerParams(vmem_limit_bytes=62 << 20),
     )(do, probs, qkv, o, value_bias, rows_table, cols_table, takers(True))
 
@@ -1130,7 +1162,8 @@
 
 
 def back_kernel(
-    do, o, value_bias, rows_table, cols_table, take, o_turned, da, n2_turned, cw, xw, n1_turned, gain, sums, up_sum, taker, probs, qkv_in, dh_in, g_in, dm_in, wq_in, raw_r, *refs
+    value_bias, rows_table, cols_table, take, o_turned, da, cw, gain, sums, up_sum, taker,
+    do_in, o_in, n2_in, xw_in, n1_in, probs, qkv_in, dh_in, g_in, dm_in, wq_in, raw_r, *refs
 ):
     out, grad_out, gq, go, gu, gd, small_out, table_out = refs[:8]
     qkv, probs_s, image_grad, shared_h, shared_g, own_r = refs[8:14]
@@ -1140,7 +1173,8 @@
     small, table, small_land, table_land, small_z, table_z = refs[29:35]
     count = len(SUM_CHUNKS)
     lands = refs[35 : 35 + 5 * count]
-    send, recv, load_sem, probs_sem, wsend, wrecv, ssend, srecv = refs[35 + 5 * count :]
+    do, o, n2_turned, xw, n1_turned, hot = refs[35 + 5 * count : 41 + 5 * count]
+    send, recv, load_sem, probs_sem, wsend, wrecv, ssend, srecv = refs[41 + 5 * count :]
     img, row, col = place()
     y_row = lax.rem(row + 2, 4)
     core_row = row + 1 - 2 * lax.rem(row, 2)
@@ -1156,10 +1190,15 @@
             (wq_in, shared_h.at[:, pl.ds(0, 3 * FEATURES)]),
             (raw_r.at[pl.ds(8, 14), pl.ds(1, 2)], own_r.at[0]),
             (raw_r.at[pl.ds(30, 14), pl.ds(1, 2)], own_r.at[1]),
+            (do_in, do),
+            (o_in, o),
+            (n2_in, n2_turned),
+            (xw_in, xw),
+            (n1_in, n1_turned),
         )
         return pltpu.make_async_copy(pairs[i][0], pairs[i][1], load_sem.at[i])
 
-    for i in (1, 2, 0, 3, 5, 6):
+    for i in (1, 2, 7, 8, 9, 0, 11, 10, 3, 5, 6):
         load(i).start()
     windows = window_count(row, col)
 
@@ -1193,11 +1232,13 @@
     norm_sums[...] = jnp.zeros_like(norm_sums)
     build_table(tab, rows_table, cols_table, take)
     row_bias[...] = as_row(value_bias)
+    key_marks(hot)
     load(1).wait()
 
     def grad_rows(i):
         if i == 0:
             load(4).start()
+            load(10).wait()
             load(3).wait()
             load(4).wait()
         input_grad(pl.ds(i * BLOCK, BLOCK), qkv, shared_h[:, 0 : 3 * FEATURES], xw, image_grad, gain, norm_sums)
@@ -1264,7 +1305,8 @@
     run_all(slots[0])
     load(2).wait()
     clear_idle(qkv, row, col)
-    load(0).wait()
+    for i in (7, 8, 9, 0, 11):
+        load(i).wait()
 
     def head_pair(k, _):
         pair_index = lax.rem(k, 2) * 3 + k // 2
@@ -1291,6 +1333,7 @@
                 qkv,
                 o,
                 tab,
+                hot,
                 row_bias,
                 bias_sums,
                 table_sums,
@@ -1330,7 +1373,7 @@
         out_shape=[shape((2, 16, 16, FEATURES), BF), shape((2, 16, 16, FEATURES), BF)]
         + [shape((k // 16, n // 2), F32) for k, n in WHOLES]
         + [shape((16, FEATURES), F32), shape((64, 128), F32)],
-        in_specs=[vm] * 16 + [an] * 7,
+        in_specs=[vm] * 11 + [an] * 12,
         out_specs=[vm] * 8,
         scratch_shapes=[
             pltpu.VMEM((SPAN, 3 * FEATURES), BF),
@@ -1357,11 +1400,13 @@
             pltpu.VMEM((4, 64, 128), F32),
         ]
         + land_shapes(SUM_CHUNKS)
-        + [dma((2, 4, 3)), dma((2, 2, 3)), dma((7,)), dma((2,)), dma((count, 13)), dma((count, 13)), dma((12,)), dma((12,))],
+        + [pltpu.VMEM(s, BF) for s in ((SPAN, FEATURES), (SPAN, FEATURES), (FEATURES, ROWS), (ROWS, FEATURES), (FEATURES, ROWS))]
+        + [pltpu.VMEM((2, 224, 128), F32)]
+        + [dma((2, 4, 3)), dma((2, 2, 3)), dma((12,)), dma((2,)), dma((count, 13)), dma((count, 13)), dma((12,)), dma((12,))],
         compiler_params=pltpu.CompilerParams(collective_id=1, has_side_effects=True, vmem_limit_bytes=67043328),
     )(
-        do, o, value_bias, rows_table, cols_table, takers(True), o_turned, da, n2_turned, cw, xw, n1_turned, gain, sums, up_sum, jnp.asarray(table_taker()),
-        probs, qkv, dh, g.reshape(128, 3, 8, FEATURES), dm, wq, raw_r,
+        value_bias, rows_table, cols_table, takers(True), o_turned, da, cw, gain, sums, up_sum, jnp.asarray(table_taker()),
+        do, o, n2_turned, xw, n1_turned, probs, qkv, dh, g.reshape(128, 3, 8, FEATURES), dm, wq, raw_r,
     )
 
 

time: 237 us -> 231 us (0.975)
  Pallas kernels: 236 us -> 230 us
    pallas_call x1, Pallas kernels: 122 us -> 114 us  [open_windows(): pl.pallas_call(functools.partial(open_kernel, weights), out_shape=[shape(...]
where the time goes in v5:
time: 231 us
  Pallas kernels  230 us (100%)
    pallas_call x1, Pallas kernels, open_windows(): pl.pallas_call(functools.partial(open_kernel, weights), out_shape=[shape(...  114 us
    pallas_call x1, Pallas kernels, back(): pl.pallas_call(back_kernel, out_shape=[shape((2, 16, 16, FEATURES), BF),...  112 us

profile of v5, /device:TPU:0, one launch (start us, length us, event | category | flops | bytes accessed | tf_op | source)
XLA Modules:
  0.0 230.7 jit_solution(11321212617284895891)
XLA Ops:
  0.7 114.2 %shard_map.323 = (bf16[704,768]{1,0:T(8,128)(2,1)}, bf16[704,768]{1,0:T(8,128)(2,1)}, bf16[768,704]{1,0:T(8,128)(2,1)}, bf16[800,2304]{1,0:T(8,128)(2,1)}, bf16[...) custom-call(bf16[2,16,2,8,768]{4,3,2,1,0:T(8,128)(2,1)} %bitcast.5, ...), custom_call_target="tpu_custom_call" | custom-call | tf_op jit(solution)/shard_map/pallas_call | solution.py:679
  114.8 111.8 %shard_map.324 = (bf16[2,16,16,768]{3,2,1,0:T(8,128)(2,1)}, bf16[2,16,16,768]{3,2,1,0:T(8,128)(2,1)}, f32[48,1152]{1,0:T(8,128)}, f32[48,384]{1,0:T(8,128)}, f32...) custom-call(f32[768]{0:T(1024)} %value_bias.3, bf16[27,64]{1,0:T(8,128)(2,1)} %rows_table.3, ...), custom_call_target="tpu_custom_call" | custom-call | tf_op jit(solution)/shard_map/pallas_call | solution.py:1371
  226.6 3.9 %shard_map.325 = (bf16[2,16,16,768]{3,2,1,0:T(8,128)(2,1)}, f32[2,16,16,768]{3,2,1,0:T(8,128)}, f32[48,1152]{1,0:T(8,128)}, f32[48,384]{1,0:T(8,128)}, f32[48,15...) custom-call(bf16[2,16,16,768]{3,2,1,0:T(8,128)(2,1)} %get-tuple-elem, ...), custom_call_target="tpu_custom_call" | custom-call | tf_op jit(solution)/shard_map/pallas_call | solution.py:1440

commit v6 on v5

--- a/solution.py
+++ b/solution.py
@@ -563,13 +563,11 @@
         slots = plan_slots(OPEN_PLAN, acts)
     else:
         slots = plan_slots(("Wx", "Wc", "X", "P", *("|",) * 18, "T", "U", "K", "M", *("|",) * 4), acts)
+    run_all(slots[0][:3])
     o[...] = jnp.zeros_like(o)
     build_table(tab, rows_table, cols_table, take)
     row_bias[0] = as_row(query_bias)
     row_bias[1] = as_row(value_bias)
-    run_all(slots[0])
-    row_of = lax.broadcasted_iota(jnp.int32, (224, 1), 0)
-    lane = lax.broadcasted_iota(jnp.int32, (1, 128), 1)
     key_place = lax.broadcasted_iota(jnp.int32, (224, 128), 0)
     key_lane = lax.broadcasted_iota(jnp.int32, (224, 128), 1)
     key_a, key_b = key_place // 16, key_place % 16
@@ -584,7 +582,9 @@
                 jnp.where((key_on % 32 >= 16) & (key_on % 32 < 30) & (key_b == key_on % 32 - 16), 1.0, 0.0),
             ),
         )
-
+    run_all(slots[0][3:])
+    row_of = lax.broadcasted_iota(jnp.int32, (224, 1), 0)
+    lane = lax.broadcasted_iota(jnp.int32, (1, 128), 1)
     def probs_copy(index):
         window, pair_index = index // 6, index % 6
         part = pl.ds(2 * pair_index, 2)
@@ -1230,9 +1230,6 @@
     bias_sums[...] = jnp.zeros_like(bias_sums)
     table_sums[...] = jnp.zeros_like(table_sums)
     norm_sums[...] = jnp.zeros_like(norm_sums)
-    build_table(tab, rows_table, cols_table, take)
-    row_bias[...] = as_row(value_bias)
-    key_marks(hot)
     load(1).wait()
 
     def grad_rows(i):
@@ -1303,6 +1300,9 @@
     acts = {"p": pair_stage, "1": first, "2": second, "3": third, "4": fourth, "5": fifth, "G": grad_rows, "s": small_step, "S": send_grad}
     slots = plan_slots(CLOSE_PLAN, acts)
     run_all(slots[0])
+    build_table(tab, rows_table, cols_table, take)
+    row_bias[...] = as_row(value_bias)
+    key_marks(hot)
     load(2).wait()
     clear_idle(qkv, row, col)
     for i in (7, 8, 9, 0, 11):
@@ -1415,29 +1415,42 @@
     outs[0][...] = out_in[...]
 
     def widen(i, _):
-        outs[1][i // 16, i % 16] = grad_in[i // 16, i % 16].astype(F32)
+        outs[1][0, i] = grad_in[0, i].astype(F32)
         return 0
 
-    lax.fori_loop(0, 32, widen, 0)
-    for given, goal in zip(sums_in, outs[2:6]):
-        goal[...] = given[...]
-    for i, goal in zip((0, 1, 2, None, 3, 4, 5, 6, 7), outs[6:15]):
-        if i is None:
-            goal[...] = jnp.concatenate([small[8 + j : 9 + j, :] for j in range(4)], axis=1).reshape(4 * FEATURES)
-        else:
-            goal[...] = small[i : i + 1, :].reshape(FEATURES)
-    turned = table[...].T
-    outs[15][...] = turned[0:27, :]
-    outs[16][...] = turned[64:91, :]
+    lax.fori_loop(0, 16, widen, 0)
+
+    @pl.when(pl.program_id(0) == 0)
+    def _():
+        for given, goal in zip(sums_in, outs[2:6]):
+            goal[...] = given[...]
+        for i, goal in zip((0, 1, 2, None, 3, 4, 5, 6, 7), outs[6:15]):
+            if i is None:
+                goal[...] = jnp.concatenate([small[8 + j : 9 + j, :] for j in range(4)], axis=1).reshape(4 * FEATURES)
+            else:
+                goal[...] = small[i : i + 1, :].reshape(FEATURES)
+        turned = table[...].T
+        outs[15][...] = turned[0:27, :]
+        outs[16][...] = turned[64:91, :]
 
 
 def deliver(*given):
-    vm = pl.BlockSpec(memory_space=pltpu.VMEM)
     shape = jax.ShapeDtypeStruct
     lengths = [FEATURES] * 3 + [4 * FEATURES] + [FEATURES] * 5
     outs = [shape((2, 16, 16, FEATURES), BF), shape((2, 16, 16, FEATURES), F32)] + [shape((k // 16, n // 2), F32) for k, n in WHOLES]
     outs += [shape((n,), F32) for n in lengths] + [shape((27, 64), F32)] * 2
-    return pl.pallas_call(deliver_kernel, out_shape=outs, in_specs=[vm] * 8, out_specs=[vm] * len(outs))(*given)
+    image = pl.BlockSpec((1, 16, 16, FEATURES), lambda i: (i, 0, 0, 0))
+
+    def spec(array):
+        return pl.BlockSpec(array.shape, lambda i: (0,) * len(array.shape))
+
+    return pl.pallas_call(
+        deliver_kernel,
+        grid=(2,),
+        out_shape=outs,
+        in_specs=[image] * 2 + [spec(v) for v in given[2:]],
+        out_specs=[image] * 2 + [spec(v) for v in outs[2:]],
+    )(*given)
 
 
 def on_device(

time: 231 us -> 231 us (level)
  no operation moved by 1% of the time
where the time goes in v6:
time: 231 us; the launch traced here: 230 us
  Pallas kernels  229 us (99%)
    pallas_call x1, Pallas kernels, open_windows(): pl.pallas_call(functools.partial(open_kernel, weights), out_shape=[shape(...  114 us
    pallas_call x1, Pallas kernels, back(): pl.pallas_call(back_kernel, out_shape=[shape((2, 16, 16, FEATURES), BF),...  112 us

profile of v6, /device:TPU:0, one launch (start us, length us, event | category | flops | bytes accessed | tf_op | source)
XLA Modules:
  0.0 230.1 jit_solution(4450590456176077113)
XLA Ops:
  0.7 114.0 %shard_map.323 = (bf16[704,768]{1,0:T(8,128)(2,1)}, bf16[704,768]{1,0:T(8,128)(2,1)}, bf16[768,704]{1,0:T(8,128)(2,1)}, bf16[800,2304]{1,0:T(8,128)(2,1)}, bf16[...) custom-call(bf16[2,16,2,8,768]{4,3,2,1,0:T(8,128)(2,1)} %bitcast.5, ...), custom_call_target="tpu_custom_call" | custom-call | tf_op jit(solution)/shard_map/pallas_call | solution.py:679
  114.6 111.9 %shard_map.324 = (bf16[2,16,16,768]{3,2,1,0:T(8,128)(2,1)}, bf16[2,16,16,768]{3,2,1,0:T(8,128)(2,1)}, f32[48,1152]{1,0:T(8,128)}, f32[48,384]{1,0:T(8,128)}, f32...) custom-call(f32[768]{0:T(1024)} %value_bias.3, bf16[27,64]{1,0:T(8,128)(2,1)} %rows_table.3, ...), custom_call_target="tpu_custom_call" | custom-call | tf_op jit(solution)/shard_map/pallas_call | solution.py:1371
  226.5 3.4 %shard_map.325 = (bf16[2,16,16,768]{3,2,1,0:T(8,128)(2,1)}, f32[2,16,16,768]{3,2,1,0:T(8,128)}, f32[48,1152]{1,0:T(8,128)}, f32[48,384]{1,0:T(8,128)}, f32[48,15...) custom-call(bf16[2,16,16,768]{3,2,1,0:T(8,128)(2,1)} %get-tuple-elem, ...), custom_call_target="tpu_custom_call" | custom-call | tf_op jit(solution)/shard_map/pallas_call | solution.py:1447

commit v7 on v6

--- a/solution.py
+++ b/solution.py
@@ -384,7 +384,7 @@
     lax.fori_loop(0, 44, step, 0)
 
 
-OPEN_PLAN = ("a0", "a2", "a1", "b0", "b2", "a6", "10", "b1", "a5", "Wx", "11", "b5", "b6", "12", "20", "22", "21", "15", "a3", "X", "16", "a4", "b3", "31", "30", "25", "L1", "L0", "P", "32", "13", "b4", "26", "|", "|", "L2", "|", "|", "Wc", "|", "|", "|", "|", "|", "|", "|", "35", "|", "|", "|", "|", "23", "14", "|", "36", "|", "U", "|", "M", "K", "T", "33", "24", "L3", "L5", "L6", "|", "34", "|", "L4", "|", "|")
+OPEN_PLAN = ("a0", "a2", "a1", "b0", "b2", "a6", "10", "b1", "a5", "Wx", "11", "b5", "b6", "12", "20", "22", "21", "15", "a3", "X", "16", "a4", "b3", "31", "30", "25", "L1", "L0", "P", "32", "13", "b4", "26", "|", "|", "L2", "|", "|", "Wc", "|", "|", "|", "|", "|", "|", "|", "35", "|", "|", "|", "|", "23", "14", "|", "36", "|", "U", "|", "M", "K", "33", "T", "24", "L3", "L5", "L6", "|", "34", "|", "L4", "|", "|")
 
 
 def open_kernel(weights, x_ref, c_ref, gain, shift, query_bias, value_bias, rows_table, cols_table, take, out_bias, up_bias, down_bias, gain2, shift2, *refs):

time: 231 us -> 231 us (level)
  no operation moved by 1% of the time
where the time goes in v7:
time: 231 us; the launch traced here: 230 us
  Pallas kernels  229 us (99%)
    pallas_call x1, Pallas kernels, open_windows(): pl.pallas_call(functools.partial(open_kernel, weights), out_shape=[shape(...  114 us
    pallas_call x1, Pallas kernels, back(): pl.pallas_call(back_kernel, out_shape=[shape((2, 16, 16, FEATURES), BF),...  112 us

profile of v7, /device:TPU:0, one launch (start us, length us, event | category | flops | bytes accessed | tf_op | source)
XLA Modules:
  0.0 230.1 jit_solution(4360215261903251733)
XLA Ops:
  0.7 114.0 %shard_map.323 = (bf16[704,768]{1,0:T(8,128)(2,1)}, bf16[704,768]{1,0:T(8,128)(2,1)}, bf16[768,704]{1,0:T(8,128)(2,1)}, bf16[800,2304]{1,0:T(8,128)(2,1)}, bf16[...) custom-call(bf16[2,16,2,8,768]{4,3,2,1,0:T(8,128)(2,1)} %bitcast.5, ...), custom_call_target="tpu_custom_call" | custom-call | tf_op jit(solution)/shard_map/pallas_call | solution.py:679
  114.6 111.9 %shard_map.324 = (bf16[2,16,16,768]{3,2,1,0:T(8,128)(2,1)}, bf16[2,16,16,768]{3,2,1,0:T(8,128)(2,1)}, f32[48,1152]{1,0:T(8,128)}, f32[48,384]{1,0:T(8,128)}, f32...) custom-call(f32[768]{0:T(1024)} %value_bias.3, bf16[27,64]{1,0:T(8,128)(2,1)} %rows_table.3, ...), custom_call_target="tpu_custom_call" | custom-call | tf_op jit(solution)/shard_map/pallas_call | solution.py:1371
  226.5 3.4 %shard_map.325 = (bf16[2,16,16,768]{3,2,1,0:T(8,128)(2,1)}, f32[2,16,16,768]{3,2,1,0:T(8,128)}, f32[48,1152]{1,0:T(8,128)}, f32[48,384]{1,0:T(8,128)}, f32[48,15...) custom-call(bf16[2,16,16,768]{3,2,1,0:T(8,128)(2,1)} %get-tuple-elem, ...), custom_call_target="tpu_custom_call" | custom-call | tf_op jit(solution)/shard_map/pallas_call | solution.py:1447
